TPU v7x, 32 devices: a whole 2x2x4 slice. The times are simulated.
32 devices in a mesh: grp: 4 (over x, core), rep: 8 (over z, y).
Axes of the slice: x: 2, y: 2, z: 4, core: 2. Of those that a mesh axis runs over, the one named last changes fastest.
Arguments:
- block_input: bfloat16 [8, 512, 960], P('rep', 'grp'), may hold values from -32 to 32
- cotangent: bfloat16 [8, 512, 960], P('rep', 'grp'), may hold values from -6 to 6
- norm_gains: bfloat16 [2, 960], P(None, 'grp'), may hold values from 0.099609375 to 1.8984375
- w_query: bfloat16 [960, 960], P(None, 'grp'), may hold values from -8 to 8
- key_weight: bfloat16 [960, 320], P(None, 'grp'), may hold values from -0.1875 to 0.1875
- value_weight: bfloat16 [960, 320], P(None, 'grp'), may hold values from -0.1875 to 0.1875
- w_out: bfloat16 [960, 960], P(None, 'grp'), may hold values from -0.75 to 0.75
- w_gate: bfloat16 [960, 2560], P(None, 'grp'), may hold values from -0.1875 to 0.1875
- w_up: bfloat16 [960, 2560], P(None, 'grp'), may hold values from -0.1875 to 0.1875
- w_down: bfloat16 [2560, 960], P(None, 'grp'), may hold values from -0.25 to 0.25
Outputs:
- block_output: float32 [8, 512, 960], P('rep', 'grp')
- input_grad: float32 [8, 512, 960], P('rep', 'grp')
- grad_gains: float32 [2, 960], P(None, 'grp')
- grad_query: float32 [960, 960], P('rep', 'grp')
- grad_key: float32 [960, 320], P('rep', 'grp')
- grad_value: float32 [960, 320], P('rep', 'grp')
- grad_out: float32 [960, 960], P('rep', 'grp')
- grad_gate: float32 [960, 2560], P('rep', 'grp')
- grad_up: float32 [960, 2560], P('rep', 'grp')
- grad_down: float32 [2560, 960], P('rep', 'grp')
All inputs are finite; a program needn't handle non-finite values.
Results may differ from a plain program's by a relative error of at most 0.014.
Values may be sent and summed in bfloat16 or wider, within the bound.
No kernel may reach another device: no remote copies, remote signals or barrier semaphores. Data moves between devices by JAX's collectives and lax.ppermute only.
A program may use at most 192 MiB of HBM per device.

v0:
```python
import math

import jax
import jax.numpy as jnp
import numpy as np
from jax import lax
from jax.experimental.layout import Layout, with_layout_constraint
from jax.sharding import PartitionSpec as P

HEAD_SIZE = 64
QUERY_HEADS = 15
KEY_VALUE_HEADS = 5
GROUP_QUERIES = QUERY_HEADS // KEY_VALUE_HEADS
EPS = 1e-05
THETA = 10000.0

BLOCK_ORDER = (0, 3, 1, 2)

CORE_SWAP = [(0, 1), (1, 0), (2, 3), (3, 2)]
CHIP_SWAP = [(0, 2), (2, 0), (1, 3), (3, 1)]
CROSS_SWAP = [(0, 3), (3, 0), (1, 2), (2, 1)]


def norm_scale(values):
    return lax.rsqrt(jnp.mean(values * values, axis=-1, keepdims=True) + EPS)


def rope_tables(positions):
    half = HEAD_SIZE // 2
    freq = jnp.exp(
        jnp.arange(half, dtype=jnp.int32).astype(jnp.float32) * (-2.0 * math.log(THETA) / HEAD_SIZE)
    )
    angle = positions.astype(jnp.float32)[:, None] * freq[None, :]
    return (jnp.cos(angle)[:, None, :], jnp.sin(angle)[:, None, :])


def rotate(values, cosine, sine):
    half = values.shape[-1] // 2
    first = values[..., :half]
    second = values[..., half:]
    return jnp.concatenate([first * cosine - second * sine, second * cosine + first * sine], axis=-1)


def dot_nn(left, right):
    return jnp.dot(left, right, preferred_element_type=jnp.float32)


def dot_nt(left, right):
    return lax.dot_general(
        left, right, (((1,), (1,)), ((), ())), preferred_element_type=jnp.float32
    )


def dot_tn(left, right):
    return lax.dot_general(
        left, right, (((0,), (0,)), ((), ())), preferred_element_type=jnp.float32
    )


def after(value, *tokens):
    return lax.optimization_barrier((value,) + tokens)[0]


class Order:
    def __init__(self):
        self.token = None

    def mark(self, value):
        self.token = value

    def hold(self, *values):
        if self.token is None:
            return values if len(values) > 1 else values[0]
        held = lax.optimization_barrier(values + (self.token,))[:-1]
        return held if len(held) > 1 else held[0]


def rep_bits():
    count = lax.axis_size("rep")
    bits = count.bit_length() - 1
    assert 1 << bits == count and bits >= 3
    return bits


def swap_over_rep(held, bit, axis):
    count = lax.axis_size("rep")
    mine = (lax.axis_index("rep") >> bit) & 1
    away = lax.dynamic_index_in_dim(held, 1 - mine, axis, keepdims=False).astype(jnp.bfloat16)
    came = lax.ppermute(away, "rep", [(i, i ^ (1 << bit)) for i in range(count)])
    return lax.dynamic_index_in_dim(held, mine, axis, keepdims=False), came, away


def joined(pair):
    return pair[0] + pair[1].astype(jnp.float32)


class RepSum:
    def __init__(self, partial, order):
        bits = rep_bits()
        self.bits_to_go = list(order) + list(range(len(order), bits))
        self.left = list(range(bits))
        self.held = partial.reshape((2,) * bits + partial.shape[1:])
        self.step()

    def step(self):
        bit = self.bits_to_go.pop(0)
        axis = len(self.left) - 1 - self.left.index(bit)
        self.left.remove(bit)
        self.kept, self.came, self.sent = swap_over_rep(self.held, bit, axis)

    def next(self, order):
        self.held = joined((self.kept, order.hold(self.came)))
        self.step()
        order.mark(self.sent)

    def end(self, order):
        while self.bits_to_go:
            self.next(order)
        return joined((self.kept, order.hold(self.came)))


def by_rep(partial):
    count = lax.axis_size("rep")
    return partial.reshape((count, partial.shape[0] // count) + partial.shape[1:])


def per_device(
    block_input,
    cotangent,
    norm_gains,
    w_query,
    key_weight,
    value_weight,
    w_out,
    w_gate,
    w_up,
    w_down,
):
    bf16 = jnp.bfloat16
    me = lax.axis_index("grp")
    rows = block_input.shape[1]
    width = block_input.shape[2]
    half_rows = 2 * rows
    kv_width = KEY_VALUE_HEADS * HEAD_SIZE
    slice_width = w_query.shape[1]
    kv_slice = key_weight.shape[1]
    hidden_slice = w_gate.shape[1]
    scale = 1.0 / math.sqrt(HEAD_SIZE)
    second_set = (me == 1) | (me == 2)
    own_start = second_set.astype(jnp.int32) * half_rows
    beside_start = half_rows - own_start
    own_block_start = jnp.where(me < 2, 0, rows)

    def own_half(values):
        return lax.dynamic_slice_in_dim(values, own_start, half_rows, 0)

    def own_block(values):
        return lax.dynamic_slice_in_dim(values, own_block_start, rows, 0)

    def own_cols(values):
        return lax.dynamic_slice_in_dim(values, me * (values.shape[1] // 4), values.shape[1] // 4, 1)

    def in_pair(own, cross):
        return jnp.concatenate([jnp.where(me < 2, own, cross), jnp.where(me < 2, cross, own)], axis=0)

    def sets(own, beside):
        return jnp.where(second_set, beside, own), jnp.where(second_set, own, beside)

    def core_swap(values):
        return lax.ppermute(values, "grp", CORE_SWAP)

    def chip_cross(values):
        return lax.ppermute(values, "grp", CROSS_SWAP)

    def two_halves(own, beside):
        return jnp.concatenate(sets(own, beside), axis=0)

    def in_order(own, beside, cross, corner, order=(0, 1, 2, 3)):
        out = []
        for device in order:
            out.append(
                jnp.where(
                    me == device,
                    own,
                    jnp.where(me == device ^ 1, beside, jnp.where(me == device ^ 3, cross, corner)),
                )
            )
        return jnp.concatenate(out, axis=0)

    turn = Order()

    x_cross = chip_cross(block_input[0])
    qkv_sent = jnp.concatenate(
        [
            w_query.T,
            key_weight.T,
            value_weight.T,
            jnp.pad(norm_gains, ((0, 6), (0, width - slice_width))),
        ],
        axis=0,
    )
    qkv_cross = chip_cross(qkv_sent)
    turn.mark(qkv_sent)
    qkv_beside = core_swap(turn.hold(qkv_sent))
    places = np.concatenate([np.arange(b * rows, (b + 1) * rows, dtype=np.int32) for b in BLOCK_ORDER])
    all_positions = turn.hold(jnp.asarray(places))
    own_positions = own_half(all_positions)
    cos_all, sin_all = rope_tables(all_positions)
    cos_own, sin_own = rope_tables(own_positions)
    allowed = all_positions[None, :] <= own_positions[:, None]
    wo_sent = turn.hold(w_out).T
    dy_here, down_t = turn.hold(cotangent, w_down)
    dy_here = dy_here[0]
    down_t = down_t.T
    wo_beside = core_swap(wo_sent)
    dy_beside = core_swap(dy_here)

    def down_piece(k):
        return lax.dynamic_slice_in_dim(down_t, (me ^ k) * hidden_slice, hidden_slice, 1)

    down_pieces = [down_piece(k) for k in range(4)]
    down_beside = core_swap(down_pieces[1])
    cos_all, sin_all, cos_own, sin_own, allowed, wo_sent, down_0, down_2, down_3 = lax.optimization_barrier(
        (cos_all, sin_all, cos_own, sin_own, allowed, wo_sent, down_pieces[0], down_pieces[2], down_pieces[3])
    )
    turn.mark(down_3)

    xf = in_pair(block_input[0], turn.hold(x_cross)).astype(jnp.float32)
    r1 = norm_scale(xf)
    n1 = xf * r1
    turn.mark(r1)
    qkv_cross = turn.hold(qkv_cross)
    qkv_corner = core_swap(qkv_cross)
    turn.mark(qkv_cross)
    wo_cross = chip_cross(turn.hold(wo_sent))
    dy_cross = chip_cross(turn.hold(dy_here))
    down_across = lax.ppermute(turn.hold(down_2), "grp", CHIP_SWAP)
    down_cross = chip_cross(turn.hold(down_3))
    qkv_all = (qkv_sent, qkv_beside, qkv_cross, qkv_corner)

    def rows_of_all(start, size):
        return in_order(*(part[start : start + size] for part in qkv_all))

    gain_row = slice_width + 2 * kv_slice
    gains = rows_of_all(gain_row, 8).reshape(4, 8, width)[:, :2, :slice_width]
    gains = gains.transpose(1, 0, 2).reshape(2, width).astype(jnp.float32)
    gain_attn = gains[0]
    gain_ffn = gains[1]
    a1_own = (n1 * gain_attn).astype(bf16)
    a1 = two_halves(a1_own, core_swap(a1_own))
    wq_t = rows_of_all(0, slice_width)
    wk_t = rows_of_all(slice_width, kv_slice)
    wv_t = rows_of_all(slice_width + kv_slice, kv_slice)

    k = rotate(dot_nt(a1, wk_t).reshape(4 * rows, KEY_VALUE_HEADS, HEAD_SIZE), cos_all, sin_all).astype(bf16)
    v = dot_nt(a1, wv_t).astype(bf16).reshape(4 * rows, KEY_VALUE_HEADS, HEAD_SIZE)
    k = k.transpose(1, 0, 2)
    v = v.transpose(1, 0, 2)
    q = rotate(dot_nt(a1_own, wq_t).reshape(half_rows, QUERY_HEADS, HEAD_SIZE), cos_own, sin_own).astype(bf16)
    q = q.reshape(half_rows, KEY_VALUE_HEADS, GROUP_QUERIES, HEAD_SIZE).transpose(1, 2, 0, 3)
    scores = jnp.einsum("hgcd,hld->hgcl", q, k, preferred_element_type=jnp.float32) * scale
    scores = jnp.where(allowed, scores, -jnp.inf)
    peak = jnp.max(scores, axis=-1, keepdims=True)
    logsum = peak + jnp.log(jnp.sum(jnp.exp(scores - peak), axis=-1, keepdims=True))
    probs = jnp.exp(scores - logsum)
    probs_low = probs.astype(bf16)
    mixed = jnp.einsum("hgcl,hld->hgcd", probs_low, v, preferred_element_type=jnp.float32).astype(bf16)
    o_own = mixed.transpose(2, 0, 1, 3).reshape(half_rows, width)
    turn.mark(o_own)

    wo_cross, dy_cross = turn.hold(wo_cross, dy_cross)
    wo_t = in_order(wo_sent, wo_beside, wo_cross, core_swap(wo_cross))
    x2 = xf + dot_nt(o_own, wo_t)
    r2 = norm_scale(x2)
    n2 = x2 * r2
    a2_own = (n2 * gain_ffn).astype(bf16)
    a2_beside = core_swap(a2_own)
    turn.mark(a2_own)
    down_across = turn.hold(down_across)
    dy_all = in_order(dy_here, dy_beside, dy_cross, core_swap(dy_cross), BLOCK_ORDER)
    a2 = two_halves(a2_own, a2_beside)

    gate = dot_nn(a2, w_gate)
    up = dot_nn(a2, w_up)
    gate, up, dy_all, down_across = lax.optimization_barrier((gate, up, dy_all, down_across))
    turn.mark(up)
    o_beside = core_swap(turn.hold(o_own))
    sig = jax.nn.sigmoid(gate)
    act = gate * sig
    hidden = (act * up).astype(bf16)
    down_cross = turn.hold(down_cross)
    down_rows_t = in_order(down_0, down_beside, down_cross, down_across)
    d_hidden = dot_nn(dy_all, down_rows_t)
    d_gate = (d_hidden * up * sig * (1.0 + gate * (1.0 - sig))).astype(bf16)
    d_up = (d_hidden * act).astype(bf16)
    d_a2_part = (dot_nt(d_gate, w_gate) + dot_nt(d_up, w_up)).astype(bf16)

    beside_part = core_swap(lax.dynamic_slice_in_dim(d_a2_part, beside_start, half_rows, 0))
    chip_sum = own_half(d_a2_part).astype(jnp.float32) + beside_part.astype(jnp.float32)
    chip_sent = chip_sum.astype(bf16)
    other_chip = chip_cross(chip_sent)
    turn.mark(chip_sent)
    a2_late, d_gate, d_up, hidden = turn.hold(a2, d_gate, d_up, hidden)
    gate_sum = RepSum(by_rep(dot_tn(a2_late, d_gate)), (0, 1))
    turn.mark(gate_sum.sent)
    up_sum = RepSum(by_rep(dot_tn(turn.hold(a2_late), d_up)), (1, 0))
    turn.mark(up_sum.sent)
    g_down = dot_tn(turn.hold(dy_all), hidden).reshape(2, 2, slice_width, hidden_slice)
    down_pair = swap_over_rep(g_down, 0, 1)
    turn.mark(down_pair[2])

    out_part = dot_nt(turn.hold(hidden), down_rows_t).astype(bf16)
    out_beside = core_swap(lax.dynamic_slice_in_dim(out_part, beside_start, half_rows, 0))
    out_chip = own_half(out_part).astype(jnp.float32) + out_beside.astype(jnp.float32)
    out_away = lax.dynamic_slice_in_dim(out_chip, rows - own_block_start, rows, 0).astype(bf16)
    turn.mark(out_away)

    other_chip = turn.hold(other_chip)
    d_a2 = chip_sum + other_chip.astype(jnp.float32)
    dyf = own_half(dy_all).astype(jnp.float32)
    d_n2 = d_a2 * gain_ffn
    d_x2 = dyf + r2 * (d_n2 - n2 * jnp.mean(d_n2 * n2, axis=-1, keepdims=True))
    d_x2_low = d_x2.astype(bf16)

    def column_parts(own):
        away = lax.dynamic_slice_in_dim(own, (me ^ 1) * slice_width, slice_width, 1)
        return own_cols(own), core_swap(away)

    d_o = dot_nn(d_x2_low, wo_t).astype(bf16)
    turn.mark(d_o)
    out_cross = chip_cross(turn.hold(out_away))
    up_sum.next(turn)
    d_o = turn.hold(d_o)
    d_o = d_o.reshape(half_rows, KEY_VALUE_HEADS, GROUP_QUERIES, HEAD_SIZE).transpose(1, 2, 0, 3)
    delta = jnp.sum(d_o.astype(jnp.float32) * mixed.astype(jnp.float32), axis=-1, keepdims=True)
    d_probs = jnp.einsum("hgcd,hld->hgcl", d_o, v, preferred_element_type=jnp.float32)
    d_scores = (probs * (d_probs - delta) * scale).astype(bf16)
    d_v = jnp.einsum("hgcl,hgcd->hld", probs_low, d_o, preferred_element_type=jnp.float32)
    d_k = jnp.einsum("hgcl,hgcd->hld", d_scores, q, preferred_element_type=jnp.float32)
    d_kv = jnp.concatenate([d_k, d_v], axis=0).transpose(1, 0, 2).reshape(4 * rows, 2 * kv_width)
    d_kv_sent = d_kv.astype(bf16)
    d_kv_beside = core_swap(d_kv_sent)
    turn.mark(d_kv_sent)
    d_scores = turn.hold(d_scores)
    d_q = jnp.einsum("hgcl,hld->hgcd", d_scores, k, preferred_element_type=jnp.float32)
    d_q = rotate(d_q.transpose(2, 0, 1, 3).reshape(half_rows, QUERY_HEADS, HEAD_SIZE), cos_own, -sin_own)
    d_q = d_q.reshape(half_rows, width).astype(bf16)
    d_q_columns = column_parts(d_q)
    turn.mark(d_q)
    gate_sum.next(turn)
    down_held = joined((down_pair[0], turn.hold(down_pair[1])))
    down_pair = swap_over_rep(down_held, 1, 0)
    turn.mark(down_pair[2])

    d_kv, d_kv_beside = turn.hold(d_kv, d_kv_beside)
    d_kv = d_kv + d_kv_beside.astype(jnp.float32)
    d_k = rotate(
        d_kv[:, :kv_width].reshape(4 * rows, KEY_VALUE_HEADS, HEAD_SIZE), cos_all, -sin_all
    ).reshape(4 * rows, kv_width).astype(bf16)
    d_v = d_kv[:, kv_width:].astype(bf16)
    d_a1 = (
        dot_nn(own_block(d_q), wq_t)
        + dot_nn(own_block(own_half(d_k)), wk_t)
        + dot_nn(own_block(own_half(d_v)), wv_t)
    )
    n1_block = own_block(n1)
    g_attn = jnp.sum(d_a1 * n1_block, axis=0)
    g_ffn = jnp.sum(own_block(d_a2 * n2), axis=0)
    g_gains = jnp.stack([g_attn, g_ffn]).reshape(2, 4, slice_width).transpose(1, 0, 2)

    def gain_piece(k):
        return lax.dynamic_index_in_dim(g_gains, me ^ k, 0, keepdims=False)

    gains_came = (
        core_swap(gain_piece(1)),
        lax.ppermute(gain_piece(2), "grp", CHIP_SWAP),
        chip_cross(gain_piece(3)),
    )
    turn.mark(g_gains)

    g_kv = by_rep(dot_tn(turn.hold(a1), jnp.concatenate([own_cols(d_k), own_cols(d_v)], axis=1)))
    g_q = by_rep(dot_tn(turn.hold(a1), two_halves(*d_q_columns)))
    g_out = by_rep(dot_tn(turn.hold(two_halves(o_own, o_beside)), two_halves(*column_parts(d_x2_low))))
    turn.mark(g_out)
    gains_came = turn.hold(*gains_came)
    g_gains = gain_piece(0) + gains_came[0] + gains_came[1] + gains_came[2]
    count = g_q.shape[0]
    share = g_q.shape[1]
    riders = jnp.broadcast_to(jnp.pad(g_gains, ((0, 6), (0, 0))), (count, 8, slice_width))
    g_kv = jnp.pad(g_kv, ((0, 0), (0, 0), (0, slice_width - 2 * kv_slice)))
    bundle = jnp.concatenate([g_q, g_out, g_kv, riders], axis=1)
    bundle = with_layout_constraint(bundle, Layout(major_to_minor=(0, 1, 2)))
    attn_sum = RepSum(bundle, (0, 1))
    turn.mark(attn_sum.sent)

    up_sum.next(turn)
    gate_sum.next(turn)
    down_held = joined((down_pair[0], turn.hold(down_pair[1])))
    parts = count // 4
    down_held = down_held.reshape(slice_width, parts, hidden_slice // parts).transpose(1, 0, 2)
    down_held = down_held.reshape((2,) * (parts.bit_length() - 1) + (slice_width, hidden_slice // parts))
    down_pair = swap_over_rep(down_held, rep_bits() - 1, 0)
    turn.mark(down_pair[2])

    attn_sum.next(turn)
    d_a1_late, d_x2_late = turn.hold(d_a1, d_x2)
    d_n1 = d_a1_late * gain_attn
    input_grad = own_block(d_x2_late) + own_block(r1) * (
        d_n1 - n1_block * jnp.mean(d_n1 * n1_block, axis=-1, keepdims=True)
    )
    block_output = own_block(x2) + own_block(out_chip) + turn.hold(out_cross).astype(jnp.float32)
    input_grad, block_output = lax.optimization_barrier((input_grad, block_output))
    turn.mark(block_output)

    down_held = joined((down_pair[0], turn.hold(down_pair[1])))
    for bit in reversed(range(2, rep_bits() - 1)):
        down_held = joined(swap_over_rep(down_held, bit, 0))
    homes = [
        (j * count + r, (r & 3) * count + j * parts + (r >> 2)) for r in range(count) for j in range(4)
    ]
    down_sent = down_held.astype(bf16)
    g_down = lax.ppermute(down_sent, ("grp", "rep"), homes)
    turn.mark(down_sent)
    attn_sum.next(turn)
    g_gate = gate_sum.end(turn)
    g_up = up_sum.end(turn)
    g_down = turn.hold(g_down).astype(jnp.float32).T
    g_gate, g_up, g_down = lax.optimization_barrier((g_gate, g_up, g_down))
    turn.mark(g_down)
    g_attn_w = attn_sum.end(turn)
    g_kv = g_attn_w[2 * share : 3 * share]
    return (
        block_output[None],
        input_grad[None],
        g_attn_w[3 * share : 3 * share + 2],
        g_attn_w[:share],
        g_kv[:, :kv_slice],
        g_kv[:, kv_slice : 2 * kv_slice],
        g_attn_w[share : 2 * share],
        g_gate,
        g_up,
        g_down,
    )


def solution(mesh):
    rows = P("rep", "grp", None)
    weight = P(None, "grp")
    grad = P("rep", "grp")
    return jax.shard_map(
        per_device,
        mesh=mesh,
        in_specs=(rows, rows) + (weight,) * 8,
        out_specs=(rows, rows, weight) + (grad,) * 7,
        check_vma=False,
    )
```

profile of v0, /device:TPU:5, one launch (start us, length us, event | category | flops | bytes accessed | tf_op | source)
XLA Modules:
  0.0 206.3 jit_solution(5297859501089913483)
XLA Ops:
  0.7 1.4 copy.46
  2.8 2.0 pad_maximum_fusion.8
  4.8 1.8 collective-permute-start.2
  6.6 1.2 copy.47
  10.4 15.9 %collective-permute-done.2 = bf16[408,960]{1,0:T(8,128)(2,1)} collective-permute-done((bf16[408,960]{1,0:T(8,128)(2,1)}, bf16[408,960]{1,0:T(8,128)(2,1)}, u32[]{:S(2)}, u32[]{:S(2)}) %collective-permute-start.2) | collective-permute-done | bytes 783392 | tf_op jit(solution)/shard_map/ppermute | solution.py:173
  26.6 1.1 dynamic-slice_bitcast_fusion
  27.8 3.7 %collective-permute-done = bf16[128,960]{0,1:T(8,128)(2,1)} collective-permute-done((bf16[128,960]{0,1:T(8,128)(2,1)}, bf16[128,960]{0,1:T(8,128)(2,1)}, u32[]{:S(2)}, u32[]{:S(2)}) %collective-permute-start) | collective-permute-done | bytes 245792 | tf_op jit(solution)/shard_map/ppermute | solution.py:173
  31.5 1.1 broadcast_select_fusion.7
  32.8 1.6 collective-permute-start.7
  36.3 1.1 convert_multiply_fusion
  37.8 1.6 select_select_fusion.7
  40.8 1.2 select_select_fusion.19
  42.2 1.3 select_select_fusion.23
  44.7 1.6 fusion.1
  46.3 2.1 %exponential_reduce_fusion = f32[5,3,256]{2,1,0:T(4,128)S(1)} fusion(f32[5,3,256,512]{3,2,1,0:T(8,128)S(1)} %get-tuple-element.252, f32[5,3,256]{2,1,0:T(4,128)S(1)} %get-tuple-element.251, pred[256,512]{1,0:T(8,128)(4,1)S(1)} %broadcast_compare_fusion), kind=kLoop, calls=%fused_computation.2 | loop fusion | flops 7860480 | bytes 8026112 | tf_op jit(solution)/shard_map/reduce_sum | solution.py:264
  49.5 2.4 %convolution_convert_fusion.2 = bf16[5,3,256,64]{2,3,1,0:T(8,128)(2,1)S(1)} fusion(bf16[5,512,64,1]{1,2,3,0:T(8,128)(2,1)S(1)} %bitcast.246, f32[5,3,256,512]{3,2,1,0:T(8,128)S(1)} %get-tuple-element.252, f32[5,3,256]{2,1,0:T(4,128)S(1)} %log_add_fusion, pred[256,512]{1,0:T(8,128)(4,1)S(1)} %broadcast_compare_fusion), kind=kOutput, calls=%fused_computation.27 | convolution fusion | flops 259768320 | bytes 8829952 | tf_op jit(solution)/shard_map/hgcl,hld->hgcd/dot_general | solution.py:267
  52.8 1.4 collective-permute-done.8
  54.2 1.4 select_select_fusion.3
  56.8 1.1 multiply_convert_fusion.4
  58.5 1.3 collective-permute-start.14
  60.0 1.4 select_select_fusion.15
  61.5 12.6 %collective-permute-done.12 = bf16[240,640]{1,0:T(8,128)(2,1)S(1)} collective-permute-done((bf16[240,640]{1,0:T(8,128)(2,1)}, bf16[240,640]{1,0:T(8,128)(2,1)S(1)}, u32[]{:S(2)}, u32[]{:S(2)}) %collective-permute-start.12) | collective-permute-done | bytes 307232 | tf_op jit(solution)/shard_map/ppermute | solution.py:237
  74.1 1.2 broadcast_select_fusion.3
  75.4 1.0 fusion.79
  77.7 1.2 select_select_fusion.11
  78.9 1.5 multiply_convert_fusion.1
  87.8 1.1 fusion.10
  92.2 1.1 pad_maximum_fusion.4
  93.3 1.3 collective-permute-start.16
  94.8 1.3 collective-permute-start.18
  96.1 1.2 collective-permute-start.20
  97.4 1.0 pad_maximum_fusion.7
  99.4 7.3 %collective-permute-done.16 = bf16[256,960]{0,1:T(8,128)(2,1)S(1)} collective-permute-done((bf16[256,960]{0,1:T(8,128)(2,1)S(1)}, bf16[256,960]{0,1:T(8,128)(2,1)S(1)}, u32[]{:S(2)}, u32[]{:S(2)}) %collective-permute-start.16) | collective-permute-done | bytes 491552 | tf_op jit(solution)/shard_map/ppermute | solution.py:173
  107.0 1.4 fusion.80
  108.7 2.9 %convolution_convert_fusion.1 = bf16[256,960]{0,1:T(8,128)(2,1)S(1)} fusion(bf16[256,960]{0,1:T(8,128)(2,1)} %get-tuple-element.176, bf16[240,960]{1,0:T(8,128)(2,1)} %copy-done.58, bf16[240,960]{1,0:T(8,128)(2,1)} %copy-done.59, bf16[240,960]{1,0:T(8,128)(2,1)} %copy-done.60, bf16[240,960]{1,0:T(8,128)(2,1)} %copy-done.57), kind=kOutput, calls=%fused_computation.26 | convolution fusion | flops 479477760 | bytes 2826240 | tf_op jit(solution)/shard_map/dot_general | solution.py:45
  111.8 1.6 collective-permute-start.32
  113.4 2.5 %bitcast_add_fusion.3 = f32[2,2,120,640]{3,2,0,1:T(8,128)} fusion(bf16[2,2,120,640]{3,2,0,1:T(8,128)(2,1)} %collective-permute-done.18, f32[2,2,2,120,640]{4,3,2,1,0:T(8,128)S(1)} %bitcast.203, s32[]{:T(128)S(6)} %select_n.681), kind=kLoop, calls=%fused_computation.35 | loop fusion | flops 614400 | bytes 3072004 | tf_op jit(solution)/shard_map/add | solution.py:94
  115.9 1.8 fusion.16
  118.2 4.6 %convolution_bitcast_fusion = f32[5,512,64]{1,2,0:T(8,128)S(1)} fusion(bf16[5,3,256,64]{2,3,1,0:T(8,128)(2,1)S(1)} %bitcast.240, f32[5,3,256,512]{3,2,1,0:T(8,128)} %copy-done.7, f32[5,3,256]{2,1,0:T(4,128)S(1)} %copy-done.86, pred[256,512]{1,0:T(8,128)(4,1)S(1)} %copy-done.48), kind=kOutput, calls=%fused_computation.28 | convolution fusion | flops 259522560 | bytes 9157632 | tf_op jit(solution)/shard_map/hgcl,hgcd->hld/dot_general | solution.py:338
  122.8 3.3 %multiply_convert_fusion = bf16[5,3,256,512]{3,2,1,0:T(8,128)(2,1)S(1)} fusion(f32[5,3,256,512]{3,2,1,0:T(8,128)S(1)} %bitcast.208, f32[5,3,256]{2,1,0:T(4,128)S(1)} %multiply_reduce_fusion, f32[5,3,256]{2,1,0:T(4,128)S(1)} %copy-done.86, pred[256,512]{1,0:T(8,128)(4,1)S(1)} %copy-done.48, bf16[5,3,256,64]{2,3,1,0:T(8,128)(2,1)S(1)} %bitcast.241, ...), kind=kOutput, calls=%fused_computation | convolution fusion | flops 265420800 | bytes 12777472 | tf_op jit(solution)/shard_map/hgcd,hld->hgcl/dot_general | solution.py:336
  128.0 1.3 fusion.28
  129.9 1.1 copy-done.3
  131.0 1.2 bitcast_add_fusion.1
  133.4 1.2 bitcast_add_fusion.2
  141.8 1.4 collective-permute-start.26
  143.1 1.5 fusion.19
  145.6 1.3 collective-permute-start.29
  147.5 1.3 constant_dynamic-slice_fusion.5
  148.7 3.0 %copy.53 = f32[2,2,1,368,240]{3,4,1,0,2:T(8,128)} copy(f32[2,2,1,368,240]{4,3,2,1,0:T(8,128)} %constant_dynamic-slice_fusion.5) | data formatting | bytes 2826240 | tf_op jit(solution)/shard_map/jit(dynamic_index_in_dim)/dynamic_slice | solution.py:90
  152.7 2.4 %copy.66 = bf16[2,2,1,368,240]{3,4,1,0,2:T(8,128)(2,1)} copy(bf16[2,2,1,368,240]{4,3,2,1,0:T(8,128)(2,1)} %constant_dynamic-slice_fusion.4) | data formatting | bytes 1413120
  155.1 1.1 collective-permute-start.28
  156.2 1.2 bitcast_add_fusion.5
  158.2 2.3 %collective-permute-start.37 = (bf16[120,640]{1,0:T(8,128)(2,1)}, bf16[120,640]{1,0:T(8,128)(2,1)}, u32[]{:S(2)}, u32[]{:S(2)}) collective-permute-start(bf16[120,640]{1,0:T(8,128)(2,1)} %fusion.36), channel_id=1, source_target_pairs={{0,4},{1,5},{2,6},{3,7},{4,0},{5,1},{6,2},{7,3},{8,12},{9,13},{10,... | collective-permute-start | bytes 460808 | tf_op jit(solution)/shard_map/ppermute | solution.py:89
  162.7 2.3 %collective-permute-start.36 = (bf16[120,640]{1,0:T(8,128)(2,1)}, bf16[120,640]{1,0:T(8,128)(2,1)}, u32[]{:S(2)}, u32[]{:S(2)}) collective-permute-start(bf16[120,640]{1,0:T(8,128)(2,1)} %fusion.37), channel_id=1, source_target_pairs={{0,4},{1,5},{2,6},{3,7},{4,0},{5,1},{6,2},{7,3},{8,12},{9,13},{10,... | collective-permute-start | bytes 460808 | tf_op jit(solution)/shard_map/ppermute | solution.py:89
  166.6 5.8 %collective-permute-done.28 = bf16[2,2,368,240]{2,3,1,0:T(8,128)(2,1)} collective-permute-done((bf16[2,2,368,240]{2,3,1,0:T(8,128)(2,1)}, bf16[2,2,368,240]{2,3,1,0:T(8,128)(2,1)}, u32[]{:S(2)}, u32[]{:S(2)}) %collective-permute-start.28) | collective-permute-done | bytes 706592 | tf_op jit(solution)/shard_map/ppermute | solution.py:89
  172.4 1.2 bitcast_add_fusion
  173.7 1.3 collective-permute-start.33
  176.2 1.9 convert_add_fusion.5
  178.1 2.7 %collective-permute-done.34 = bf16[240,320]{0,1:T(8,128)(2,1)S(1)} collective-permute-done((bf16[240,320]{0,1:T(8,128)(2,1)S(1)}, bf16[240,320]{0,1:T(8,128)(2,1)S(1)}, u32[]{:S(2)}, u32[]{:S(2)}) %collective-permute-start.34) | collective-permute-done | bytes 153632 | tf_op jit(solution)/shard_map/ppermute | solution.py:89
  180.8 3.4 %collective-permute-start.38 = (bf16[240,320]{0,1:T(8,128)(2,1)S(1)}, bf16[240,320]{0,1:T(8,128)(2,1)S(1)}, u32[]{:S(2)}, u32[]{:S(2)}) collective-permute-start(bf16[240,320]{0,1:T(8,128)(2,1)S(1)} %fusion.14), channel_id=1, source_target_pairs={{0,0},{8,2},{16,4},{24,6},{1,8},{9,10},{17,12},{25,14},{2,16},{10,... | collective-permute-start | bytes 460808 | tf_op jit(solution)/shard_map/ppermute | solution.py:422
  184.2 8.8 %collective-permute-done.33 = bf16[2,368,240]{1,2,0:T(8,128)(2,1)S(1)} collective-permute-done((bf16[2,368,240]{1,2,0:T(8,128)(2,1)S(1)}, bf16[2,368,240]{1,2,0:T(8,128)(2,1)S(1)}, u32[]{:S(2)}, u32[]{:S(2)}) %collective-permute-start.33) | collective-permute-done | bytes 353312 | tf_op jit(solution)/shard_map/ppermute | solution.py:89
  193.9 1.8 bitcast_add_fusion.10
  196.4 1.7 bitcast_add_fusion.11
  198.1 5.0 %collective-permute-done.35 = bf16[368,240]{0,1:T(8,128)(2,1)S(1)} collective-permute-done((bf16[368,240]{0,1:T(8,128)(2,1)S(1)}, bf16[368,240]{0,1:T(8,128)(2,1)S(1)}, u32[]{:S(2)}, u32[]{:S(2)}) %collective-permute-start.35) | collective-permute-done | bytes 176672 | tf_op jit(solution)/shard_map/ppermute | solution.py:89
  (345 shorter events, 50.5 us)
Async XLA Ops:
  0.6 74.7 %copy-start = (bf16[960,640]{1,0:T(8,128)(2,1)S(1)}, bf16[960,640]{1,0:T(8,128)(2,1)}, u32[]{:S(2)}) copy-start(bf16[960,640]{1,0:T(8,128)(2,1)} %param.18) | copy-start | bytes 3686404
  0.7 7.9 %copy-start.88 = (s32[512]{0:T(512)S(1)}, s32[512]{0:T(512)}, u32[]{:S(2)}) copy-start(s32[512]{0:T(512)} %constant.164.clone) | copy-start | bytes 6148
  0.7 25.9 %copy-start.32 = (bf16[2560,240]{0,1:T(8,128)(2,1)S(1)}, bf16[2560,240]{0,1:T(8,128)(2,1)}, u32[]{:S(2)}) copy-start(bf16[2560,240]{0,1:T(8,128)(2,1)} %param.20) | copy-start | bytes 3686404
  4.8 21.5 %collective-permute-start.2 = (bf16[408,960]{1,0:T(8,128)(2,1)}, bf16[408,960]{1,0:T(8,128)(2,1)}, u32[]{:S(2)}, u32[]{:S(2)}) collective-permute-start(bf16[408,960]{1,0:T(8,128)(2,1)} %pad_maximum_fusion.8), channel_id=1, source_target_pairs={{0,24},{24,0},{8,16},{16,8},{1,25},{25,1},{9,17},{17,9},{2,26},{26... | collective-permute-start | bytes 2350088 | tf_op jit(solution)/shard_map/ppermute | solution.py:173
  6.5 24.9 %collective-permute-start = (bf16[128,960]{0,1:T(8,128)(2,1)}, bf16[128,960]{0,1:T(8,128)(2,1)}, u32[]{:S(2)}, u32[]{:S(2)}) collective-permute-start(bf16[128,960]{0,1:T(8,128)(2,1)} %bitcast.7), channel_id=1, source_target_pairs={{0,24},{24,0},{8,16},{16,8},{1,25},{25,1},{9,17},{17,9},{2,26},{26... | collective-permute-start | bytes 737288 | tf_op jit(solution)/shard_map/ppermute | solution.py:173
  7.8 45.0 %collective-permute-start.5 = (bf16[240,960]{1,0:T(8,128)(2,1)S(1)}, bf16[240,960]{1,0:T(8,128)(2,1)}, u32[]{:S(2)}, u32[]{:S(2)}) collective-permute-start(bf16[240,960]{1,0:T(8,128)(2,1)S(1)} %bitcast.219), channel_id=1, source_target_pairs={{0,8},{8,0},{16,24},{24,16},{1,9},{9,1},{17,25},{25,17},{2,10},{10... | collective-permute-start | bytes 1382408 | tf_op jit(solution)/shard_map/ppermute | solution.py:170
  8.5 26.1 %collective-permute-start.1 = (bf16[408,960]{1,0:T(8,128)(2,1)}, bf16[408,960]{1,0:T(8,128)(2,1)}, u32[]{:S(2)}, u32[]{:S(2)}) collective-permute-start(bf16[408,960]{1,0:T(8,128)(2,1)} %pad_maximum_fusion.8), channel_id=1, source_target_pairs={{0,8},{8,0},{16,24},{24,16},{1,9},{9,1},{17,25},{25,17},{2,10},{10... | collective-permute-start | bytes 2350088 | tf_op jit(solution)/shard_map/ppermute | solution.py:170
  10.4 24.2 %copy-start.89 = (bf16[2,240]{1,0:T(2,128)(2,1)S(1)}, bf16[2,240]{1,0:T(2,128)(2,1)}, u32[]{:S(2)}) copy-start(bf16[2,240]{1,0:T(2,128)(2,1)} %param.13) | copy-start | bytes 2884
  26.3 8.3 %collective-permute-start.3 = (bf16[408,960]{1,0:T(8,128)(2,1)}, bf16[408,960]{1,0:T(8,128)(2,1)}, u32[]{:S(2)}, u32[]{:S(2)}) collective-permute-start(bf16[408,960]{1,0:T(8,128)(2,1)} %collective-permute-done.2), channel_id=1, source_target_pairs={{0,8},{8,0},{16,24},{24,16},{1,9},{9,1},{17,25},{25,17},{2,10},{10... | collective-permute-start | bytes 2350088 | tf_op jit(solution)/shard_map/ppermute | solution.py:170
  27.8 21.2 %copy-start.47 = (pred[256,512]{1,0:T(8,128)(4,1)}, pred[256,512]{1,0:T(8,128)(4,1)S(1)}, u32[]{:S(2)}) copy-start(pred[256,512]{1,0:T(8,128)(4,1)S(1)} %broadcast_compare_fusion) | copy-start | bytes 393220
  32.8 51.8 %copy-start.87 = (f32[256]{0:T(256)}, f32[256]{0:T(256)S(1)}, u32[]{:S(2)}) copy-start(f32[256]{0:T(256)S(1)} %add_rsqrt_fusion.1) | copy-start | bytes 3076
  32.8 19.2 %collective-permute-start.7 = (bf16[128,960]{0,1:T(8,128)(2,1)}, bf16[128,960]{0,1:T(8,128)(2,1)}, u32[]{:S(2)}, u32[]{:S(2)}) collective-permute-start(bf16[128,960]{0,1:T(8,128)(2,1)} %bitcast.28), channel_id=1, source_target_pairs={{0,24},{24,0},{8,16},{16,8},{1,25},{25,1},{9,17},{17,9},{2,26},{26... | collective-permute-start | bytes 737288 | tf_op jit(solution)/shard_map/ppermute | solution.py:173
  34.4 17.7 %collective-permute-start.6 = (bf16[240,960]{1,0:T(8,128)(2,1)S(1)}, bf16[240,960]{1,0:T(8,128)(2,1)}, u32[]{:S(2)}, u32[]{:S(2)}) collective-permute-start(bf16[240,960]{1,0:T(8,128)(2,1)S(1)} %bitcast.220), channel_id=1, source_target_pairs={{0,24},{24,0},{8,16},{16,8},{1,25},{25,1},{9,17},{17,9},{2,26},{26... | collective-permute-start | bytes 1382408 | tf_op jit(solution)/shard_map/ppermute | solution.py:173
  37.4 6.1 %collective-permute-start.4 = (bf16[256,960]{0,1:T(8,128)(2,1)S(1)}, bf16[256,960]{0,1:T(8,128)(2,1)S(1)}, u32[]{:S(2)}, u32[]{:S(2)}) collective-permute-start(bf16[256,960]{0,1:T(8,128)(2,1)S(1)} %get-tuple-element.237), channel_id=1, source_target_pairs={{0,8},{8,0},{16,24},{24,16},{1,9},{9,1},{17,25},{25,17},{2,10},{10... | collective-permute-start | bytes 1474568 | tf_op jit(solution)/shard_map/ppermute | solution.py:170
  41.9 6.5 %copy-start.76 = (bf16[80,960]{1,0:T(8,128)(2,1)}, bf16[80,960]{1,0:T(8,128)(2,1)S(1)}, u32[]{:S(2)}) copy-start(bf16[80,960]{1,0:T(8,128)(2,1)S(1)} %get-tuple-element.192) | copy-start | bytes 460804
  42.0 6.5 %copy-start.78 = (bf16[80,960]{1,0:T(8,128)(2,1)}, bf16[80,960]{1,0:T(8,128)(2,1)S(1)}, u32[]{:S(2)}) copy-start(bf16[80,960]{1,0:T(8,128)(2,1)S(1)} %get-tuple-element.193) | copy-start | bytes 460804
  42.0 6.5 %copy-start.80 = (bf16[80,960]{1,0:T(8,128)(2,1)}, bf16[80,960]{1,0:T(8,128)(2,1)S(1)}, u32[]{:S(2)}) copy-start(bf16[80,960]{1,0:T(8,128)(2,1)S(1)} %get-tuple-element.194) | copy-start | bytes 460804
  42.0 6.5 %copy-start.82 = (bf16[80,960]{1,0:T(8,128)(2,1)}, bf16[80,960]{1,0:T(8,128)(2,1)S(1)}, u32[]{:S(2)}) copy-start(bf16[80,960]{1,0:T(8,128)(2,1)S(1)} %get-tuple-element.195) | copy-start | bytes 460804
  43.6 4.9 %copy-start.24 = (bf16[256,960]{0,1:T(8,128)(2,1)}, bf16[256,960]{0,1:T(8,128)(2,1)S(1)}, u32[]{:S(2)}) copy-start(bf16[256,960]{0,1:T(8,128)(2,1)S(1)} %get-tuple-element.226) | copy-start | bytes 1474564
  52.0 2.1 %collective-permute-start.8 = (bf16[240,960]{1,0:T(8,128)(2,1)}, bf16[240,960]{1,0:T(8,128)(2,1)S(1)}, u32[]{:S(2)}, u32[]{:S(2)}) collective-permute-start(bf16[240,960]{1,0:T(8,128)(2,1)} %collective-permute-done.6), channel_id=1, source_target_pairs={{0,8},{8,0},{16,24},{24,16},{1,9},{9,1},{17,25},{25,17},{2,10},{10... | collective-permute-start | bytes 1382408 | tf_op jit(solution)/shard_map/ppermute | solution.py:170
  52.2 7.6 %collective-permute-start.10 = (bf16[128,960]{0,1:T(8,128)(2,1)}, bf16[128,960]{0,1:T(8,128)(2,1)}, u32[]{:S(2)}, u32[]{:S(2)}) collective-permute-start(bf16[128,960]{0,1:T(8,128)(2,1)} %bitcast.28), channel_id=1, source_target_pairs={{0,8},{8,0},{16,24},{24,16},{1,9},{9,1},{17,25},{25,17},{2,10},{10... | collective-permute-start | bytes 737288 | tf_op jit(solution)/shard_map/ppermute | solution.py:170
  52.7 7.3 %collective-permute-start.11 = (bf16[128,960]{0,1:T(8,128)(2,1)}, bf16[128,960]{0,1:T(8,128)(2,1)}, u32[]{:S(2)}, u32[]{:S(2)}) collective-permute-start(bf16[128,960]{0,1:T(8,128)(2,1)} %collective-permute-done.7), channel_id=1, source_target_pairs={{0,8},{8,0},{16,24},{24,16},{1,9},{9,1},{17,25},{25,17},{2,10},{10... | collective-permute-start | bytes 737288 | tf_op jit(solution)/shard_map/ppermute | solution.py:170
  57.9 16.2 %collective-permute-start.9 = (bf16[256,960]{0,1:T(8,128)(2,1)}, bf16[256,960]{0,1:T(8,128)(2,1)}, u32[]{:S(2)}, u32[]{:S(2)}) collective-permute-start(bf16[256,960]{0,1:T(8,128)(2,1)} %get-tuple-element.180), channel_id=1, source_target_pairs={{0,8},{8,0},{16,24},{24,16},{1,9},{9,1},{17,25},{25,17},{2,10},{10... | collective-permute-start | bytes 1474568 | tf_op jit(solution)/shard_map/ppermute | solution.py:170
  58.1 19.6 %collective-permute-start.13 = (bf16[240,640]{1,0:T(8,128)(2,1)}, bf16[240,640]{1,0:T(8,128)(2,1)}, u32[]{:S(2)}, u32[]{:S(2)}) collective-permute-start(bf16[240,640]{1,0:T(8,128)(2,1)} %get-tuple-element.210), channel_id=1, source_target_pairs={{0,8},{8,0},{16,24},{24,16},{1,9},{9,1},{17,25},{25,17},{2,10},{10... | collective-permute-start | bytes 921608 | tf_op jit(solution)/shard_map/ppermute | solution.py:170
  58.5 19.2 %collective-permute-start.14 = (bf16[240,640]{1,0:T(8,128)(2,1)}, bf16[240,640]{1,0:T(8,128)(2,1)S(1)}, u32[]{:S(2)}, u32[]{:S(2)}) collective-permute-start(bf16[240,640]{1,0:T(8,128)(2,1)} %get-tuple-element.99), channel_id=1, source_target_pairs={{0,24},{24,0},{8,16},{16,8},{1,25},{25,1},{9,17},{17,9},{2,26},{26... | collective-permute-start | bytes 921608 | tf_op jit(solution)/shard_map/ppermute | solution.py:173
  59.7 14.4 %collective-permute-start.12 = (bf16[240,640]{1,0:T(8,128)(2,1)}, bf16[240,640]{1,0:T(8,128)(2,1)S(1)}, u32[]{:S(2)}, u32[]{:S(2)}) collective-permute-start(bf16[240,640]{1,0:T(8,128)(2,1)} %get-tuple-element.95), channel_id=1, source_target_pairs={{0,16},{16,0},{8,24},{24,8},{1,17},{17,1},{9,25},{25,9},{2,18},{18... | collective-permute-start | bytes 921608 | tf_op jit(solution)/shard_map/ppermute | solution.py:237
  82.4 2.4 %collective-permute-start.15 = (bf16[256,960]{0,1:T(8,128)(2,1)S(1)}, bf16[256,960]{0,1:T(8,128)(2,1)S(1)}, u32[]{:S(2)}, u32[]{:S(2)}) collective-permute-start(bf16[256,960]{0,1:T(8,128)(2,1)S(1)} %constant_dynamic-slice_fusion.19), channel_id=1, source_target_pairs={{0,8},{8,0},{16,24},{24,16},{1,9},{9,1},{17,25},{25,17},{2,10},{10... | collective-permute-start | bytes 1474568 | tf_op jit(solution)/shard_map/ppermute | solution.py:170
  84.6 11.5 %collective-permute-start.23 = (bf16[256,960]{0,1:T(8,128)(2,1)S(1)}, bf16[256,960]{0,1:T(8,128)(2,1)S(1)}, u32[]{:S(2)}, u32[]{:S(2)}) collective-permute-start(bf16[256,960]{0,1:T(8,128)(2,1)S(1)} %bitcast.218), channel_id=1, source_target_pairs={{0,8},{8,0},{16,24},{24,16},{1,9},{9,1},{17,25},{25,17},{2,10},{10... | collective-permute-start | bytes 1474568 | tf_op jit(solution)/shard_map/ppermute | solution.py:170
  91.8 6.7 %collective-permute-start.17 = (bf16[256,960]{0,1:T(8,128)(2,1)S(1)}, bf16[256,960]{0,1:T(8,128)(2,1)S(1)}, u32[]{:S(2)}, u32[]{:S(2)}) collective-permute-start(bf16[256,960]{0,1:T(8,128)(2,1)S(1)} %constant_dynamic-slice_fusion.16), channel_id=1, source_target_pairs={{0,8},{8,0},{16,24},{24,16},{1,9},{9,1},{17,25},{25,17},{2,10},{10... | collective-permute-start | bytes 1474568 | tf_op jit(solution)/shard_map/ppermute | solution.py:170
  93.3 13.4 %collective-permute-start.16 = (bf16[256,960]{0,1:T(8,128)(2,1)S(1)}, bf16[256,960]{0,1:T(8,128)(2,1)S(1)}, u32[]{:S(2)}, u32[]{:S(2)}) collective-permute-start(bf16[256,960]{0,1:T(8,128)(2,1)S(1)} %fusion.7), channel_id=1, source_target_pairs={{0,24},{24,0},{8,16},{16,8},{1,25},{25,1},{9,17},{17,9},{2,26},{26... | collective-permute-start | bytes 1474568 | tf_op jit(solution)/shard_map/ppermute | solution.py:173
  94.6 34.9 %collective-permute-start.21 = (bf16[2,2,120,640]{3,2,0,1:T(8,128)(2,1)}, bf16[2,2,120,640]{3,2,0,1:T(8,128)(2,1)}, u32[]{:S(2)}, u32[]{:S(2)}) collective-permute-start(bf16[2,2,120,640]{3,2,0,1:T(8,128)(2,1)} %fusion.9), channel_id=1, source_target_pairs={{0,1},{1,0},{2,3},{3,2},{4,5},{5,4},{6,7},{7,6},{8,9},{9,8},{10,11... | collective-permute-start | bytes 1843208 | tf_op jit(solution)/shard_map/ppermute | solution.py:89
  94.8 18.6 %collective-permute-start.18 = (bf16[2,2,120,640]{3,2,0,1:T(8,128)(2,1)}, bf16[2,2,120,640]{3,2,0,1:T(8,128)(2,1)}, u32[]{:S(2)}, u32[]{:S(2)}) collective-permute-start(bf16[2,2,120,640]{3,2,0,1:T(8,128)(2,1)} %fusion.10), channel_id=1, source_target_pairs={{0,2},{1,3},{2,0},{3,1},{4,6},{5,7},{6,4},{7,5},{8,10},{9,11},{10,... | collective-permute-start | bytes 1843208 | tf_op jit(solution)/shard_map/ppermute | solution.py:89
  96.1 36.9 %collective-permute-start.20 = (bf16[2,240,640]{2,1,0:T(8,128)(2,1)}, bf16[2,240,640]{2,1,0:T(8,128)(2,1)}, u32[]{:S(2)}, u32[]{:S(2)}) collective-permute-start(bf16[2,240,640]{2,1,0:T(8,128)(2,1)} %fusion.8), channel_id=1, source_target_pairs={{0,1},{1,0},{2,3},{3,2},{4,5},{5,4},{6,7},{7,6},{8,9},{9,8},{10,11... | collective-permute-start | bytes 1843208 | tf_op jit(solution)/shard_map/ppermute | solution.py:89
  98.6 8.1 %copy-start.16 = (f32[256,960]{0,1:T(8,128)}, f32[256,960]{0,1:T(8,128)S(1)}, u32[]{:S(2)}) copy-start(f32[256,960]{0,1:T(8,128)S(1)} %convert_add_fusion.3) | copy-start | bytes 2949124
  111.6 6.3 %copy-start.23 = (bf16[5,3,256,64]{2,3,1,0:T(8,128)(2,1)S(1)}, bf16[5,3,256,64]{2,3,1,0:T(8,128)(2,1)}, u32[]{:S(2)}) copy-start(bf16[5,3,256,64]{2,3,1,0:T(8,128)(2,1)} %copy-done.21) | copy-start | bytes 1474564
  111.7 6.5 %copy-start.48 = (pred[256,512]{1,0:T(8,128)(4,1)S(1)}, pred[256,512]{1,0:T(8,128)(4,1)}, u32[]{:S(2)}) copy-start(pred[256,512]{1,0:T(8,128)(4,1)} %copy-done.47) | copy-start | bytes 393220
  111.7 6.5 %copy-start.86 = (f32[5,3,256]{2,1,0:T(4,128)S(1)}, f32[5,3,256]{2,1,0:T(4,128)}, u32[]{:S(2)}) copy-start(f32[5,3,256]{2,1,0:T(4,128)} %copy-done.85) | copy-start | bytes 46084
  111.7 23.8 %collective-permute-start.24 = (bf16[256,240]{0,1:T(8,128)(2,1)S(1)}, bf16[256,240]{0,1:T(8,128)(2,1)S(1)}, u32[]{:S(2)}, u32[]{:S(2)}) collective-permute-start(bf16[256,240]{0,1:T(8,128)(2,1)S(1)} %constant_dynamic-slice_fusion.12), channel_id=1, source_target_pairs={{0,8},{8,0},{16,24},{24,16},{1,9},{9,1},{17,25},{25,17},{2,10},{10... | collective-permute-start | bytes 368648 | tf_op jit(solution)/shard_map/ppermute | solution.py:170
  111.8 63.2 %collective-permute-start.32 = (bf16[128,960]{0,1:T(8,128)(2,1)}, bf16[128,960]{0,1:T(8,128)(2,1)}, u32[]{:S(2)}, u32[]{:S(2)}) collective-permute-start(bf16[128,960]{0,1:T(8,128)(2,1)} %dynamic-slice_convert_fusion.5), channel_id=1, source_target_pairs={{0,24},{24,0},{8,16},{16,8},{1,25},{25,1},{9,17},{17,9},{2,26},{26... | collective-permute-start | bytes 737288 | tf_op jit(solution)/shard_map/ppermute | solution.py:173
  113.4 9.4 %slice-start = ((s8[7864320]{0:T(1024)(128)(4,1)}), s8[4194304]{0:T(1024)(128)(4,1)S(1)}, s32[]{:S(2)}) async-start(s8[7864320]{0:T(1024)(128)(4,1)} %bitcast.207), calls=%async_computation | async-start | bytes 8388608
  117.7 38.5 %collective-permute-start.31 = (bf16[2,120,640]{2,1,0:T(8,128)(2,1)}, bf16[2,120,640]{2,1,0:T(8,128)(2,1)}, u32[]{:S(2)}, u32[]{:S(2)}) collective-permute-start(bf16[2,120,640]{2,1,0:T(8,128)(2,1)} %fusion.16), channel_id=1, source_target_pairs={{0,1},{1,0},{2,3},{3,2},{4,5},{5,4},{6,7},{7,6},{8,9},{9,8},{10,11... | collective-permute-start | bytes 921608 | tf_op jit(solution)/shard_map/ppermute | solution.py:89
  129.5 6.9 %collective-permute-start.19 = (bf16[512,640]{0,1:T(8,128)(2,1)S(1)}, bf16[512,640]{0,1:T(8,128)(2,1)S(1)}, u32[]{:S(2)}, u32[]{:S(2)}) collective-permute-start(bf16[512,640]{0,1:T(8,128)(2,1)S(1)} %bitcast_convert_fusion), channel_id=1, source_target_pairs={{0,8},{8,0},{16,24},{24,16},{1,9},{9,1},{17,25},{25,17},{2,10},{10... | collective-permute-start | bytes 1966088 | tf_op jit(solution)/shard_map/ppermute | solution.py:170
  133.0 2.5 %collective-permute-start.22 = (bf16[256,240]{0,1:T(8,128)(2,1)S(1)}, bf16[256,240]{0,1:T(8,128)(2,1)S(1)}, u32[]{:S(2)}, u32[]{:S(2)}) collective-permute-start(bf16[256,240]{0,1:T(8,128)(2,1)S(1)} %constant_dynamic-slice_fusion.13), channel_id=1, source_target_pairs={{0,8},{8,0},{16,24},{24,16},{1,9},{9,1},{17,25},{25,17},{2,10},{10... | collective-permute-start | bytes 368648 | tf_op jit(solution)/shard_map/ppermute | solution.py:170
  141.2 4.4 %collective-permute-start.27 = (f32[2,240]{1,0:T(2,128)S(1)}, f32[2,240]{1,0:T(2,128)S(1)}, u32[]{:S(2)}, u32[]{:S(2)}) collective-permute-start(f32[2,240]{1,0:T(2,128)S(1)} %get-tuple-element.244), channel_id=1, source_target_pairs={{0,24},{24,0},{8,16},{16,8},{1,25},{25,1},{9,17},{17,9},{2,26},{26... | collective-permute-start | bytes 5768 | tf_op jit(solution)/shard_map/ppermute | solution.py:173
  141.3 5.6 %collective-permute-start.25 = (f32[2,240]{1,0:T(2,128)S(1)}, f32[2,240]{1,0:T(2,128)S(1)}, u32[]{:S(2)}, u32[]{:S(2)}) collective-permute-start(f32[2,240]{1,0:T(2,128)S(1)} %get-tuple-element.245), channel_id=1, source_target_pairs={{0,8},{8,0},{16,24},{24,16},{1,9},{9,1},{17,25},{25,17},{2,10},{10... | collective-permute-start | bytes 5768 | tf_op jit(solution)/shard_map/ppermute | solution.py:170
  141.8 5.4 %collective-permute-start.26 = (f32[2,240]{1,0:T(2,128)S(1)}, f32[2,240]{1,0:T(2,128)S(1)}, u32[]{:S(2)}, u32[]{:S(2)}) collective-permute-start(f32[2,240]{1,0:T(2,128)S(1)} %get-tuple-element.246), channel_id=1, source_target_pairs={{0,16},{16,0},{8,24},{24,8},{1,17},{17,1},{9,25},{25,9},{2,18},{18... | collective-permute-start | bytes 5768 | tf_op jit(solution)/shard_map/ppermute | solution.py:376
  145.6 19.4 %collective-permute-start.29 = (bf16[240,640]{1,0:T(8,128)(2,1)}, bf16[240,640]{1,0:T(8,128)(2,1)}, u32[]{:S(2)}, u32[]{:S(2)}) collective-permute-start(bf16[240,640]{1,0:T(8,128)(2,1)} %fusion.18), channel_id=1, source_target_pairs={{0,2},{1,3},{2,0},{3,1},{4,6},{5,7},{6,4},{7,5},{8,10},{9,11},{10,... | collective-permute-start | bytes 921608 | tf_op jit(solution)/shard_map/ppermute | solution.py:89
  146.9 14.1 %collective-permute-start.30 = (bf16[2,120,640]{2,1,0:T(8,128)(2,1)}, bf16[2,120,640]{2,1,0:T(8,128)(2,1)}, u32[]{:S(2)}, u32[]{:S(2)}) collective-permute-start(bf16[2,120,640]{2,1,0:T(8,128)(2,1)} %fusion.17), channel_id=1, source_target_pairs={{0,2},{1,3},{2,0},{3,1},{4,6},{5,7},{6,4},{7,5},{8,10},{9,11},{10,... | collective-permute-start | bytes 921608 | tf_op jit(solution)/shard_map/ppermute | solution.py:89
  152.7 8.3 %copy-start.13 = (f32[2,2,120,640]{3,2,0,1:T(8,128)S(1)}, f32[2,2,120,640]{3,2,0,1:T(8,128)}, u32[]{:S(2)}) copy-start(f32[2,2,120,640]{3,2,0,1:T(8,128)} %copy-done.12) | copy-start | bytes 3686404
  155.0 10.0 %copy-start.15 = (f32[2,240,640]{2,1,0:T(8,128)S(1)}, f32[2,240,640]{2,1,0:T(8,128)}, u32[]{:S(2)}) copy-start(f32[2,240,640]{2,1,0:T(8,128)} %copy-done.14) | copy-start | bytes 3686404
  155.1 17.3 %collective-permute-start.28 = (bf16[2,2,368,240]{2,3,1,0:T(8,128)(2,1)}, bf16[2,2,368,240]{2,3,1,0:T(8,128)(2,1)}, u32[]{:S(2)}, u32[]{:S(2)}) collective-permute-start(bf16[2,2,368,240]{2,3,1,0:T(8,128)(2,1)} %bitcast.167), channel_id=1, source_target_pairs={{0,1},{1,0},{2,3},{3,2},{4,5},{5,4},{6,7},{7,6},{8,9},{9,8},{10,11... | collective-permute-start | bytes 2119688 | tf_op jit(solution)/shard_map/ppermute | solution.py:89
  158.2 35.7 %collective-permute-start.37 = (bf16[120,640]{1,0:T(8,128)(2,1)}, bf16[120,640]{1,0:T(8,128)(2,1)}, u32[]{:S(2)}, u32[]{:S(2)}) collective-permute-start(bf16[120,640]{1,0:T(8,128)(2,1)} %fusion.36), channel_id=1, source_target_pairs={{0,4},{1,5},{2,6},{3,7},{4,0},{5,1},{6,2},{7,3},{8,12},{9,13},{10,... | collective-permute-start | bytes 460808 | tf_op jit(solution)/shard_map/ppermute | solution.py:89
  162.0 10.4 %copy-start.8 = (f32[2,2,1,368,240]{3,4,1,0,2:T(8,128)S(1)}, f32[2,2,1,368,240]{3,4,1,0,2:T(8,128)}, u32[]{:S(2)}) copy-start(f32[2,2,1,368,240]{3,4,1,0,2:T(8,128)} %copy.53) | copy-start | bytes 4239364
  162.7 33.0 %collective-permute-start.36 = (bf16[120,640]{1,0:T(8,128)(2,1)}, bf16[120,640]{1,0:T(8,128)(2,1)}, u32[]{:S(2)}, u32[]{:S(2)}) collective-permute-start(bf16[120,640]{1,0:T(8,128)(2,1)} %fusion.37), channel_id=1, source_target_pairs={{0,4},{1,5},{2,6},{3,7},{4,0},{5,1},{6,2},{7,3},{8,12},{9,13},{10,... | collective-permute-start | bytes 460808 | tf_op jit(solution)/shard_map/ppermute | solution.py:89
  166.3 8.7 %copy-start.10 = (f32[256,960]{0,1:T(8,128)S(1)}, f32[256,960]{0,1:T(8,128)}, u32[]{:S(2)}) copy-start(f32[256,960]{0,1:T(8,128)} %get-tuple-element.236) | copy-start | bytes 2949124
  166.3 8.9 %copy-start.20 = (f32[256,960]{0,1:T(8,128)S(1)}, f32[256,960]{0,1:T(8,128)}, u32[]{:S(2)}) copy-start(f32[256,960]{0,1:T(8,128)} %get-tuple-element.129) | copy-start | bytes 2949124
  166.3 8.9 %dynamic-slice-start = ((f32[256]{0:T(256)}, s32[]{:T(128)}), f32[128]{0:T(128)S(1)}, s32[]{:S(2)}) async-start(f32[256]{0:T(256)} %copy-done.87, s32[]{:T(128)} %select_n.679), calls=%async_computation.2 | async-start | bytes 1536 | tf_op jit(solution)/shard_map/dynamic-slice.10
  166.4 14.4 %collective-permute-start.34 = (bf16[240,320]{0,1:T(8,128)(2,1)S(1)}, bf16[240,320]{0,1:T(8,128)(2,1)S(1)}, u32[]{:S(2)}, u32[]{:S(2)}) collective-permute-start(bf16[240,320]{0,1:T(8,128)(2,1)S(1)} %fusion.31), channel_id=1, source_target_pairs={{0,4},{1,5},{2,6},{3,7},{4,0},{5,1},{6,2},{7,3},{8,12},{9,13},{10,... | collective-permute-start | bytes 460808 | tf_op jit(solution)/shard_map/ppermute | solution.py:89
  173.7 19.4 %collective-permute-start.33 = (bf16[2,368,240]{1,2,0:T(8,128)(2,1)S(1)}, bf16[2,368,240]{1,2,0:T(8,128)(2,1)S(1)}, u32[]{:S(2)}, u32[]{:S(2)}) collective-permute-start(bf16[2,368,240]{1,2,0:T(8,128)(2,1)S(1)} %fusion.12), channel_id=1, source_target_pairs={{0,2},{1,3},{2,0},{3,1},{4,6},{5,7},{6,4},{7,5},{8,10},{9,11},{10,... | collective-permute-start | bytes 1059848 | tf_op jit(solution)/shard_map/ppermute | solution.py:89
  176.2 17.7 %copy-start.29 = (f32[2,120,640]{2,1,0:T(8,128)S(1)}, f32[2,120,640]{2,1,0:T(8,128)}, u32[]{:S(2)}) copy-start(f32[2,120,640]{2,1,0:T(8,128)} %copy-done.28) | copy-start | bytes 1843204
  178.1 18.3 %copy-start.31 = (f32[2,120,640]{2,1,0:T(8,128)S(1)}, f32[2,120,640]{2,1,0:T(8,128)}, u32[]{:S(2)}) copy-start(f32[2,120,640]{2,1,0:T(8,128)} %copy-done.30) | copy-start | bytes 1843204
  180.8 13.1 %collective-permute-start.38 = (bf16[240,320]{0,1:T(8,128)(2,1)S(1)}, bf16[240,320]{0,1:T(8,128)(2,1)S(1)}, u32[]{:S(2)}, u32[]{:S(2)}) collective-permute-start(bf16[240,320]{0,1:T(8,128)(2,1)S(1)} %fusion.14), channel_id=1, source_target_pairs={{0,0},{8,2},{16,4},{24,6},{1,8},{9,10},{17,12},{25,14},{2,16},{10,... | collective-permute-start | bytes 460808 | tf_op jit(solution)/shard_map/ppermute | solution.py:422
  193.2 10.0 %collective-permute-start.35 = (bf16[368,240]{0,1:T(8,128)(2,1)S(1)}, bf16[368,240]{0,1:T(8,128)(2,1)S(1)}, u32[]{:S(2)}, u32[]{:S(2)}) collective-permute-start(bf16[368,240]{0,1:T(8,128)(2,1)S(1)} %fusion.30), channel_id=1, source_target_pairs={{0,4},{1,5},{2,6},{3,7},{4,0},{5,1},{6,2},{7,3},{8,12},{9,13},{10,... | collective-permute-start | bytes 529928 | tf_op jit(solution)/shard_map/ppermute | solution.py:89
  193.9 12.3 %copy-start.1 = (bf16[960,640]{1,0:T(8,128)(2,1)S(1)}, bf16[960,640]{1,0:T(8,128)(2,1)}, u32[]{:S(2)}) copy-start(bf16[960,640]{1,0:T(8,128)(2,1)} %param.18) | copy-start | bytes 3686404
  (71 other events, 142.2 us)
where the time goes:
time: 209 us; the launch traced here: 206 us
  waiting for transfers between devices  64.4 us (31%)
  other arithmetic  45.5 us (22%)
  matrix products  33 us (16%)
  local copies, waits for them, and re-layouts  31 us (15%)
  starting transfers between devices  30.2 us (14%)
  between operations  2.21 us (1%)
    ppermute x8, waiting for transfers between devices, chip_cross(): return lax.ppermute(values, 'grp', CROSS_SWAP)  26.8 us
    ppermute x12, waiting for transfers between devices, swap_over_rep(): came = lax.ppermute(away, 'rep', [(i, i ^ 1 << bit) for i in range(count)])  22.8 us
    add x11, other arithmetic, joined(): return pair[0] + pair[1].astype(jnp.float32)  13 us
    ppermute x1, waiting for transfers between devices, per_device(): down_across = lax.ppermute(turn.hold(down_2), 'grp', CHIP_SWAP)  12.6 us
    ppermute x12, starting transfers between devices, swap_over_rep(): came = lax.ppermute(away, 'rep', [(i, i ^ 1 << bit) for i in range(count)])  11.9 us
    unnamed x195, local copies, waits for them, and re-layouts  11.6 us
    select_n x8, other arithmetic, in_order(): jnp.where(me == device, own, jnp.where(me == device ^ 1, beside, jnp.wher...  9.62 us
    dot_general x7, matrix products, dot_nn(): return jnp.dot(left, right, preferred_element_type=jnp.float32)  8.53 us
  transfers between devices with their start and end apart: 39, of which 12 were waited for; matrix products, arithmetic and copies ran while one was open for 45% of the time, Pallas kernels for 0%

commit v1 on v0

v1 whole, which is shorter than its diff:
```python
import math

import jax
import jax.numpy as jnp
import numpy as np
from jax import lax
from jax.experimental.layout import Layout, with_layout_constraint
from jax.experimental import pallas as pl
from jax.experimental.pallas import tpu as pltpu
from jax.sharding import PartitionSpec as P

HEAD_SIZE = 64
QUERY_HEADS = 15
KEY_VALUE_HEADS = 5
GROUP_QUERIES = QUERY_HEADS // KEY_VALUE_HEADS
EPS = 1e-05
THETA = 10000.0

BLOCK_ORDER = (0, 3, 1, 2)

CORE_SWAP = [(0, 1), (1, 0), (2, 3), (3, 2)]
CHIP_SWAP = [(0, 2), (2, 0), (1, 3), (3, 1)]
CROSS_SWAP = [(0, 3), (3, 0), (1, 2), (2, 1)]


def norm_scale(values):
    return lax.rsqrt(jnp.mean(values * values, axis=-1, keepdims=True) + EPS)


def rope_tables(positions):
    half = HEAD_SIZE // 2
    freq = jnp.exp(
        jnp.arange(half, dtype=jnp.int32).astype(jnp.float32) * (-2.0 * math.log(THETA) / HEAD_SIZE)
    )
    angle = freq[:, None] * positions.astype(jnp.float32)[None, :]
    return jnp.cos(angle), jnp.sin(angle)


def dot_nn(left, right):
    return jnp.dot(left, right, preferred_element_type=jnp.float32)


def dot_nt(left, right):
    return lax.dot_general(
        left, right, (((1,), (1,)), ((), ())), preferred_element_type=jnp.float32
    )


def dot_tn(left, right):
    return lax.dot_general(
        left, right, (((0,), (0,)), ((), ())), preferred_element_type=jnp.float32
    )


def dot_any(left, right, left_dim, right_dim):
    return lax.dot_general(
        left, right, (((left_dim,), (right_dim,)), ((), ())), preferred_element_type=jnp.float32
    )


def turned(values, cosine, sine):
    half = HEAD_SIZE // 2
    out = []
    for head in range(values.shape[0] // HEAD_SIZE):
        first = values[head * HEAD_SIZE : head * HEAD_SIZE + half]
        second = values[head * HEAD_SIZE + half : (head + 1) * HEAD_SIZE]
        out.append(first * cosine - second * sine)
        out.append(second * cosine + first * sine)
    return jnp.concatenate(out, axis=0)


def by_position(values):
    block = values.shape[1] // 4
    place = [BLOCK_ORDER.index(i) for i in range(4)]
    return jnp.concatenate([values[:, p * block : (p + 1) * block] for p in place], axis=1)


def by_block(values):
    block = values.shape[1] // 4
    return jnp.concatenate([values[:, p * block : (p + 1) * block] for p in BLOCK_ORDER], axis=1)


def queries_of(ref, group, part, block):
    start = group * GROUP_QUERIES * HEAD_SIZE
    heads = [
        ref[start + i * HEAD_SIZE : start + (i + 1) * HEAD_SIZE, part * block : (part + 1) * block]
        for i in range(GROUP_QUERIES)
    ]
    return jnp.concatenate(heads, axis=1)


def scores_of(keys, queries, block_index, block):
    scores = dot_any(keys, queries, 0, 0) * (1.0 / math.sqrt(HEAD_SIZE))
    key_place = lax.broadcasted_iota(jnp.int32, scores.shape, 0)
    lane = lax.broadcasted_iota(jnp.int32, scores.shape, 1)
    query_place = block_index * block + lax.rem(lane, block)
    return jnp.where(key_place <= query_place, scores, -1e30)


def front_kernel(
    me_ref, x_ref, own_ref, beside_ref, cross_ref, corner_ref, cos_ref, sin_ref,
    a1_ref, w_ref, gain_ref, q_ref, k_ref, v_ref, o_ref, lse_ref,
):
    me = me_ref[0]
    second = me_ref[1]
    width = x_ref.shape[0]
    block = x_ref.shape[1] // 4
    kv_width = k_ref.shape[0]
    q_rows = width // 4
    kv_rows = kv_width // 4
    for ref, k in ((own_ref, 0), (beside_ref, 1), (cross_ref, 3), (corner_ref, 2)):
        device = me ^ k
        w_ref[pl.ds(pl.multiple_of(device * q_rows, 16), q_rows), :] = ref[0:q_rows, :]
        for i in range(2):
            start = width + i * kv_width + device * kv_rows
            first = q_rows + i * kv_rows
            w_ref[pl.ds(pl.multiple_of(start, 16), kv_rows), :] = ref[first : first + kv_rows, :]
        gain_row = q_rows + 2 * kv_rows
        part_gains = ref[gain_row : gain_row + 8, 0:256].astype(jnp.float32).T
        gain_ref[pl.ds(pl.multiple_of(device * q_rows, 8), q_rows), :] = part_gains[0:q_rows, :]
    x = x_ref[...].astype(jnp.float32)
    scale = lax.rsqrt(jnp.mean(x * x, axis=0, keepdims=True) + EPS)
    a1_ref[...] = ((x * scale) * gain_ref[:, 0:1]).astype(jnp.bfloat16)
    start = pl.multiple_of(second * (2 * block), 2 * block)
    a1_own = a1_ref[:, pl.ds(start, 2 * block)]
    a1 = a1_ref[...]
    cos_own = cos_ref[:, pl.ds(start, 2 * block)]
    sin_own = sin_ref[:, pl.ds(start, 2 * block)]
    for group in range(KEY_VALUE_HEADS):
        q_start = group * GROUP_QUERIES * HEAD_SIZE
        q_stop = q_start + GROUP_QUERIES * HEAD_SIZE
        kv_start = group * HEAD_SIZE
        kv_stop = kv_start + HEAD_SIZE
        keys = dot_any(w_ref[width + kv_start : width + kv_stop, :], a1, 1, 0)
        keys = by_position(turned(keys, cos_ref[...], sin_ref[...])).astype(jnp.bfloat16)
        values = dot_any(w_ref[width + kv_width + kv_start : width + kv_width + kv_stop, :], a1, 1, 0)
        values = by_position(values).astype(jnp.bfloat16)
        k_ref[kv_start:kv_stop, :] = keys
        v_ref[kv_start:kv_stop, :] = values
        queries = dot_any(w_ref[q_start:q_stop, :], a1_own, 1, 0)
        q_ref[q_start:q_stop, :] = turned(queries, cos_own, sin_own).astype(jnp.bfloat16)
        for part in range(2):
            block_index = second if part == 0 else 3 - second
            used = 2 * block * (part + 1)
            scores = scores_of(keys[:, :used], queries_of(q_ref, group, part, block), block_index, block)
            peak = jnp.max(scores, axis=0, keepdims=True)
            probs = jnp.exp(scores - peak)
            total = jnp.sum(probs, axis=0, keepdims=True)
            mixed = dot_any(values[:, :used], probs.astype(jnp.bfloat16), 1, 0) / total
            logsum = peak + jnp.log(total)
            for i in range(GROUP_QUERIES):
                head = group * GROUP_QUERIES + i
                lanes = slice(i * block, (i + 1) * block)
                places = slice(part * block, (part + 1) * block)
                o_ref[head * HEAD_SIZE : (head + 1) * HEAD_SIZE, places] = mixed[:, lanes].astype(jnp.bfloat16)
                lse_ref[head : head + 1, places] = logsum[:, lanes]


def back_kernel(
    me_ref, do_ref, o_ref, q_ref, k_ref, v_ref, lse_ref, cos_ref, sin_ref, dq_ref, dkv_ref, sent_ref
):
    second = me_ref[1]
    block = q_ref.shape[1] // 2
    kv_width = k_ref.shape[0]
    start = pl.multiple_of(second * (2 * block), 2 * block)
    cos_own = cos_ref[:, pl.ds(start, 2 * block)]
    sin_own = sin_ref[:, pl.ds(start, 2 * block)]
    scale = 1.0 / math.sqrt(HEAD_SIZE)
    for group in range(KEY_VALUE_HEADS):
        kv_start = group * HEAD_SIZE
        kv_stop = kv_start + HEAD_SIZE
        d_keys = d_values = None
        for part in (1, 0):
            block_index = second if part == 0 else 3 - second
            used = 2 * block * (part + 1)
            keys = k_ref[kv_start:kv_stop, :used]
            values = v_ref[kv_start:kv_stop, :used]
            queries = queries_of(q_ref, group, part, block)
            grads = queries_of(do_ref, group, part, block)
            outs = queries_of(o_ref, group, part, block)
            heads = range(group * GROUP_QUERIES, (group + 1) * GROUP_QUERIES)
            logsum = jnp.concatenate(
                [lse_ref[h : h + 1, part * block : (part + 1) * block] for h in heads], axis=1
            )
            probs = jnp.exp(scores_of(keys, queries, block_index, block) - logsum)
            delta = jnp.sum(grads.astype(jnp.float32) * outs.astype(jnp.float32), axis=0, keepdims=True)
            d_probs = dot_any(values, grads, 0, 0)
            d_scores = (probs * (d_probs - delta) * scale).astype(jnp.bfloat16)
            d_queries = dot_any(keys, d_scores, 1, 0)
            for i, h in enumerate(heads):
                places = slice(part * block, (part + 1) * block)
                back = turned(d_queries[:, i * block : (i + 1) * block], cos_own[:, places], -sin_own[:, places])
                dq_ref[h * HEAD_SIZE : (h + 1) * HEAD_SIZE, places] = back.astype(jnp.bfloat16)
            more_keys = dot_any(queries, d_scores, 1, 1)
            more_values = dot_any(grads, probs.astype(jnp.bfloat16), 1, 1)
            if part == 1:
                d_keys, d_values = more_keys, more_values
            else:
                d_keys = jnp.concatenate([d_keys[:, :used] + more_keys, d_keys[:, used:]], axis=1)
                d_values = jnp.concatenate([d_values[:, :used] + more_values, d_values[:, used:]], axis=1)
        d_keys = turned(by_block(d_keys), cos_ref[...], -sin_ref[...])
        d_values = by_block(d_values)
        dkv_ref[kv_start:kv_stop, :] = d_keys
        dkv_ref[kv_width + kv_start : kv_width + kv_stop, :] = d_values
        sent_ref[kv_start:kv_stop, :] = d_keys.astype(jnp.bfloat16)
        sent_ref[kv_width + kv_start : kv_width + kv_stop, :] = d_values.astype(jnp.bfloat16)


def whole(kernel, outs, *args):
    vmem = pl.BlockSpec(memory_space=pltpu.VMEM)
    return pl.pallas_call(
        kernel,
        out_shape=outs,
        in_specs=[pl.BlockSpec(memory_space=pltpu.SMEM)] + [vmem] * (len(args) - 1),
        out_specs=[vmem] * len(outs),
        compiler_params=pltpu.CompilerParams(vmem_limit_bytes=40 * 1024 * 1024),
        cost_estimate=pl.CostEstimate(flops=1000000, transcendentals=0, bytes_accessed=1000000),
    )(*args)


class Order:
    def __init__(self):
        self.token = None

    def mark(self, value):
        self.token = value

    def hold(self, *values):
        if self.token is None:
            return values if len(values) > 1 else values[0]
        held = lax.optimization_barrier(values + (self.token,))[:-1]
        return held if len(held) > 1 else held[0]


def rep_bits():
    count = lax.axis_size("rep")
    bits = count.bit_length() - 1
    assert 1 << bits == count and bits >= 3
    return bits


def row_major(values):
    return with_layout_constraint(values, Layout(major_to_minor=tuple(range(values.ndim))))


def swap_over_rep(held, bit, axis):
    count = lax.axis_size("rep")
    mine = (lax.axis_index("rep") >> bit) & 1
    away = lax.dynamic_index_in_dim(held, 1 - mine, axis, keepdims=False).astype(jnp.bfloat16)
    came = lax.ppermute(away, "rep", [(i, i ^ (1 << bit)) for i in range(count)])
    return lax.dynamic_index_in_dim(held, mine, axis, keepdims=False), came, away


def joined(pair):
    return pair[0] + pair[1].astype(jnp.float32)


def halve_lanes_over_rep(held, bit):
    count = lax.axis_size("rep")
    upper = ((lax.axis_index("rep") >> bit) & 1) == 1
    half = held.shape[1] // 2
    away = jnp.where(upper, held[:, :half], held[:, half:]).astype(jnp.bfloat16)
    came = lax.ppermute(away, "rep", [(i, i ^ (1 << bit)) for i in range(count)])
    return jnp.where(upper, held[:, half:], held[:, :half]), came, away


class RepSum:
    def __init__(self, partial, order):
        bits = rep_bits()
        self.bits_to_go = list(order) + list(range(len(order), bits))
        self.left = list(range(bits))
        self.held = partial.reshape((2,) * bits + partial.shape[1:])
        self.step()

    def step(self):
        bit = self.bits_to_go.pop(0)
        axis = len(self.left) - 1 - self.left.index(bit)
        self.left.remove(bit)
        self.kept, self.came, self.sent = swap_over_rep(self.held, bit, axis)

    def next(self, order):
        self.held = joined((self.kept, order.hold(self.came)))
        self.step()
        order.mark(self.sent)

    def end(self, order):
        while self.bits_to_go:
            self.next(order)
        return joined((self.kept, order.hold(self.came)))


def by_rep(partial):
    count = lax.axis_size("rep")
    return partial.reshape((count, partial.shape[0] // count) + partial.shape[1:])


def per_device(
    block_input,
    cotangent,
    norm_gains,
    w_query,
    key_weight,
    value_weight,
    w_out,
    w_gate,
    w_up,
    w_down,
):
    bf16 = jnp.bfloat16
    me = lax.axis_index("grp")
    rows = block_input.shape[1]
    width = block_input.shape[2]
    half_rows = 2 * rows
    kv_width = KEY_VALUE_HEADS * HEAD_SIZE
    slice_width = w_query.shape[1]
    kv_slice = key_weight.shape[1]
    hidden_slice = w_gate.shape[1]
    scale = 1.0 / math.sqrt(HEAD_SIZE)
    second_set = (me == 1) | (me == 2)
    own_start = second_set.astype(jnp.int32) * half_rows
    beside_start = half_rows - own_start
    own_block_start = jnp.where(me < 2, 0, rows)

    def own_half(values):
        return lax.dynamic_slice_in_dim(values, own_start, half_rows, 0)

    def own_block(values):
        return lax.dynamic_slice_in_dim(values, own_block_start, rows, 0)

    def own_cols(values):
        return lax.dynamic_slice_in_dim(values, me * (values.shape[1] // 4), values.shape[1] // 4, 1)

    def in_pair(own, cross):
        return jnp.concatenate([jnp.where(me < 2, own, cross), jnp.where(me < 2, cross, own)], axis=0)

    def sets(own, beside):
        return jnp.where(second_set, beside, own), jnp.where(second_set, own, beside)

    def core_swap(values):
        return lax.ppermute(values, "grp", CORE_SWAP)

    def chip_cross(values):
        return lax.ppermute(values, "grp", CROSS_SWAP)

    def two_halves(own, beside):
        return jnp.concatenate(sets(own, beside), axis=0)

    def in_order(own, beside, cross, corner, order=(0, 1, 2, 3)):
        out = []
        for device in order:
            out.append(
                jnp.where(
                    me == device,
                    own,
                    jnp.where(me == device ^ 1, beside, jnp.where(me == device ^ 3, cross, corner)),
                )
            )
        return jnp.concatenate(out, axis=0)

    turn = Order()

    x_here = block_input[0]
    x_cross = chip_cross(x_here)
    qkv_sent = row_major(
        jnp.concatenate(
            [
                w_query.T,
                key_weight.T,
                value_weight.T,
                jnp.pad(norm_gains, ((0, 6), (0, width - slice_width))),
            ],
            axis=0,
        )
    )
    qkv_cross = chip_cross(qkv_sent)
    turn.mark(qkv_sent)
    qkv_beside = core_swap(turn.hold(qkv_sent))
    x_pair = in_pair(x_here, turn.hold(x_cross))
    x_all = two_halves(x_pair, core_swap(x_pair))
    turn.mark(x_pair)
    places = np.concatenate([np.arange(b * rows, (b + 1) * rows, dtype=np.int32) for b in BLOCK_ORDER])
    cosine, sine = rope_tables(turn.hold(jnp.asarray(places)))
    wo_sent = turn.hold(w_out).T
    dy_here, down_t = turn.hold(cotangent, w_down)
    dy_here = dy_here[0]
    down_t = down_t.T
    wo_beside = core_swap(wo_sent)
    dy_beside = core_swap(dy_here)

    def down_piece(k):
        return lax.dynamic_slice_in_dim(down_t, (me ^ k) * hidden_slice, hidden_slice, 1)

    down_own, down_near = down_piece(0), down_piece(1)
    down_far = jnp.concatenate([down_piece(3), down_piece(2)], axis=0)
    cosine, sine, wo_sent, down_own, down_near, down_far, x_all, dy_here = lax.optimization_barrier(
        (cosine, sine, wo_sent, down_own, down_near, down_far, x_all, dy_here)
    )
    turn.mark(down_far)
    qkv_cross = row_major(turn.hold(qkv_cross))
    qkv_corner = row_major(core_swap(qkv_cross))
    turn.mark(qkv_cross)
    wo_cross = chip_cross(turn.hold(wo_sent))
    dy_cross = chip_cross(turn.hold(dy_here))
    place = jnp.stack([me, second_set.astype(jnp.int32)])

    def shaped(*shape, kind=bf16):
        return jax.ShapeDtypeStruct(shape, kind)

    a1_t, weights, gains, q_t, k_t, v_t, o_t, logsum = whole(
        front_kernel,
        [
            shaped(width, 4 * rows),
            shaped(width + 2 * kv_width, width),
            shaped(width, 8, kind=jnp.float32),
            shaped(width, half_rows),
            shaped(kv_width, 4 * rows),
            shaped(kv_width, 4 * rows),
            shaped(width, half_rows),
            shaped(QUERY_HEADS + 1, half_rows, kind=jnp.float32),
        ],
        place, x_all.T, qkv_sent, qkv_beside, qkv_cross, qkv_corner, cosine, sine,
    )
    gain_attn = gains[:, 0]
    gain_ffn = gains[:, 1]
    xf = x_pair.astype(jnp.float32)
    turn.mark(o_t)
    down_cross = chip_cross(turn.hold(down_far))

    wo_cross, dy_cross = turn.hold(wo_cross, dy_cross)
    wo_t = in_order(wo_sent, wo_beside, wo_cross, core_swap(wo_cross))
    x2 = xf + dot_any(o_t, wo_t, 0, 1)
    r2 = norm_scale(x2)
    n2 = x2 * r2
    a2_own = (n2 * gain_ffn).astype(bf16)
    a2_beside = core_swap(a2_own)
    turn.mark(a2_own)
    down_cross = turn.hold(down_cross)
    down_core = core_swap(jnp.concatenate([down_near, down_cross[slice_width:]], axis=0))
    dy_all = in_order(dy_here, dy_beside, dy_cross, core_swap(dy_cross), BLOCK_ORDER)
    a2 = two_halves(a2_own, a2_beside)

    gate = dot_nn(a2, w_gate)
    up = dot_nn(a2, w_up)
    gate, up, dy_all = lax.optimization_barrier((gate, up, dy_all))
    turn.mark(up)
    o_beside = core_swap(turn.hold(o_t))
    sig = jax.nn.sigmoid(gate)
    act = gate * sig
    hidden = (act * up).astype(bf16)
    down_core = turn.hold(down_core)
    down_rows_t = in_order(
        down_own, down_core[:slice_width], down_cross[:slice_width], down_core[slice_width:]
    )
    d_hidden = dot_nn(dy_all, down_rows_t)
    d_gate = (d_hidden * up * sig * (1.0 + gate * (1.0 - sig))).astype(bf16)
    d_up = (d_hidden * act).astype(bf16)
    d_a2_part = (dot_nt(d_gate, w_gate) + dot_nt(d_up, w_up)).astype(bf16)

    beside_part = core_swap(lax.dynamic_slice_in_dim(d_a2_part, beside_start, half_rows, 0))
    chip_sum = own_half(d_a2_part).astype(jnp.float32) + beside_part.astype(jnp.float32)
    chip_sent = chip_sum.astype(bf16)
    other_chip = chip_cross(chip_sent)
    turn.mark(chip_sent)
    a2_late, d_gate, d_up, hidden = turn.hold(a2, d_gate, d_up, hidden)
    gate_sum = RepSum(by_rep(dot_tn(a2_late, d_gate)), (0, 1))
    turn.mark(gate_sum.sent)
    up_sum = RepSum(by_rep(dot_tn(turn.hold(a2_late), d_up)), (1, 0))
    turn.mark(up_sum.sent)
    g_down = dot_tn(turn.hold(dy_all), hidden).reshape(2, 2, slice_width, hidden_slice)
    down_pair = swap_over_rep(g_down, 0, 1)
    turn.mark(down_pair[2])

    out_part = dot_nt(turn.hold(hidden), down_rows_t).astype(bf16)
    out_beside = core_swap(lax.dynamic_slice_in_dim(out_part, beside_start, half_rows, 0))
    out_chip = own_half(out_part).astype(jnp.float32) + out_beside.astype(jnp.float32)
    out_away = lax.dynamic_slice_in_dim(out_chip, rows - own_block_start, rows, 0).astype(bf16)
    turn.mark(out_away)

    other_chip = turn.hold(other_chip)
    d_a2 = chip_sum + other_chip.astype(jnp.float32)
    dyf = own_half(dy_all).astype(jnp.float32)
    d_n2 = d_a2 * gain_ffn
    d_x2 = dyf + r2 * (d_n2 - n2 * jnp.mean(d_n2 * n2, axis=-1, keepdims=True))
    d_x2_low = d_x2.astype(bf16)

    def columns_of(own):
        away = lax.dynamic_slice_in_dim(own, (me ^ 1) * slice_width, slice_width, 1)
        return two_halves(own_cols(own), core_swap(away))

    d_o = row_major(dot_any(wo_t, d_x2_low, 0, 1).astype(bf16))
    turn.mark(d_o)
    out_cross = chip_cross(turn.hold(out_away))
    d_o = turn.hold(d_o)
    d_q, d_kv, d_kv_sent = whole(
        back_kernel,
        [
            shaped(width, half_rows),
            shaped(2 * kv_width, 4 * rows, kind=jnp.float32),
            shaped(2 * kv_width, 4 * rows),
        ],
        place, d_o, o_t, q_t, k_t, v_t, logsum, cosine, sine,
    )
    d_kv_beside = core_swap(d_kv_sent)
    d_q_away = lax.dynamic_slice_in_dim(d_q, (me ^ 1) * slice_width, slice_width, 0)
    d_q_kept = lax.dynamic_slice_in_dim(d_q, me * slice_width, slice_width, 0)
    d_q_halves = sets(d_q_kept, core_swap(d_q_away))
    turn.mark(d_q_away)
    gate_sum.next(turn)
    d_kv, d_kv_beside = turn.hold(d_kv, d_kv_beside)
    d_kv = (d_kv + d_kv_beside.astype(jnp.float32)).astype(bf16)

    def block_lanes(values):
        return jnp.where(me < 2, values[:, :rows], values[:, rows:])

    d_kv_half = jnp.where(second_set, d_kv[:, half_rows:], d_kv[:, :half_rows])
    d_block = lax.optimization_barrier(
        jnp.concatenate([block_lanes(d_q), block_lanes(d_kv_half)], axis=0)
    )
    d_a1 = dot_any(d_block, weights, 0, 0)
    x_block = x_here.astype(jnp.float32)
    r1_block = norm_scale(x_block)
    n1_block = x_block * r1_block
    g_attn = jnp.sum(d_a1 * n1_block, axis=0)
    g_ffn = jnp.sum(own_block(d_a2 * n2), axis=0)
    g_gains = jnp.stack([g_attn, g_ffn]).reshape(2, 4, slice_width).transpose(1, 0, 2)

    def gain_piece(k):
        return lax.dynamic_index_in_dim(g_gains, me ^ k, 0, keepdims=False)

    gains_came = (
        core_swap(gain_piece(1)),
        lax.ppermute(gain_piece(2), "grp", CHIP_SWAP),
        chip_cross(gain_piece(3)),
    )
    turn.mark(g_gains)

    kv_mine = [
        lax.dynamic_slice_in_dim(d_kv, i * kv_width + me * kv_slice, kv_slice, 0) for i in range(2)
    ]
    g_q = by_rep(dot_any(turn.hold(a1_t), jnp.concatenate(d_q_halves, axis=1), 1, 1))
    g_kv = by_rep(dot_any(turn.hold(a1_t), jnp.concatenate(kv_mine, axis=0), 1, 1))
    o_all = jnp.concatenate(sets(o_t, o_beside), axis=1)
    g_out = by_rep(dot_nn(turn.hold(o_all), columns_of(d_x2_low)))
    turn.mark(g_out)
    gains_came = turn.hold(*gains_came)
    g_gains = gain_piece(0) + gains_came[0] + gains_came[1] + gains_came[2]
    count = g_q.shape[0]
    share = g_q.shape[1]
    riders = jnp.broadcast_to(jnp.pad(g_gains, ((0, 6), (0, 0))), (count, 8, slice_width))

    def full_lanes(values):
        return jnp.pad(values, ((0, 0), (0, 0), (0, -values.shape[2] % 128)))

    bundle = jnp.concatenate([full_lanes(part) for part in (g_q, g_out, g_kv, riders)], axis=1)
    attn_sum = RepSum(row_major(bundle), (0, 1))
    turn.mark(attn_sum.sent)

    down_held = joined((down_pair[0], turn.hold(down_pair[1])))
    down_pair = swap_over_rep(down_held, 1, 0)
    turn.mark(down_pair[2])
    up_sum.next(turn)
    gate_sum.next(turn)

    d_a1_late, d_x2_late = turn.hold(d_a1, d_x2)
    d_n1 = d_a1_late * gain_attn
    input_grad = own_block(d_x2_late) + r1_block * (
        d_n1 - n1_block * jnp.mean(d_n1 * n1_block, axis=-1, keepdims=True)
    )
    block_output = own_block(x2) + own_block(out_chip) + turn.hold(out_cross).astype(jnp.float32)
    input_grad, block_output = lax.optimization_barrier((input_grad, block_output))
    turn.mark(block_output)

    attn_sum.next(turn)
    down_held = joined((down_pair[0], turn.hold(down_pair[1])))
    parts = count // 4
    down_pair = halve_lanes_over_rep(down_held, rep_bits() - 1)
    turn.mark(down_pair[2])
    up_sum.next(turn)
    attn_sum.next(turn)
    down_held = joined((down_pair[0], turn.hold(down_pair[1])))
    for bit in reversed(range(2, rep_bits() - 1)):
        down_held = joined(halve_lanes_over_rep(down_held, bit))
    homes = [
        (j * count + r, (r & 3) * count + j * parts + (r >> 2)) for r in range(count) for j in range(4)
    ]
    down_sent = down_held.astype(bf16)
    g_down = lax.ppermute(down_sent, ("grp", "rep"), homes)
    turn.mark(down_sent)
    g_gate = gate_sum.end(turn)
    g_up = up_sum.end(turn)
    g_down = turn.hold(g_down).astype(jnp.float32).T
    g_gate, g_up, g_down = lax.optimization_barrier((g_gate, g_up, g_down))
    turn.mark(g_down)
    g_attn_w = row_major(attn_sum.end(turn))
    g_kv = g_attn_w[2 * share : 3 * share]
    return (
        block_output[None],
        input_grad[None],
        g_attn_w[3 * share : 3 * share + 2, :slice_width],
        g_attn_w[:share, :slice_width],
        g_kv[:, :kv_slice],
        g_kv[:, kv_slice : 2 * kv_slice],
        g_attn_w[share : 2 * share, :slice_width],
        g_gate,
        g_up,
        g_down,
    )


def solution(mesh):
    rows = P("rep", "grp", None)
    weight = P(None, "grp")
    grad = P("rep", "grp")
    return jax.shard_map(
        per_device,
        mesh=mesh,
        in_specs=(rows, rows) + (weight,) * 8,
        out_specs=(rows, rows, weight) + (grad,) * 7,
        check_vma=False,
    )
```

time: 209 us -> 193 us (0.923)
  other arithmetic: 45.5 us -> 27.3 us
  matrix products: 33 us -> 17.1 us
  Pallas kernels: 0 us -> 14.8 us
  waiting for transfers between devices: 64.4 us -> 69.1 us
    ppermute x1, waiting for transfers between devices: 0.64 us -> 16.2 us  [per_device(): g_down = lax.ppermute(down_sent, ('grp', 'rep'), homes)]
    pallas_call x0 -> x2, Pallas kernels: none -> 14.8 us  [whole(): pl.pallas_call(kernel, out_shape=outs, in_specs=[pl.BlockSpec(memory_spac...]
    ppermute x1, waiting for transfers between devices: 12.6 us -> 0.01 us  [halve_lanes_over_rep(): came = lax.ppermute(away, 'rep', [(i, i ^ 1 << bit) for i in range(count)])]
    dot_general x6 -> x5, matrix products: 14 us -> 5.2 us  [dot_any(): lax.dot_general(left, right, (((left_dim,), (right_dim,)), ((), ())), pre...]
    add x11, other arithmetic: 13 us -> 5.54 us  [joined(): return pair[0] + pair[1].astype(jnp.float32)]
    unnamed x195 -> x154, local copies, waits for them, and re-layouts: 11.6 us -> 18.4 us
    select_n x8 -> x3, other arithmetic: 9.62 us -> 3.17 us  [in_order(): jnp.where(me == device, own, jnp.where(me == device ^ 1, beside, jnp.wher...]
    ppermute x8, waiting for transfers between devices: 26.8 us -> 31.3 us  [chip_cross(): return lax.ppermute(values, 'grp', CROSS_SWAP)]
  transfers between devices with their start and end apart: 39 -> 38, of which waited for: 12 -> 12; matrix products, arithmetic and copies ran while one was open for 45% -> 28% of each run, Pallas kernels for 0% -> 8%
where the time goes in v1:
time: 193 us; the launch traced here: 192 us
  waiting for transfers between devices  69.1 us (36%)
  local copies, waits for them, and re-layouts  32.4 us (17%)
  starting transfers between devices  29.6 us (15%)
  other arithmetic  27.3 us (14%)
  matrix products  17.1 us (9%)
  Pallas kernels  14.8 us (8%)
    ppermute x8, waiting for transfers between devices, chip_cross(): return lax.ppermute(values, 'grp', CROSS_SWAP)  31.3 us
    ppermute x11, waiting for transfers between devices, swap_over_rep(): came = lax.ppermute(away, 'rep', [(i, i ^ 1 << bit) for i in range(count)])  21.1 us
    unnamed x154, local copies, waits for them, and re-layouts  18.4 us
    ppermute x1, waiting for transfers between devices, per_device(): g_down = lax.ppermute(down_sent, ('grp', 'rep'), homes)  16.2 us
    pallas_call x2, Pallas kernels, whole(): pl.pallas_call(kernel, out_shape=outs, in_specs=[pl.BlockSpec(memory_spac...  14.8 us
    ppermute x8, starting transfers between devices, chip_cross(): return lax.ppermute(values, 'grp', CROSS_SWAP)  10.4 us
    ppermute x11, starting transfers between devices, swap_over_rep(): came = lax.ppermute(away, 'rep', [(i, i ^ 1 << bit) for i in range(count)])  10 us
    add x11, other arithmetic, joined(): return pair[0] + pair[1].astype(jnp.float32)  5.54 us
  transfers between devices with their start and end apart: 38, of which 12 were waited for; matrix products, arithmetic and copies ran while one was open for 28% of the time, Pallas kernels for 8%

profile of v1, /device:TPU:5, one launch (start us, length us, event | category | flops | bytes accessed | tf_op | source)
XLA Modules:
  0.0 192.0 jit_solution(7069011674263909818)
XLA Ops:
  0.7 1.8 collective-permute-start
  2.5 1.2 copy.43
  3.7 1.1 fusion.5.own_ref
  5.6 4.1 %collective-permute-done = bf16[128,960]{0,1:T(8,128)(2,1)S(1)} collective-permute-done((bf16[128,960]{0,1:T(8,128)(2,1)}, bf16[128,960]{0,1:T(8,128)(2,1)S(1)}, u32[]{:S(2)}, u32[]{:S(2)}) %collective-permute-start) | collective-permute-done | bytes 245792 | tf_op jit(solution)/shard_map/ppermute | solution.py:343
  10.0 2.2 %dynamic-slice_bitcast_fusion.1 = (bf16[240,640]{1,0:T(8,128)(2,1)S(1)}, bf16[240,640]{1,0:T(8,128)(2,1)S(1)}, bf16[240,640]{1,0:T(8,128)(2,1)}, bf16[240,640]{1,0:T(8,128)(2,1)}) fusion(bf16[2560,240]{0,1:T(8,128)(2,1)} %param.20, s32[]{:T(128)S(6)} %select_n.383, s32[]{:T(128)S(6)} %select_n.384, s32[]{:T(128)S(6)} %select_n.382, s32[]{:T(128)S(6)} %select_n.381), kind=kLoop, calls=%fused_computation.109 | loop fusion | bytes 2457616 | tf_op jit(solution)/shard_map/dynamic_slice | solution.py:391
  13.8 13.7 %collective-permute-done.3.cross_ref = bf16[408,960]{1,0:T(8,128)(2,1)} collective-permute-done((bf16[408,960]{1,0:T(8,128)(2,1)S(1)}, bf16[408,960]{1,0:T(8,128)(2,1)}, u32[]{:S(2)}, u32[]{:S(2)}) %collective-permute-start.3) | collective-permute-done | bytes 783392 | tf_op jit(solution)/shard_map/ppermute | solution.py:343
  27.8 1.3 collective-permute-start.4
  30.2 1.1 copy-done.3
  31.3 8.6 %shard_map.186 = (bf16[960,512]{1,0:T(8,128)(2,1)S(1)}, bf16[1600,960]{1,0:T(8,128)(2,1)S(1)}, f32[960,8]{1,0:T(8,128)S(1)}, bf16[960,256]{1,0:T(8,128)(2,1)S(1)...) custom-call(s32[2]{0:T(128)S(1)} %pad_add_fusion.me_ref, ...), custom_call_target="tpu_custom_call" | custom-call | flops 1000000 | bytes 1000000 | tf_op jit(solution)/shard_map/pallas_call | solution.py:211
  39.9 1.7 copy-done.4
  45.5 0.9 collective-permute-done.5
  47.1 1.4 collective-permute-start.12
  48.6 1.8 slice_reduce_fusion
  50.4 1.8 select_select_fusion.3
  52.3 1.9 multiply_reduce_fusion.1
  54.2 1.3 multiply_convert_fusion.3
  55.8 1.2 select_select_fusion.11
  57.1 6.0 %collective-permute-done.12 = bf16[480,640]{1,0:T(8,128)(2,1)S(1)} collective-permute-done((bf16[480,640]{1,0:T(8,128)(2,1)}, bf16[480,640]{1,0:T(8,128)(2,1)S(1)}, u32[]{:S(2)}, u32[]{:S(2)}) %collective-permute-start.12) | collective-permute-done | bytes 614432 | tf_op jit(solution)/shard_map/ppermute | solution.py:343
  63.8 1.2 fusion.58
  65.4 1.0 fusion.57
  66.7 2.3 %multiply_convert_fusion = (bf16[512,640]{1,0:T(8,128)(2,1)}, bf16[512,640]{1,0:T(8,128)(2,1)S(1)}, bf16[512,640]{1,0:T(8,128)(2,1)S(1)}) fusion(f32[512,640]{1,0:T(8,128)S(1)} %fusion.57, f32[512,640]{1,0:T(8,128)S(1)} %fusion.58, bf16[512,960]{0,1:T(8,128)(2,1)S(1)} %pad_maximum_fusion.4, bf16[240,640]{1,0:T(8,128)(2,1)S(1)} %get-tuple-element.206, ...), kind=kOutput, calls=%fused_computation.20 | convolution fusion | flops 638976000 | bytes 6799360 | tf_op jit(solution)/shard_map/dot_general | solution.py:40
  69.1 1.0 fusion.62
  70.2 1.0 add_convert_fusion
  72.7 1.2 pad_maximum_fusion.3
  74.2 1.9 %fusion.4 = bf16[256,960]{0,1:T(8,128)(2,1)} fusion(bf16[256,960]{0,1:T(8,128)(2,1)} %collective-permute-done.14, bf16[512,960]{0,1:T(8,128)(2,1)S(1)} %add_convert_fusion, s32[]{:T(128)S(6)} %mul.174), kind=kLoop, calls=%fused_computation.44 | loop fusion | flops 983040 | bytes 1474564 | tf_op jit(solution)/shard_map/convert_element_type | solution.py:461
  76.2 2.1 %fusion.63 = f32[960,640]{1,0:T(8,128)S(1)} fusion(bf16[512,960]{0,1:T(8,128)(2,1)S(1)} %pad_maximum_fusion.3, bf16[512,640]{1,0:T(8,128)(2,1)} %copy-done.50), kind=kOutput, calls=%fused_computation.193 | convolution fusion | flops 629145600 | bytes 4096000 | tf_op jit(solution)/shard_map/dot_general | solution.py:50
  78.3 1.5 copy-done.19
  81.6 1.0 fusion.8
  82.7 0.9 fusion.65
  83.6 1.4 copy-done.17
  85.9 1.0 convolution_convert_fusion
  86.9 1.0 copy-done.45
  88.9 1.2 broadcast_select_fusion.1
  90.0 1.6 collective-permute-start.15
  91.6 1.0 pad_maximum_fusion.5
  92.9 1.3 collective-permute-start.20
  94.2 1.2 collective-permute-start.21
  95.4 1.1 convert_add_fusion.1
  97.4 6.6 %collective-permute-done.15 = bf16[256,960]{0,1:T(8,128)(2,1)S(1)} collective-permute-done((bf16[256,960]{0,1:T(8,128)(2,1)}, bf16[256,960]{0,1:T(8,128)(2,1)S(1)}, u32[]{:S(2)}, u32[]{:S(2)}) %collective-permute-start.15) | collective-permute-done | bytes 491552 | tf_op jit(solution)/shard_map/ppermute | solution.py:343
  103.9 1.3 multiply_reduce_fusion
  105.3 1.3 fusion.59
  108.4 1.1 constant_dynamic-slice_fusion.12
  109.5 6.2 %shard_map.187 = (bf16[960,256]{1,0:T(8,128)(2,1)S(1)}, f32[640,512]{1,0:T(8,128)S(1)}, bf16[640,512]{1,0:T(8,128)(2,1)S(1)}) custom-call(s32[2]{0:T(128)S(1)} %pad_add_fusion.me_ref, bf16[960,256]{1,0:T(8,128)(2,1)S(1)} %convolution_convert_fusion.1.do_ref, bf16[960,256]{1,0:T(8,128)(2,1)S(1)} %copy-done.7, bf16[960,256]{1,0:T(8,128)(2,1)S(1)} %copy-done.10, ...), custom_call_target="tpu_custom_call" | custom-call | flops 1000000 | bytes 1000000 | tf_op jit(solution)/shard_map/pallas_call | solution.py:211
  116.4 1.2 bitcast_add_fusion.3
  117.6 1.6 broadcast_select_fusion.9
  121.9 1.1 copy-done.5
  123.0 1.5 fusion.13
  124.6 1.7 collective-permute-start.27
  126.5 0.9 constant_dynamic-slice_fusion.11
  129.2 1.9 %collective-permute-start.28 = (bf16[128,960]{0,1:T(8,128)(2,1)S(1)}, bf16[128,960]{0,1:T(8,128)(2,1)S(1)}, u32[]{:S(2)}, u32[]{:S(2)}) collective-permute-start(bf16[128,960]{0,1:T(8,128)(2,1)S(1)} %copy-done.72), channel_id=1, source_target_pairs={{0,24},{24,0},{8,16},{16,8},{1,25},{25,1},{9,17},{17,9},{2,26},{26... | collective-permute-start | bytes 737288 | tf_op jit(solution)/shard_map/ppermute | solution.py:343
  131.1 1.3 collective-permute-start.19
  133.2 1.0 copy-done.18
  134.2 1.2 bitcast_add_fusion.1
  135.6 1.2 bitcast_add_fusion.2
  137.3 2.9 %collective-permute-done.19 = bf16[2,120,640]{2,1,0:T(8,128)(2,1)S(1)} collective-permute-done((bf16[2,120,640]{2,1,0:T(8,128)(2,1)S(1)}, bf16[2,120,640]{2,1,0:T(8,128)(2,1)S(1)}, u32[]{:S(2)}, u32[]{:S(2)}) %collective-permute-start.19) | collective-permute-done | bytes 307232 | tf_op jit(solution)/shard_map/ppermute | solution.py:250
  140.3 2.4 %collective-permute-start.34 = (bf16[120,640]{1,0:T(8,128)(2,1)S(1)}, bf16[120,640]{1,0:T(8,128)(2,1)S(1)}, u32[]{:S(2)}, u32[]{:S(2)}) collective-permute-start(bf16[120,640]{1,0:T(8,128)(2,1)S(1)} %fusion.38), channel_id=1, source_target_pairs={{0,4},{1,5},{2,6},{3,7},{4,0},{5,1},{6,2},{7,3},{8,12},{9,13},{10,... | collective-permute-start | bytes 460808 | tf_op jit(solution)/shard_map/ppermute | solution.py:250
  142.9 1.2 fusion.17
  144.1 7.3 %collective-permute-done.29 = bf16[2,2,368,256]{3,2,0,1:T(8,128)(2,1)S(1)} collective-permute-done((bf16[2,2,368,256]{3,2,0,1:T(8,128)(2,1)S(1)}, bf16[2,2,368,256]{3,2,0,1:T(8,128)(2,1)S(1)}, u32[]{:S(2)}, u32[]{:S(2)}) %collective-permute-start.29) | collective-permute-done | bytes 753696 | tf_op jit(solution)/shard_map/ppermute | solution.py:250
  152.1 2.4 %collective-permute-start.35 = (bf16[240,320]{1,0:T(8,128)(2,1)S(1)}, bf16[240,320]{1,0:T(8,128)(2,1)S(1)}, u32[]{:S(2)}, u32[]{:S(2)}) collective-permute-start(bf16[240,320]{1,0:T(8,128)(2,1)S(1)} %select_convert_fusion), channel_id=1, source_target_pairs={{0,4},{1,5},{2,6},{3,7},{4,0},{5,1},{6,2},{7,3},{8,12},{9,13},{10,... | collective-permute-start | bytes 460808 | tf_op jit(solution)/shard_map/ppermute | solution.py:263
  154.4 3.5 %collective-permute-done.31 = bf16[2,120,640]{2,1,0:T(8,128)(2,1)S(1)} collective-permute-done((bf16[2,120,640]{2,1,0:T(8,128)(2,1)S(1)}, bf16[2,120,640]{2,1,0:T(8,128)(2,1)S(1)}, u32[]{:S(2)}, u32[]{:S(2)}) %collective-permute-start.31) | collective-permute-done | bytes 307232 | tf_op jit(solution)/shard_map/ppermute | solution.py:250
  158.1 2.4 %collective-permute-start.36 = (bf16[120,640]{1,0:T(8,128)(2,1)S(1)}, bf16[120,640]{1,0:T(8,128)(2,1)S(1)}, u32[]{:S(2)}, u32[]{:S(2)}) collective-permute-start(bf16[120,640]{1,0:T(8,128)(2,1)S(1)} %fusion.39), channel_id=1, source_target_pairs={{0,4},{1,5},{2,6},{3,7},{4,0},{5,1},{6,2},{7,3},{8,12},{9,13},{10,... | collective-permute-start | bytes 460808 | tf_op jit(solution)/shard_map/ppermute | solution.py:250
  160.4 7.3 %collective-permute-done.30 = bf16[2,368,256]{2,1,0:T(8,128)(2,1)S(1)} collective-permute-done((bf16[2,368,256]{2,1,0:T(8,128)(2,1)S(1)}, bf16[2,368,256]{2,1,0:T(8,128)(2,1)S(1)}, u32[]{:S(2)}, u32[]{:S(2)}) %collective-permute-start.30) | collective-permute-done | bytes 376864 | tf_op jit(solution)/shard_map/ppermute | solution.py:250
  168.1 2.4 %collective-permute-start.37 = (bf16[240,320]{1,0:T(8,128)(2,1)S(1)}, bf16[240,320]{1,0:T(8,128)(2,1)S(1)}, u32[]{:S(2)}, u32[]{:S(2)}) collective-permute-start(bf16[240,320]{1,0:T(8,128)(2,1)S(1)} %add_convert_fusion.2), channel_id=1, source_target_pairs={{0,0},{8,2},{16,4},{24,6},{1,8},{9,10},{17,12},{25,14},{2,16},{10,... | collective-permute-start | bytes 460808 | tf_op jit(solution)/shard_map/ppermute | solution.py:587
  172.1 16.2 %collective-permute-done.37 = bf16[240,320]{1,0:T(8,128)(2,1)S(1)} collective-permute-done((bf16[240,320]{1,0:T(8,128)(2,1)S(1)}, bf16[240,320]{1,0:T(8,128)(2,1)S(1)}, u32[]{:S(2)}, u32[]{:S(2)}) %collective-permute-start.37) | collective-permute-done | bytes 153632 | tf_op jit(solution)/shard_map/ppermute | solution.py:587
  (266 shorter events, 32.1 us)
Async XLA Ops:
  0.6 63.1 %copy-start = (bf16[960,640]{1,0:T(8,128)(2,1)S(1)}, bf16[960,640]{1,0:T(8,128)(2,1)}, u32[]{:S(2)}) copy-start(bf16[960,640]{1,0:T(8,128)(2,1)} %param.18) | copy-start | bytes 3686404
  0.7 9.0 %copy-start.24 = (bf16[1,128,960]{1,2,0:T(8,128)(2,1)S(1)}, bf16[1,128,960]{1,2,0:T(8,128)(2,1)}, u32[]{:S(2)}) copy-start(bf16[1,128,960]{1,2,0:T(8,128)(2,1)} %param.11) | copy-start | bytes 737284
  0.7 9.0 %collective-permute-start = (bf16[128,960]{0,1:T(8,128)(2,1)}, bf16[128,960]{0,1:T(8,128)(2,1)S(1)}, u32[]{:S(2)}, u32[]{:S(2)}) collective-permute-start(bf16[128,960]{0,1:T(8,128)(2,1)} %bitcast.126), channel_id=1, source_target_pairs={{0,24},{24,0},{8,16},{16,8},{1,25},{25,1},{9,17},{17,9},{2,26},{26... | collective-permute-start | bytes 737288 | tf_op jit(solution)/shard_map/ppermute | solution.py:343
  4.8 7.4 %copy-start.2 = (bf16[408,960]{1,0:T(8,128)(2,1)}, bf16[408,960]{1,0:T(8,128)(2,1)S(1)}, u32[]{:S(2)}) copy-start(bf16[408,960]{1,0:T(8,128)(2,1)S(1)} %fusion.5.own_ref) | copy-start | bytes 2350084
  4.9 22.6 %collective-permute-start.3 = (bf16[408,960]{1,0:T(8,128)(2,1)S(1)}, bf16[408,960]{1,0:T(8,128)(2,1)}, u32[]{:S(2)}, u32[]{:S(2)}) collective-permute-start(bf16[408,960]{1,0:T(8,128)(2,1)S(1)} %fusion.5.own_ref), channel_id=1, source_target_pairs={{0,24},{24,0},{8,16},{16,8},{1,25},{25,1},{9,17},{17,9},{2,26},{26... | collective-permute-start | bytes 2350088 | tf_op jit(solution)/shard_map/ppermute | solution.py:343
  5.1 24.8 %collective-permute-start.6 = (bf16[408,960]{1,0:T(8,128)(2,1)S(1)}, bf16[408,960]{1,0:T(8,128)(2,1)}, u32[]{:S(2)}, u32[]{:S(2)}) collective-permute-start(bf16[408,960]{1,0:T(8,128)(2,1)S(1)} %fusion.5.own_ref), channel_id=1, source_target_pairs={{0,8},{8,0},{16,24},{24,16},{1,9},{9,1},{17,25},{25,17},{2,10},{10... | collective-permute-start | bytes 2350088 | tf_op jit(solution)/shard_map/ppermute | solution.py:340
  9.7 3.8 %copy-start.36 = (bf16[128,960]{0,1:T(8,128)(2,1)}, bf16[128,960]{0,1:T(8,128)(2,1)S(1)}, u32[]{:S(2)}) copy-start(bf16[128,960]{0,1:T(8,128)(2,1)S(1)} %get-tuple-element.229) | copy-start | bytes 737284
  9.7 3.8 %copy-start.38 = (bf16[128,960]{0,1:T(8,128)(2,1)}, bf16[128,960]{0,1:T(8,128)(2,1)S(1)}, u32[]{:S(2)}) copy-start(bf16[128,960]{0,1:T(8,128)(2,1)S(1)} %get-tuple-element.230) | copy-start | bytes 737284
  9.8 3.7 %collective-permute-start.1 = (bf16[256,960]{0,1:T(8,128)(2,1)S(1)}, bf16[256,960]{0,1:T(8,128)(2,1)S(1)}, u32[]{:S(2)}, u32[]{:S(2)}) collective-permute-start(bf16[256,960]{0,1:T(8,128)(2,1)S(1)} %pad_maximum_fusion.8), channel_id=1, source_target_pairs={{0,8},{8,0},{16,24},{24,16},{1,9},{9,1},{17,25},{25,17},{2,10},{10... | collective-permute-start | bytes 1474568 | tf_op jit(solution)/shard_map/ppermute | solution.py:340
  27.4 2.7 %collective-permute-start.7 = (bf16[408,960]{1,0:T(8,128)(2,1)}, bf16[408,960]{1,0:T(8,128)(2,1)}, u32[]{:S(2)}, u32[]{:S(2)}) collective-permute-start(bf16[408,960]{1,0:T(8,128)(2,1)} %collective-permute-done.3.cross_ref), channel_id=1, source_target_pairs={{0,8},{8,0},{16,24},{24,16},{1,9},{9,1},{17,25},{25,17},{2,10},{10... | collective-permute-start | bytes 2350088 | tf_op jit(solution)/shard_map/ppermute | solution.py:340
  27.8 18.6 %collective-permute-start.4 = (bf16[240,960]{0,1:T(8,128)(2,1)}, bf16[240,960]{0,1:T(8,128)(2,1)}, u32[]{:S(2)}, u32[]{:S(2)}) collective-permute-start(bf16[240,960]{0,1:T(8,128)(2,1)} %bitcast.6), channel_id=1, source_target_pairs={{0,24},{24,0},{8,16},{16,8},{1,25},{25,1},{9,17},{17,9},{2,26},{26... | collective-permute-start | bytes 1382408 | tf_op jit(solution)/shard_map/ppermute | solution.py:343
  29.1 17.3 %collective-permute-start.5 = (bf16[128,960]{0,1:T(8,128)(2,1)}, bf16[128,960]{0,1:T(8,128)(2,1)}, u32[]{:S(2)}, u32[]{:S(2)}) collective-permute-start(bf16[128,960]{0,1:T(8,128)(2,1)} %bitcast.11), channel_id=1, source_target_pairs={{0,24},{24,0},{8,16},{16,8},{1,25},{25,1},{9,17},{17,9},{2,26},{26... | collective-permute-start | bytes 737288 | tf_op jit(solution)/shard_map/ppermute | solution.py:343
  29.7 20.7 %collective-permute-start.2 = (bf16[240,960]{0,1:T(8,128)(2,1)}, bf16[240,960]{0,1:T(8,128)(2,1)}, u32[]{:S(2)}, u32[]{:S(2)}) collective-permute-start(bf16[240,960]{0,1:T(8,128)(2,1)} %bitcast.6), channel_id=1, source_target_pairs={{0,8},{8,0},{16,24},{24,16},{1,9},{9,1},{17,25},{25,17},{2,10},{10... | collective-permute-start | bytes 1382408 | tf_op jit(solution)/shard_map/ppermute | solution.py:340
  46.4 4.0 %collective-permute-start.8 = (bf16[240,960]{0,1:T(8,128)(2,1)}, bf16[240,960]{0,1:T(8,128)(2,1)}, u32[]{:S(2)}, u32[]{:S(2)}) collective-permute-start(bf16[240,960]{0,1:T(8,128)(2,1)} %collective-permute-done.4), channel_id=1, source_target_pairs={{0,8},{8,0},{16,24},{24,16},{1,9},{9,1},{17,25},{25,17},{2,10},{10... | collective-permute-start | bytes 1382408 | tf_op jit(solution)/shard_map/ppermute | solution.py:340
  46.6 9.1 %collective-permute-start.10 = (bf16[128,960]{0,1:T(8,128)(2,1)}, bf16[128,960]{0,1:T(8,128)(2,1)S(1)}, u32[]{:S(2)}, u32[]{:S(2)}) collective-permute-start(bf16[128,960]{0,1:T(8,128)(2,1)} %bitcast.11), channel_id=1, source_target_pairs={{0,8},{8,0},{16,24},{24,16},{1,9},{9,1},{17,25},{25,17},{2,10},{10... | collective-permute-start | bytes 737288 | tf_op jit(solution)/shard_map/ppermute | solution.py:340
  46.9 8.8 %collective-permute-start.11 = (bf16[128,960]{0,1:T(8,128)(2,1)}, bf16[128,960]{0,1:T(8,128)(2,1)S(1)}, u32[]{:S(2)}, u32[]{:S(2)}) collective-permute-start(bf16[128,960]{0,1:T(8,128)(2,1)} %collective-permute-done.5), channel_id=1, source_target_pairs={{0,8},{8,0},{16,24},{24,16},{1,9},{9,1},{17,25},{25,17},{2,10},{10... | collective-permute-start | bytes 737288 | tf_op jit(solution)/shard_map/ppermute | solution.py:340
  47.1 16.0 %collective-permute-start.12 = (bf16[480,640]{1,0:T(8,128)(2,1)}, bf16[480,640]{1,0:T(8,128)(2,1)S(1)}, u32[]{:S(2)}, u32[]{:S(2)}) collective-permute-start(bf16[480,640]{1,0:T(8,128)(2,1)} %pad_maximum_fusion.6), channel_id=1, source_target_pairs={{0,24},{24,0},{8,16},{16,8},{1,25},{25,1},{9,17},{17,9},{2,26},{26... | collective-permute-start | bytes 1843208 | tf_op jit(solution)/shard_map/ppermute | solution.py:343
  55.5 7.6 %copy-start.42 = (bf16[240,640]{1,0:T(8,128)(2,1)S(1)}, bf16[240,640]{1,0:T(8,128)(2,1)}, u32[]{:S(2)}) copy-start(bf16[240,640]{1,0:T(8,128)(2,1)} %get-tuple-element.106) | copy-start | bytes 921604
  55.5 8.1 %collective-permute-start.9 = (bf16[256,960]{0,1:T(8,128)(2,1)S(1)}, bf16[256,960]{0,1:T(8,128)(2,1)S(1)}, u32[]{:S(2)}, u32[]{:S(2)}) collective-permute-start(bf16[256,960]{0,1:T(8,128)(2,1)S(1)} %get-tuple-element.196), channel_id=1, source_target_pairs={{0,8},{8,0},{16,24},{24,16},{1,9},{9,1},{17,25},{25,17},{2,10},{10... | collective-permute-start | bytes 1474568 | tf_op jit(solution)/shard_map/ppermute | solution.py:340
  57.1 9.6 %copy-start.22 = (bf16[512,960]{0,1:T(8,128)(2,1)}, bf16[512,960]{0,1:T(8,128)(2,1)S(1)}, u32[]{:S(2)}) copy-start(bf16[512,960]{0,1:T(8,128)(2,1)S(1)} %pad_maximum_fusion.4) | copy-start | bytes 2949124
  63.2 3.2 %collective-permute-start.13 = (bf16[480,640]{1,0:T(8,128)(2,1)S(1)}, bf16[480,640]{1,0:T(8,128)(2,1)S(1)}, u32[]{:S(2)}, u32[]{:S(2)}) collective-permute-start(bf16[480,640]{1,0:T(8,128)(2,1)S(1)} %pad_maximum_fusion.7), channel_id=1, source_target_pairs={{0,8},{8,0},{16,24},{24,16},{1,9},{9,1},{17,25},{25,17},{2,10},{10... | collective-permute-start | bytes 1843208 | tf_op jit(solution)/shard_map/ppermute | solution.py:340
  71.1 5.0 %copy-start.34 = (bf16[512,960]{0,1:T(8,128)(2,1)}, bf16[512,960]{0,1:T(8,128)(2,1)S(1)}, u32[]{:S(2)}) copy-start(bf16[512,960]{0,1:T(8,128)(2,1)S(1)} %add_convert_fusion) | copy-start | bytes 2949124
  72.0 2.2 %collective-permute-start.14 = (bf16[256,960]{0,1:T(8,128)(2,1)}, bf16[256,960]{0,1:T(8,128)(2,1)}, u32[]{:S(2)}, u32[]{:S(2)}) collective-permute-start(bf16[256,960]{0,1:T(8,128)(2,1)} %constant_dynamic-slice_fusion.19), channel_id=1, source_target_pairs={{0,8},{8,0},{16,24},{24,16},{1,9},{9,1},{17,25},{25,17},{2,10},{10... | collective-permute-start | bytes 1474568 | tf_op jit(solution)/shard_map/ppermute | solution.py:340
  72.3 16.5 %collective-permute-start.23 = (bf16[960,256]{1,0:T(8,128)(2,1)S(1)}, bf16[960,256]{1,0:T(8,128)(2,1)}, u32[]{:S(2)}, u32[]{:S(2)}) collective-permute-start(bf16[960,256]{1,0:T(8,128)(2,1)S(1)} %copy-done.7), channel_id=1, source_target_pairs={{0,8},{8,0},{16,24},{24,16},{1,9},{9,1},{17,25},{25,17},{2,10},{10... | collective-permute-start | bytes 1474568 | tf_op jit(solution)/shard_map/ppermute | solution.py:340
  76.2 4.5 %copy-start.49 = (bf16[512,640]{1,0:T(8,128)(2,1)S(1)}, bf16[512,640]{1,0:T(8,128)(2,1)}, u32[]{:S(2)}) copy-start(bf16[512,640]{1,0:T(8,128)(2,1)} %copy-done.48) | copy-start | bytes 1966084
  82.6 3.3 %copy-start.65 = (bf16[240,640]{1,0:T(8,128)(2,1)S(1)}, bf16[240,640]{1,0:T(8,128)(2,1)}, u32[]{:S(2)}) copy-start(bf16[240,640]{1,0:T(8,128)(2,1)} %copy-done.64) | copy-start | bytes 921604
  82.7 3.3 %copy-start.67 = (bf16[240,640]{1,0:T(8,128)(2,1)S(1)}, bf16[240,640]{1,0:T(8,128)(2,1)}, u32[]{:S(2)}) copy-start(bf16[240,640]{1,0:T(8,128)(2,1)} %copy-done.66) | copy-start | bytes 921604
  82.7 3.3 %copy-start.69 = (bf16[240,640]{1,0:T(8,128)(2,1)S(1)}, bf16[240,640]{1,0:T(8,128)(2,1)}, u32[]{:S(2)}) copy-start(bf16[240,640]{1,0:T(8,128)(2,1)} %copy-done.68) | copy-start | bytes 921604
  82.7 3.3 %copy-start.71 = (bf16[240,640]{1,0:T(8,128)(2,1)S(1)}, bf16[240,640]{1,0:T(8,128)(2,1)}, u32[]{:S(2)}) copy-start(bf16[240,640]{1,0:T(8,128)(2,1)} %copy-done.70) | copy-start | bytes 921604
  88.7 6.7 %collective-permute-start.16 = (bf16[256,960]{0,1:T(8,128)(2,1)}, bf16[256,960]{0,1:T(8,128)(2,1)}, u32[]{:S(2)}, u32[]{:S(2)}) collective-permute-start(bf16[256,960]{0,1:T(8,128)(2,1)} %constant_dynamic-slice_fusion.16), channel_id=1, source_target_pairs={{0,8},{8,0},{16,24},{24,16},{1,9},{9,1},{17,25},{25,17},{2,10},{10... | collective-permute-start | bytes 1474568 | tf_op jit(solution)/shard_map/ppermute | solution.py:340
  88.8 6.6 %copy-start.46 = (bf16[512,960]{0,1:T(8,128)(2,1)S(1)}, bf16[512,960]{0,1:T(8,128)(2,1)}, u32[]{:S(2)}) copy-start(bf16[512,960]{0,1:T(8,128)(2,1)} %copy-done.45) | copy-start | bytes 2949124
  90.0 13.9 %collective-permute-start.15 = (bf16[256,960]{0,1:T(8,128)(2,1)}, bf16[256,960]{0,1:T(8,128)(2,1)S(1)}, u32[]{:S(2)}, u32[]{:S(2)}) collective-permute-start(bf16[256,960]{0,1:T(8,128)(2,1)} %fusion.4), channel_id=1, source_target_pairs={{0,24},{24,0},{8,16},{16,8},{1,25},{25,1},{9,17},{17,9},{2,26},{26... | collective-permute-start | bytes 1474568 | tf_op jit(solution)/shard_map/ppermute | solution.py:343
  91.6 12.3 %copy-start.21 = (f32[256,960]{0,1:T(8,128)S(1)}, f32[256,960]{0,1:T(8,128)}, u32[]{:S(2)}) copy-start(f32[256,960]{0,1:T(8,128)} %get-tuple-element.197) | copy-start | bytes 2949124
  91.6 12.3 %copy-start.35 = (bf16[512,960]{0,1:T(8,128)(2,1)S(1)}, bf16[512,960]{0,1:T(8,128)(2,1)}, u32[]{:S(2)}) copy-start(bf16[512,960]{0,1:T(8,128)(2,1)} %copy-done.34) | copy-start | bytes 2949124
  92.6 23.7 %collective-permute-start.18 = (bf16[2,2,120,640]{3,2,0,1:T(8,128)(2,1)}, bf16[2,2,120,640]{3,2,0,1:T(8,128)(2,1)}, u32[]{:S(2)}, u32[]{:S(2)}) collective-permute-start(bf16[2,2,120,640]{3,2,0,1:T(8,128)(2,1)} %fusion.7), channel_id=1, source_target_pairs={{0,1},{1,0},{2,3},{3,2},{4,5},{5,4},{6,7},{7,6},{8,9},{9,8},{10,11... | collective-permute-start | bytes 1843208 | tf_op jit(solution)/shard_map/ppermute | solution.py:250
  92.9 42.8 %collective-permute-start.20 = (bf16[2,2,120,640]{3,2,0,1:T(8,128)(2,1)}, bf16[2,2,120,640]{3,2,0,1:T(8,128)(2,1)}, u32[]{:S(2)}, u32[]{:S(2)}) collective-permute-start(bf16[2,2,120,640]{3,2,0,1:T(8,128)(2,1)} %fusion.8), channel_id=1, source_target_pairs={{0,2},{1,3},{2,0},{3,1},{4,6},{5,7},{6,4},{7,5},{8,10},{9,11},{10,... | collective-permute-start | bytes 1843208 | tf_op jit(solution)/shard_map/ppermute | solution.py:250
  94.2 39.0 %collective-permute-start.21 = (bf16[2,240,640]{2,1,0:T(8,128)(2,1)}, bf16[2,240,640]{2,1,0:T(8,128)(2,1)}, u32[]{:S(2)}, u32[]{:S(2)}) collective-permute-start(bf16[2,240,640]{2,1,0:T(8,128)(2,1)} %fusion.9), channel_id=1, source_target_pairs={{0,1},{1,0},{2,3},{3,2},{4,5},{5,4},{6,7},{7,6},{8,9},{9,8},{10,11... | collective-permute-start | bytes 1843208 | tf_op jit(solution)/shard_map/ppermute | solution.py:250
  96.6 7.4 %copy-start.29 = (f32[256,960]{0,1:T(8,128)}, f32[256,960]{0,1:T(8,128)S(1)}, u32[]{:S(2)}) copy-start(f32[256,960]{0,1:T(8,128)S(1)} %convert_add_fusion.1) | copy-start | bytes 2949124
  108.4 8.1 %copy-start.20 = (f32[960,640]{1,0:T(8,128)S(1)}, f32[960,640]{1,0:T(8,128)}, u32[]{:S(2)}) copy-start(f32[960,640]{1,0:T(8,128)} %copy-done.19) | copy-start | bytes 7372804
  109.4 8.2 %collective-permute-start.24 = (bf16[256,240]{0,1:T(8,128)(2,1)S(1)}, bf16[256,240]{0,1:T(8,128)(2,1)S(1)}, u32[]{:S(2)}, u32[]{:S(2)}) collective-permute-start(bf16[256,240]{0,1:T(8,128)(2,1)S(1)} %constant_dynamic-slice_fusion.12), channel_id=1, source_target_pairs={{0,8},{8,0},{16,24},{24,16},{1,9},{9,1},{17,25},{25,17},{2,10},{10... | collective-permute-start | bytes 368648 | tf_op jit(solution)/shard_map/ppermute | solution.py:340
  115.8 4.3 %collective-permute-start.22 = (bf16[240,256]{1,0:T(8,128)(2,1)S(1)}, bf16[240,256]{1,0:T(8,128)(2,1)S(1)}, u32[]{:S(2)}, u32[]{:S(2)}) collective-permute-start(bf16[240,256]{1,0:T(8,128)(2,1)S(1)} %constant_dynamic-slice_fusion.14), channel_id=1, source_target_pairs={{0,8},{8,0},{16,24},{24,16},{1,9},{9,1},{17,25},{25,17},{2,10},{10... | collective-permute-start | bytes 368648 | tf_op jit(solution)/shard_map/ppermute | solution.py:340
  116.3 4.4 %collective-permute-start.17 = (bf16[640,512]{1,0:T(8,128)(2,1)S(1)}, bf16[640,512]{1,0:T(8,128)(2,1)S(1)}, u32[]{:S(2)}, u32[]{:S(2)}) collective-permute-start(bf16[640,512]{1,0:T(8,128)(2,1)S(1)} %get-tuple-element.127), channel_id=1, source_target_pairs={{0,8},{8,0},{16,24},{24,16},{1,9},{9,1},{17,25},{25,17},{2,10},{10... | collective-permute-start | bytes 1966088 | tf_op jit(solution)/shard_map/ppermute | solution.py:340
  123.0 4.5 %copy-start.61 = (bf16[240,256]{1,0:T(8,128)(2,1)S(1)}, bf16[240,256]{1,0:T(8,128)(2,1)}, u32[]{:S(2)}) copy-start(bf16[240,256]{1,0:T(8,128)(2,1)} %get-tuple-element.225) | copy-start | bytes 368644
  123.0 4.5 %copy-start.62 = (bf16[240,256]{1,0:T(8,128)(2,1)S(1)}, bf16[240,256]{1,0:T(8,128)(2,1)}, u32[]{:S(2)}) copy-start(bf16[240,256]{1,0:T(8,128)(2,1)} %get-tuple-element.226) | copy-start | bytes 368644
  124.6 4.6 %collective-permute-start.27 = (f32[2,240]{1,0:T(2,128)S(1)}, f32[2,240]{1,0:T(2,128)S(1)}, u32[]{:S(2)}, u32[]{:S(2)}) collective-permute-start(f32[2,240]{1,0:T(2,128)S(1)} %get-tuple-element.235), channel_id=1, source_target_pairs={{0,24},{24,0},{8,16},{16,8},{1,25},{25,1},{9,17},{17,9},{2,26},{26... | collective-permute-start | bytes 5768 | tf_op jit(solution)/shard_map/ppermute | solution.py:343
  126.2 4.9 %collective-permute-start.25 = (f32[2,240]{1,0:T(2,128)S(1)}, f32[2,240]{1,0:T(2,128)S(1)}, u32[]{:S(2)}, u32[]{:S(2)}) collective-permute-start(f32[2,240]{1,0:T(2,128)S(1)} %get-tuple-element.236), channel_id=1, source_target_pairs={{0,8},{8,0},{16,24},{24,16},{1,9},{9,1},{17,25},{25,17},{2,10},{10... | collective-permute-start | bytes 5768 | tf_op jit(solution)/shard_map/ppermute | solution.py:340
  126.3 6.2 %collective-permute-start.26 = (f32[2,240]{1,0:T(2,128)S(1)}, f32[2,240]{1,0:T(2,128)S(1)}, u32[]{:S(2)}, u32[]{:S(2)}) collective-permute-start(f32[2,240]{1,0:T(2,128)S(1)} %get-tuple-element.237), channel_id=1, source_target_pairs={{0,16},{16,0},{8,24},{24,8},{1,17},{17,1},{9,25},{25,9},{2,18},{18... | collective-permute-start | bytes 5768 | tf_op jit(solution)/shard_map/ppermute | solution.py:532
  128.0 3.2 %copy-start.63 = (bf16[2,120,640]{2,1,0:T(8,128)(2,1)S(1)}, bf16[2,120,640]{2,1,0:T(8,128)(2,1)}, u32[]{:S(2)}) copy-start(bf16[2,120,640]{2,1,0:T(8,128)(2,1)} %fusion.21) | copy-start | bytes 921604
  129.2 13.5 %collective-permute-start.28 = (bf16[128,960]{0,1:T(8,128)(2,1)S(1)}, bf16[128,960]{0,1:T(8,128)(2,1)S(1)}, u32[]{:S(2)}, u32[]{:S(2)}) collective-permute-start(bf16[128,960]{0,1:T(8,128)(2,1)S(1)} %copy-done.72), channel_id=1, source_target_pairs={{0,24},{24,0},{8,16},{16,8},{1,25},{25,1},{9,17},{17,9},{2,26},{26... | collective-permute-start | bytes 737288 | tf_op jit(solution)/shard_map/ppermute | solution.py:343
  131.1 9.1 %collective-permute-start.19 = (bf16[2,120,640]{2,1,0:T(8,128)(2,1)S(1)}, bf16[2,120,640]{2,1,0:T(8,128)(2,1)S(1)}, u32[]{:S(2)}, u32[]{:S(2)}) collective-permute-start(bf16[2,120,640]{2,1,0:T(8,128)(2,1)S(1)} %copy-done.63), channel_id=1, source_target_pairs={{0,2},{1,3},{2,0},{3,1},{4,6},{5,7},{6,4},{7,5},{8,10},{9,11},{10,... | collective-permute-start | bytes 921608 | tf_op jit(solution)/shard_map/ppermute | solution.py:250
  132.9 2.8 %copy-start.16 = (f32[960,640]{1,0:T(8,128)S(1)}, f32[960,640]{1,0:T(8,128)}, u32[]{:S(2)}) copy-start(f32[960,640]{1,0:T(8,128)} %copy-done.15) | copy-start | bytes 7372804
  132.9 18.5 %collective-permute-start.29 = (bf16[2,2,368,256]{3,2,0,1:T(8,128)(2,1)S(1)}, bf16[2,2,368,256]{3,2,0,1:T(8,128)(2,1)S(1)}, u32[]{:S(2)}, u32[]{:S(2)}) collective-permute-start(bf16[2,2,368,256]{3,2,0,1:T(8,128)(2,1)S(1)} %fusion.6), channel_id=1, source_target_pairs={{0,1},{1,0},{2,3},{3,2},{4,5},{5,4},{6,7},{7,6},{8,9},{9,8},{10,11... | collective-permute-start | bytes 2261000 | tf_op jit(solution)/shard_map/ppermute | solution.py:250
  135.4 16.5 %collective-permute-start.32 = (bf16[240,640]{1,0:T(8,128)(2,1)S(1)}, bf16[240,640]{1,0:T(8,128)(2,1)S(1)}, u32[]{:S(2)}, u32[]{:S(2)}) collective-permute-start(bf16[240,640]{1,0:T(8,128)(2,1)S(1)} %fusion.22), channel_id=1, source_target_pairs={{0,2},{1,3},{2,0},{3,1},{4,6},{5,7},{6,4},{7,5},{8,10},{9,11},{10,... | collective-permute-start | bytes 921608 | tf_op jit(solution)/shard_map/ppermute | solution.py:250
  136.8 6.1 %copy-start.30 = (f32[256,960]{0,1:T(8,128)S(1)}, f32[256,960]{0,1:T(8,128)}, u32[]{:S(2)}) copy-start(f32[256,960]{0,1:T(8,128)} %copy-done.29) | copy-start | bytes 2949124
  136.8 6.1 %copy-start.32 = (f32[256,960]{0,1:T(8,128)S(1)}, f32[256,960]{0,1:T(8,128)}, u32[]{:S(2)}) copy-start(f32[256,960]{0,1:T(8,128)} %copy-done.31) | copy-start | bytes 2949124
  136.9 6.1 %copy-start.33 = (f32[256,960]{0,1:T(8,128)S(1)}, f32[256,960]{0,1:T(8,128)}, u32[]{:S(2)}) copy-start(f32[256,960]{0,1:T(8,128)} %get-tuple-element.142) | copy-start | bytes 2949124
  136.9 21.0 %collective-permute-start.31 = (bf16[2,120,640]{2,1,0:T(8,128)(2,1)S(1)}, bf16[2,120,640]{2,1,0:T(8,128)(2,1)S(1)}, u32[]{:S(2)}, u32[]{:S(2)}) collective-permute-start(bf16[2,120,640]{2,1,0:T(8,128)(2,1)S(1)} %fusion.23), channel_id=1, source_target_pairs={{0,1},{1,0},{2,3},{3,2},{4,5},{5,4},{6,7},{7,6},{8,9},{9,8},{10,11... | collective-permute-start | bytes 921608 | tf_op jit(solution)/shard_map/ppermute | solution.py:250
  140.3 30.3 %collective-permute-start.34 = (bf16[120,640]{1,0:T(8,128)(2,1)S(1)}, bf16[120,640]{1,0:T(8,128)(2,1)S(1)}, u32[]{:S(2)}, u32[]{:S(2)}) collective-permute-start(bf16[120,640]{1,0:T(8,128)(2,1)S(1)} %fusion.38), channel_id=1, source_target_pairs={{0,4},{1,5},{2,6},{3,7},{4,0},{5,1},{6,2},{7,3},{8,12},{9,13},{10,... | collective-permute-start | bytes 460808 | tf_op jit(solution)/shard_map/ppermute | solution.py:250
  151.6 16.1 %collective-permute-start.30 = (bf16[2,368,256]{2,1,0:T(8,128)(2,1)S(1)}, bf16[2,368,256]{2,1,0:T(8,128)(2,1)S(1)}, u32[]{:S(2)}, u32[]{:S(2)}) collective-permute-start(bf16[2,368,256]{2,1,0:T(8,128)(2,1)S(1)} %fusion.20), channel_id=1, source_target_pairs={{0,2},{1,3},{2,0},{3,1},{4,6},{5,7},{6,4},{7,5},{8,10},{9,11},{10,... | collective-permute-start | bytes 1130504 | tf_op jit(solution)/shard_map/ppermute | solution.py:250
  152.1 15.9 %collective-permute-start.35 = (bf16[240,320]{1,0:T(8,128)(2,1)S(1)}, bf16[240,320]{1,0:T(8,128)(2,1)S(1)}, u32[]{:S(2)}, u32[]{:S(2)}) collective-permute-start(bf16[240,320]{1,0:T(8,128)(2,1)S(1)} %select_convert_fusion), channel_id=1, source_target_pairs={{0,4},{1,5},{2,6},{3,7},{4,0},{5,1},{6,2},{7,3},{8,12},{9,13},{10,... | collective-permute-start | bytes 460808 | tf_op jit(solution)/shard_map/ppermute | solution.py:263
  158.1 12.5 %collective-permute-start.36 = (bf16[120,640]{1,0:T(8,128)(2,1)S(1)}, bf16[120,640]{1,0:T(8,128)(2,1)S(1)}, u32[]{:S(2)}, u32[]{:S(2)}) collective-permute-start(bf16[120,640]{1,0:T(8,128)(2,1)S(1)} %fusion.39), channel_id=1, source_target_pairs={{0,4},{1,5},{2,6},{3,7},{4,0},{5,1},{6,2},{7,3},{8,12},{9,13},{10,... | collective-permute-start | bytes 460808 | tf_op jit(solution)/shard_map/ppermute | solution.py:250
  167.9 21.3 %collective-permute-start.33 = (bf16[368,256]{1,0:T(8,128)(2,1)S(1)}, bf16[368,256]{1,0:T(8,128)(2,1)S(1)}, u32[]{:S(2)}, u32[]{:S(2)}) collective-permute-start(bf16[368,256]{1,0:T(8,128)(2,1)S(1)} %fusion.33), channel_id=1, source_target_pairs={{0,4},{1,5},{2,6},{3,7},{4,0},{5,1},{6,2},{7,3},{8,12},{9,13},{10,... | collective-permute-start | bytes 565256 | tf_op jit(solution)/shard_map/ppermute | solution.py:250
  168.1 20.1 %collective-permute-start.37 = (bf16[240,320]{1,0:T(8,128)(2,1)S(1)}, bf16[240,320]{1,0:T(8,128)(2,1)S(1)}, u32[]{:S(2)}, u32[]{:S(2)}) collective-permute-start(bf16[240,320]{1,0:T(8,128)(2,1)S(1)} %add_convert_fusion.2), channel_id=1, source_target_pairs={{0,0},{8,2},{16,4},{24,6},{1,8},{9,10},{17,12},{25,14},{2,16},{10,... | collective-permute-start | bytes 460808 | tf_op jit(solution)/shard_map/ppermute | solution.py:587
  170.6 21.4 %copy-start.1 = (bf16[960,640]{1,0:T(8,128)(2,1)S(1)}, bf16[960,640]{1,0:T(8,128)(2,1)}, u32[]{:S(2)}) copy-start(bf16[960,640]{1,0:T(8,128)(2,1)} %param.18) | copy-start | bytes 3686404
  (49 other events, 83.2 us)

commit v2 on v1

--- a/solution.py
+++ b/solution.py
@@ -99,7 +99,7 @@
 
 def front_kernel(
     me_ref, x_ref, own_ref, beside_ref, cross_ref, corner_ref, cos_ref, sin_ref,
-    a1_ref, w_ref, gain_ref, q_ref, k_ref, v_ref, o_ref, lse_ref,
+    a1_ref, w_ref, gain_ref, q_ref, k_ref, v_ref, o_ref, lse_ref, gain_column,
 ):
     me = me_ref[0]
     second = me_ref[1]
@@ -117,10 +117,11 @@
             w_ref[pl.ds(pl.multiple_of(start, 16), kv_rows), :] = ref[first : first + kv_rows, :]
         gain_row = q_rows + 2 * kv_rows
         part_gains = ref[gain_row : gain_row + 8, 0:256].astype(jnp.float32).T
-        gain_ref[pl.ds(pl.multiple_of(device * q_rows, 8), q_rows), :] = part_gains[0:q_rows, :]
+        gain_column[pl.ds(pl.multiple_of(device * q_rows, 8), q_rows), :] = part_gains[0:q_rows, :]
+    gain_ref[...] = gain_column[...].T
     x = x_ref[...].astype(jnp.float32)
     scale = lax.rsqrt(jnp.mean(x * x, axis=0, keepdims=True) + EPS)
-    a1_ref[...] = ((x * scale) * gain_ref[:, 0:1]).astype(jnp.bfloat16)
+    a1_ref[...] = ((x * scale) * gain_column[:, 0:1]).astype(jnp.bfloat16)
     start = pl.multiple_of(second * (2 * block), 2 * block)
     a1_own = a1_ref[:, pl.ds(start, 2 * block)]
     a1 = a1_ref[...]
@@ -206,14 +207,15 @@
         sent_ref[kv_width + kv_start : kv_width + kv_stop, :] = d_values.astype(jnp.bfloat16)
 
 
-def whole(kernel, outs, *args):
+def whole(kernel, outs, *args, scratch=()):
     vmem = pl.BlockSpec(memory_space=pltpu.VMEM)
     return pl.pallas_call(
         kernel,
         out_shape=outs,
         in_specs=[pl.BlockSpec(memory_space=pltpu.SMEM)] + [vmem] * (len(args) - 1),
         out_specs=[vmem] * len(outs),
-        compiler_params=pltpu.CompilerParams(vmem_limit_bytes=40 * 1024 * 1024),
+        scratch_shapes=scratch,
+        compiler_params=pltpu.CompilerParams(vmem_limit_bytes=12 * 1024 * 1024),
         cost_estimate=pl.CostEstimate(flops=1000000, transcendentals=0, bytes_accessed=1000000),
     )(*args)
 
@@ -411,7 +413,7 @@
         [
             shaped(width, 4 * rows),
             shaped(width + 2 * kv_width, width),
-            shaped(width, 8, kind=jnp.float32),
+            shaped(8, width, kind=jnp.float32),
             shaped(width, half_rows),
             shaped(kv_width, 4 * rows),
             shaped(kv_width, 4 * rows),
@@ -419,9 +421,10 @@
             shaped(QUERY_HEADS + 1, half_rows, kind=jnp.float32),
         ],
         place, x_all.T, qkv_sent, qkv_beside, qkv_cross, qkv_corner, cosine, sine,
-    )
-    gain_attn = gains[:, 0]
-    gain_ffn = gains[:, 1]
+        scratch=[pltpu.VMEM((width, 8), jnp.float32)],
+    )
+    gain_attn = gains[0]
+    gain_ffn = gains[1]
     xf = x_pair.astype(jnp.float32)
     turn.mark(o_t)
     down_cross = chip_cross(turn.hold(down_far))
@@ -456,25 +459,25 @@
     d_up = (d_hidden * act).astype(bf16)
     d_a2_part = (dot_nt(d_gate, w_gate) + dot_nt(d_up, w_up)).astype(bf16)
 
-    beside_part = core_swap(lax.dynamic_slice_in_dim(d_a2_part, beside_start, half_rows, 0))
-    chip_sum = own_half(d_a2_part).astype(jnp.float32) + beside_part.astype(jnp.float32)
+    beside_sent = lax.dynamic_slice_in_dim(d_a2_part, beside_start, half_rows, 0)
+    beside_part = core_swap(beside_sent)
+    turn.mark(beside_sent)
+    a2_late, d_gate, d_up, hidden = turn.hold(a2, d_gate, d_up, hidden)
+    g_gate = dot_tn(a2_late, d_gate)
+    g_up = dot_tn(a2_late, d_up)
+    g_down = dot_tn(dy_all, hidden)
+    g_gate, g_up, g_down = lax.optimization_barrier((g_gate, g_up, g_down))
+    turn.mark(g_gate)
+    d_a2_kept, beside_part = turn.hold(d_a2_part, beside_part)
+    chip_sum = own_half(d_a2_kept).astype(jnp.float32) + beside_part.astype(jnp.float32)
     chip_sent = chip_sum.astype(bf16)
     other_chip = chip_cross(chip_sent)
     turn.mark(chip_sent)
-    a2_late, d_gate, d_up, hidden = turn.hold(a2, d_gate, d_up, hidden)
-    gate_sum = RepSum(by_rep(dot_tn(a2_late, d_gate)), (0, 1))
-    turn.mark(gate_sum.sent)
-    up_sum = RepSum(by_rep(dot_tn(turn.hold(a2_late), d_up)), (1, 0))
-    turn.mark(up_sum.sent)
-    g_down = dot_tn(turn.hold(dy_all), hidden).reshape(2, 2, slice_width, hidden_slice)
-    down_pair = swap_over_rep(g_down, 0, 1)
+    g_gate, g_up, g_down = turn.hold(g_gate, g_up, g_down)
+    gate_sum = RepSum(by_rep(g_gate), (0, 1))
+    up_sum = RepSum(by_rep(g_up), (1, 0))
+    down_pair = swap_over_rep(g_down.reshape(2, 2, slice_width, hidden_slice), 0, 1)
     turn.mark(down_pair[2])
-
-    out_part = dot_nt(turn.hold(hidden), down_rows_t).astype(bf16)
-    out_beside = core_swap(lax.dynamic_slice_in_dim(out_part, beside_start, half_rows, 0))
-    out_chip = own_half(out_part).astype(jnp.float32) + out_beside.astype(jnp.float32)
-    out_away = lax.dynamic_slice_in_dim(out_chip, rows - own_block_start, rows, 0).astype(bf16)
-    turn.mark(out_away)
 
     other_chip = turn.hold(other_chip)
     d_a2 = chip_sum + other_chip.astype(jnp.float32)
@@ -489,7 +492,6 @@
 
     d_o = row_major(dot_any(wo_t, d_x2_low, 0, 1).astype(bf16))
     turn.mark(d_o)
-    out_cross = chip_cross(turn.hold(out_away))
     d_o = turn.hold(d_o)
     d_q, d_kv, d_kv_sent = whole(
         back_kernel,
@@ -505,33 +507,32 @@
     d_q_kept = lax.dynamic_slice_in_dim(d_q, me * slice_width, slice_width, 0)
     d_q_halves = sets(d_q_kept, core_swap(d_q_away))
     turn.mark(d_q_away)
+    gate_sum.came, up_sum.came = turn.hold(gate_sum.came, up_sum.came)
     gate_sum.next(turn)
+    up_sum.next(turn)
+
+    def full_lanes(values):
+        return jnp.pad(values, ((0, 0), (0, 0), (0, -values.shape[2] % 128)))
+
+    o_all = jnp.concatenate(sets(*turn.hold(o_t, o_beside)), axis=1)
+    out_sum = RepSum(row_major(full_lanes(by_rep(dot_nn(o_all, columns_of(d_x2_low))))), (0, 1))
+    turn.mark(out_sum.sent)
     d_kv, d_kv_beside = turn.hold(d_kv, d_kv_beside)
     d_kv = (d_kv + d_kv_beside.astype(jnp.float32)).astype(bf16)
 
-    def block_lanes(values):
-        return jnp.where(me < 2, values[:, :rows], values[:, rows:])
-
     d_kv_half = jnp.where(second_set, d_kv[:, half_rows:], d_kv[:, :half_rows])
-    d_block = lax.optimization_barrier(
-        jnp.concatenate([block_lanes(d_q), block_lanes(d_kv_half)], axis=0)
-    )
-    d_a1 = dot_any(d_block, weights, 0, 0)
+    d_a1 = dot_any(jnp.concatenate([d_q, d_kv_half], axis=0), weights, 0, 0)
     x_block = x_here.astype(jnp.float32)
     r1_block = norm_scale(x_block)
     n1_block = x_block * r1_block
-    g_attn = jnp.sum(d_a1 * n1_block, axis=0)
-    g_ffn = jnp.sum(own_block(d_a2 * n2), axis=0)
+    g_attn = jnp.sum(d_a1 * (xf * norm_scale(xf)), axis=0)
+    g_ffn = jnp.sum(d_a2 * n2, axis=0)
     g_gains = jnp.stack([g_attn, g_ffn]).reshape(2, 4, slice_width).transpose(1, 0, 2)
 
     def gain_piece(k):
         return lax.dynamic_index_in_dim(g_gains, me ^ k, 0, keepdims=False)
 
-    gains_came = (
-        core_swap(gain_piece(1)),
-        lax.ppermute(gain_piece(2), "grp", CHIP_SWAP),
-        chip_cross(gain_piece(3)),
-    )
+    gains_came = core_swap(gain_piece(1))
     turn.mark(g_gains)
 
     kv_mine = [
@@ -539,43 +540,47 @@
     ]
     g_q = by_rep(dot_any(turn.hold(a1_t), jnp.concatenate(d_q_halves, axis=1), 1, 1))
     g_kv = by_rep(dot_any(turn.hold(a1_t), jnp.concatenate(kv_mine, axis=0), 1, 1))
-    o_all = jnp.concatenate(sets(o_t, o_beside), axis=1)
-    g_out = by_rep(dot_nn(turn.hold(o_all), columns_of(d_x2_low)))
-    turn.mark(g_out)
-    gains_came = turn.hold(*gains_came)
-    g_gains = gain_piece(0) + gains_came[0] + gains_came[1] + gains_came[2]
+    turn.mark(g_q)
+    gains_came, gate_sum.came = turn.hold(gains_came, gate_sum.came)
+    g_gains = gain_piece(0) + gains_came
     count = g_q.shape[0]
     share = g_q.shape[1]
     riders = jnp.broadcast_to(jnp.pad(g_gains, ((0, 6), (0, 0))), (count, 8, slice_width))
 
-    def full_lanes(values):
-        return jnp.pad(values, ((0, 0), (0, 0), (0, -values.shape[2] % 128)))
-
-    bundle = jnp.concatenate([full_lanes(part) for part in (g_q, g_out, g_kv, riders)], axis=1)
+    bundle = jnp.concatenate([full_lanes(part) for part in (g_q, g_kv, riders)], axis=1)
     attn_sum = RepSum(row_major(bundle), (0, 1))
     turn.mark(attn_sum.sent)
 
+    out_part = dot_nt(turn.hold(hidden), down_rows_t).astype(bf16)
+    out_beside = core_swap(lax.dynamic_slice_in_dim(out_part, beside_start, half_rows, 0))
     down_held = joined((down_pair[0], turn.hold(down_pair[1])))
     down_pair = swap_over_rep(down_held, 1, 0)
     turn.mark(down_pair[2])
+    gate_sum.next(turn)
     up_sum.next(turn)
-    gate_sum.next(turn)
-
+    out_sum.next(turn)
+    out_chip = own_half(out_part).astype(jnp.float32) + turn.hold(out_beside).astype(jnp.float32)
+    out_away = lax.dynamic_slice_in_dim(out_chip, rows - own_block_start, rows, 0).astype(bf16)
+    out_cross = chip_cross(out_away)
+    turn.mark(out_away)
     d_a1_late, d_x2_late = turn.hold(d_a1, d_x2)
+    d_a1_late = own_block(d_a1_late)
     d_n1 = d_a1_late * gain_attn
     input_grad = own_block(d_x2_late) + r1_block * (
         d_n1 - n1_block * jnp.mean(d_n1 * n1_block, axis=-1, keepdims=True)
     )
-    block_output = own_block(x2) + own_block(out_chip) + turn.hold(out_cross).astype(jnp.float32)
-    input_grad, block_output = lax.optimization_barrier((input_grad, block_output))
-    turn.mark(block_output)
+    input_grad = lax.optimization_barrier(input_grad)
+    turn.mark(input_grad)
 
     attn_sum.next(turn)
     down_held = joined((down_pair[0], turn.hold(down_pair[1])))
     parts = count // 4
     down_pair = halve_lanes_over_rep(down_held, rep_bits() - 1)
     turn.mark(down_pair[2])
-    up_sum.next(turn)
+    out_sum.next(turn)
+    block_output = own_block(x2) + own_block(out_chip) + turn.hold(out_cross).astype(jnp.float32)
+    block_output = lax.optimization_barrier(block_output)
+    turn.mark(block_output)
     attn_sum.next(turn)
     down_held = joined((down_pair[0], turn.hold(down_pair[1])))
     for bit in reversed(range(2, rep_bits() - 1)):
@@ -592,15 +597,16 @@
     g_gate, g_up, g_down = lax.optimization_barrier((g_gate, g_up, g_down))
     turn.mark(g_down)
     g_attn_w = row_major(attn_sum.end(turn))
-    g_kv = g_attn_w[2 * share : 3 * share]
+    g_kv = g_attn_w[share : 2 * share]
+    g_out = row_major(out_sum.end(turn))
     return (
         block_output[None],
         input_grad[None],
-        g_attn_w[3 * share : 3 * share + 2, :slice_width],
+        g_attn_w[2 * share : 2 * share + 2, :slice_width],
         g_attn_w[:share, :slice_width],
         g_kv[:, :kv_slice],
         g_kv[:, kv_slice : 2 * kv_slice],
-        g_attn_w[share : 2 * share, :slice_width],
+        g_out[:, :slice_width],
         g_gate,
         g_up,
         g_down,

time: 193 us -> 172 us (0.89)
  local copies, waits for them, and re-layouts: 32.4 us -> 20 us
  waiting for transfers between devices: 69.1 us -> 57.4 us
  other arithmetic: 27.3 us -> 23.4 us
  starting transfers between devices: 29.6 us -> 33.3 us
    ppermute x11 -> x14, waiting for transfers between devices: 21.1 us -> 8.98 us  [swap_over_rep(): came = lax.ppermute(away, 'rep', [(i, i ^ 1 << bit) for i in range(count)])]
    unnamed x154 -> x108, local copies, waits for them, and re-layouts: 18.4 us -> 10.6 us
    ppermute x8 -> x7, waiting for transfers between devices: 31.3 us -> 35.5 us  [chip_cross(): return lax.ppermute(values, 'grp', CROSS_SWAP)]
    ppermute x1, waiting for transfers between devices: 16.2 us -> 12.6 us  [per_device(): g_down = lax.ppermute(down_sent, ('grp', 'rep'), homes)]
    add x11 -> x14, other arithmetic: 5.54 us -> 8.57 us  [joined(): return pair[0] + pair[1].astype(jnp.float32)]
    dot_general x5, matrix products: 5.2 us -> 7.22 us  [dot_any(): lax.dot_general(left, right, (((left_dim,), (right_dim,)), ((), ())), pre...]
    convert_element_type x11 -> x14, local copies, waits for them, and re-layouts: 3.85 us -> 5.46 us  [swap_over_rep(): lax.dynamic_index_in_dim(held, 1 - mine, axis, keepdims=False)]
    ppermute x8 -> x7, starting transfers between devices: 10.4 us -> 9.11 us  [chip_cross(): return lax.ppermute(values, 'grp', CROSS_SWAP)]
  transfers between devices with their start and end apart: 38 -> 39, of which waited for: 12 -> 11; matrix products, arithmetic and copies ran while one was open for 28% -> 28% of each run, Pallas kernels for 8% -> 10%
where the time goes in v2:
time: 172 us; the launch traced here: 169 us
  waiting for transfers between devices  57.4 us (33%)
  starting transfers between devices  33.3 us (19%)
  other arithmetic  23.4 us (14%)
  local copies, waits for them, and re-layouts  20 us (12%)
  matrix products  17.1 us (10%)
  Pallas kernels  16.3 us (9%)
  between operations  1.75 us (1%)
    ppermute x7, waiting for transfers between devices, chip_cross(): return lax.ppermute(values, 'grp', CROSS_SWAP)  35.5 us
    pallas_call x2, Pallas kernels, whole(): pl.pallas_call(kernel, out_shape=outs, in_specs=[pl.BlockSpec(memory_spac...  16.3 us
    ppermute x1, waiting for transfers between devices, per_device(): g_down = lax.ppermute(down_sent, ('grp', 'rep'), homes)  12.6 us
    ppermute x14, starting transfers between devices, swap_over_rep(): came = lax.ppermute(away, 'rep', [(i, i ^ 1 << bit) for i in range(count)])  11.1 us
    unnamed x108, local copies, waits for them, and re-layouts  10.6 us
    ppermute x7, starting transfers between devices, chip_cross(): return lax.ppermute(values, 'grp', CROSS_SWAP)  9.11 us
    ppermute x14, waiting for transfers between devices, swap_over_rep(): came = lax.ppermute(away, 'rep', [(i, i ^ 1 << bit) for i in range(count)])  8.98 us
    add x14, other arithmetic, joined(): return pair[0] + pair[1].astype(jnp.float32)  8.57 us
  transfers between devices with their start and end apart: 39, of which 11 were waited for; matrix products, arithmetic and copies ran while one was open for 28% of the time, Pallas kernels for 10%

profile of v2, /device:TPU:5, one launch (start us, length us, event | category | flops | bytes accessed | tf_op | source)
XLA Modules:
  0.0 169.4 jit_solution(11375579654051360569)
XLA Ops:
  0.7 1.8 %collective-permute-start = (bf16[128,960]{0,1:T(8,128)(2,1)}, bf16[128,960]{0,1:T(8,128)(2,1)S(1)}, u32[]{:S(2)}, u32[]{:S(2)}) collective-permute-start(bf16[128,960]{0,1:T(8,128)(2,1)} %bitcast.128), channel_id=1, source_target_pairs={{0,24},{24,0},{8,16},{16,8},{1,25},{25,1},{9,17},{17,9},{2,26},{26... | collective-permute-start | bytes 737288 | tf_op jit(solution)/shard_map/ppermute | solution.py:345
  2.5 1.2 copy.45
  3.7 1.1 fusion.11.own_ref
  5.6 4.1 %collective-permute-done = bf16[128,960]{0,1:T(8,128)(2,1)S(1)} collective-permute-done((bf16[128,960]{0,1:T(8,128)(2,1)}, bf16[128,960]{0,1:T(8,128)(2,1)S(1)}, u32[]{:S(2)}, u32[]{:S(2)}) %collective-permute-start) | collective-permute-done | bytes 245792 | tf_op jit(solution)/shard_map/ppermute | solution.py:345
  10.0 2.2 %dynamic-slice_bitcast_fusion.1 = (bf16[240,640]{1,0:T(8,128)(2,1)S(1)}, bf16[240,640]{1,0:T(8,128)(2,1)S(1)}, bf16[240,640]{1,0:T(8,128)(2,1)}, bf16[240,640]{1,0:T(8,128)(2,1)}) fusion(bf16[2560,240]{0,1:T(8,128)(2,1)} %param.20, s32[]{:T(128)S(6)} %select_n.368, s32[]{:T(128)S(6)} %select_n.369, s32[]{:T(128)S(6)} %select_n.367, s32[]{:T(128)S(6)} %select_n.366), kind=kLoop, calls=%fused_computation.110 | loop fusion | bytes 2457616 | tf_op jit(solution)/shard_map/dynamic_slice | solution.py:393
  12.2 0.9 pad_maximum_fusion.5
  13.7 13.7 %collective-permute-done.3.cross_ref = bf16[408,960]{1,0:T(8,128)(2,1)} collective-permute-done((bf16[408,960]{1,0:T(8,128)(2,1)S(1)}, bf16[408,960]{1,0:T(8,128)(2,1)}, u32[]{:S(2)}, u32[]{:S(2)}) %collective-permute-start.3) | collective-permute-done | bytes 783392 | tf_op jit(solution)/shard_map/ppermute | solution.py:345
  27.8 1.3 collective-permute-start.6
  29.7 1.1 fusion.26
  31.0 1.1 copy-done.3
  32.1 9.5 %shard_map.186 = (bf16[960,512]{1,0:T(8,128)(2,1)S(1)}, bf16[1600,960]{1,0:T(8,128)(2,1)S(1)}, f32[8,960]{1,0:T(8,128)S(1)}, bf16[960,256]{1,0:T(8,128)(2,1)S(1)...) custom-call(s32[2]{0:T(128)S(1)} %pad_add_fusion.me_ref, ...), custom_call_target="tpu_custom_call" | custom-call | flops 1000000 | bytes 1000000 | tf_op jit(solution)/shard_map/pallas_call | solution.py:212
  41.6 1.7 copy-done.10
  43.3 3.1 %collective-permute-done.7 = bf16[128,960]{0,1:T(8,128)(2,1)} collective-permute-done((bf16[128,960]{0,1:T(8,128)(2,1)}, bf16[128,960]{0,1:T(8,128)(2,1)}, u32[]{:S(2)}, u32[]{:S(2)}) %collective-permute-start.7) | collective-permute-done | bytes 245792 | tf_op jit(solution)/shard_map/ppermute | solution.py:345
  47.4 1.4 collective-permute-start.12
  48.8 1.4 select_select_fusion.3
  50.3 2.9 %multiply_reduce_fusion.2 = (f32[256]{0:T(256)S(1)}, f32[256,960]{0,1:T(8,128)S(1)}) fusion(bf16[960,256]{1,0:T(8,128)(2,1)} %get-tuple-element.146.o_ref, bf16[240,960]{0,1:T(8,128)(2,1)S(1)} %get-tuple-element.212, bf16[240,960]{0,1:T(8,128)(2,1)S(1)} %get-tuple-element.213, bf16[240,960]{0,1:T(8,128)(2,1)S(1)} %get-tuple-element.214, ...), kind=kOutput, calls=%fused_computation.48 | convolution fusion | flops 480952064 | bytes 3810304 | tf_op jit(solution)/shard_map/dot_general | solution.py:56
  53.7 1.2 select_select_fusion.11
  55.0 8.1 %collective-permute-done.12 = bf16[480,640]{1,0:T(8,128)(2,1)S(1)} collective-permute-done((bf16[480,640]{1,0:T(8,128)(2,1)S(1)}, bf16[480,640]{1,0:T(8,128)(2,1)S(1)}, u32[]{:S(2)}, u32[]{:S(2)}) %collective-permute-start.12) | collective-permute-done | bytes 614432 | tf_op jit(solution)/shard_map/ppermute | solution.py:345
  64.0 1.2 fusion.61
  65.3 1.0 fusion.60
  66.4 0.9 copy-done.36
  67.5 1.5 multiply_convert_fusion
  69.1 1.0 fusion.65
  70.0 1.0 add_convert_fusion
  71.2 0.9 fusion.66
  72.2 0.9 fusion.67
  73.1 0.9 fusion.68
  74.2 1.6 collective-permute-start.15
  75.9 0.9 fusion.16
  77.1 0.9 fusion.17
  78.0 1.3 collective-permute-start.20
  79.3 0.9 fusion.18
  80.2 1.2 collective-permute-start.27
  81.4 6.5 %collective-permute-done.15 = bf16[256,960]{0,1:T(8,128)(2,1)S(1)} collective-permute-done((bf16[256,960]{0,1:T(8,128)(2,1)S(1)}, bf16[256,960]{0,1:T(8,128)(2,1)S(1)}, u32[]{:S(2)}, u32[]{:S(2)}) %collective-permute-start.15) | collective-permute-done | bytes 491552 | tf_op jit(solution)/shard_map/ppermute | solution.py:345
  88.5 1.4 fusion.62
  89.9 0.9 convolution_convert_fusion.1.do_ref
  91.3 6.9 %shard_map.187 = (bf16[960,256]{1,0:T(8,128)(2,1)S(1)}, f32[640,512]{1,0:T(8,128)S(1)}, bf16[640,512]{1,0:T(8,128)(2,1)S(1)}) custom-call(s32[2]{0:T(128)S(1)} %pad_add_fusion.me_ref, bf16[960,256]{1,0:T(8,128)(2,1)S(1)} %convolution_convert_fusion.1.do_ref, bf16[960,256]{1,0:T(8,128)(2,1)} %get-tuple-element.146.o_ref, bf16[960,256]{1,0:T(8,128)(2,1)S(1)} %copy-done.5, ...), custom_call_target="tpu_custom_call" | custom-call | flops 1000000 | bytes 1000000 | tf_op jit(solution)/shard_map/pallas_call | solution.py:212
  98.8 1.3 bitcast_add_fusion.1
  101.0 1.2 bitcast_add_fusion.2
  103.0 1.2 broadcast_select_fusion.1
  104.3 1.6 collective-permute-start.23
  105.8 0.9 broadcast_select_fusion.9
  108.2 1.3 collective-permute-start.25
  110.5 1.5 copy-done.11
  111.9 2.5 %fusion.5 = (f32[960]{0:T(1024)S(1)}, f32[256,960]{0,1:T(8,128)}) fusion(f32[256]{0:T(256)S(1)} %add_rsqrt_fusion, bf16[128,960]{0,1:T(8,128)(2,1)S(1)} %copy-done.27, bf16[128,960]{0,1:T(8,128)(2,1)S(1)} %copy-done.24, bf16[1600,960]{1,0:T(8,128)(2,1)S(1)} %copy-done.11, bf16[640,256]{1,0:T(8,128)(2,1)S(1)} %slice_select_fusion, ...), kind=kOutput, calls=%fused_computation.33 | convolution fusion | flops 789789760 | bytes 5370624 | tf_op jit(solution)/shard_map/dot_general | solution.py:56
  114.5 1.1 collective-permute-start.22
  117.0 1.2 copy-done.15
  118.2 1.2 bitcast_add_fusion
  119.7 1.2 bitcast_add_fusion.5
  121.0 2.4 %collective-permute-start.34 = (bf16[120,640]{1,0:T(8,128)(2,1)S(1)}, bf16[120,640]{1,0:T(8,128)(2,1)S(1)}, u32[]{:S(2)}, u32[]{:S(2)}) collective-permute-start(bf16[120,640]{1,0:T(8,128)(2,1)S(1)} %fusion.44), channel_id=1, source_target_pairs={{0,4},{1,5},{2,6},{3,7},{4,0},{5,1},{6,2},{7,3},{8,12},{9,13},{10,... | collective-permute-start | bytes 460808 | tf_op jit(solution)/shard_map/ppermute | solution.py:252
  123.3 1.0 convolution_convert_fusion
  125.5 1.1 bitcast_add_fusion.8
  126.7 1.3 collective-permute-start.29
  128.4 1.0 fusion.25
  129.6 2.3 %collective-permute-start.28 = (bf16[128,960]{0,1:T(8,128)(2,1)S(1)}, bf16[128,960]{0,1:T(8,128)(2,1)S(1)}, u32[]{:S(2)}, u32[]{:S(2)}) collective-permute-start(bf16[128,960]{0,1:T(8,128)(2,1)S(1)} %dynamic-slice_convert_fusion.4), channel_id=1, source_target_pairs={{0,24},{24,0},{8,16},{16,8},{1,25},{25,1},{9,17},{17,9},{2,26},{26... | collective-permute-start | bytes 737288 | tf_op jit(solution)/shard_map/ppermute | solution.py:345
  132.1 1.1 collective-permute-done.30
  133.4 2.4 %collective-permute-done.29 = bf16[2,120,256]{2,1,0:T(8,128)(2,1)S(1)} collective-permute-done((bf16[2,120,256]{2,1,0:T(8,128)(2,1)S(1)}, bf16[2,120,256]{2,1,0:T(8,128)(2,1)S(1)}, u32[]{:S(2)}, u32[]{:S(2)}) %collective-permute-start.29) | collective-permute-done | bytes 122912 | tf_op jit(solution)/shard_map/ppermute | solution.py:252
  136.0 3.8 %collective-permute-start.35 = (bf16[240,320]{1,0:T(8,128)(2,1)S(1)}, bf16[240,320]{1,0:T(8,128)(2,1)S(1)}, u32[]{:S(2)}, u32[]{:S(2)}) collective-permute-start(bf16[240,320]{1,0:T(8,128)(2,1)S(1)} %select_convert_fusion), channel_id=1, source_target_pairs={{0,4},{1,5},{2,6},{3,7},{4,0},{5,1},{6,2},{7,3},{8,12},{9,13},{10,... | collective-permute-start | bytes 460808 | tf_op jit(solution)/shard_map/ppermute | solution.py:265
  139.8 1.2 collective-permute-start.38
  141.0 0.9 convert_add_fusion.4
  141.8 5.1 %collective-permute-done.32 = bf16[2,248,256]{2,1,0:T(8,128)(2,1)S(1)} collective-permute-done((bf16[2,248,256]{2,1,0:T(8,128)(2,1)S(1)}, bf16[2,248,256]{2,1,0:T(8,128)(2,1)S(1)}, u32[]{:S(2)}, u32[]{:S(2)}) %collective-permute-start.32) | collective-permute-done | bytes 253984 | tf_op jit(solution)/shard_map/ppermute | solution.py:252
  147.3 3.6 %collective-permute-start.37 = (bf16[240,320]{1,0:T(8,128)(2,1)S(1)}, bf16[240,320]{1,0:T(8,128)(2,1)S(1)}, u32[]{:S(2)}, u32[]{:S(2)}) collective-permute-start(bf16[240,320]{1,0:T(8,128)(2,1)S(1)} %add_convert_fusion.2), channel_id=1, source_target_pairs={{0,0},{8,2},{16,4},{24,6},{1,8},{9,10},{17,12},{25,14},{2,16},{10,... | collective-permute-start | bytes 460808 | tf_op jit(solution)/shard_map/ppermute | solution.py:592
  152.4 12.6 %collective-permute-done.37 = bf16[240,320]{1,0:T(8,128)(2,1)S(1)} collective-permute-done((bf16[240,320]{1,0:T(8,128)(2,1)S(1)}, bf16[240,320]{1,0:T(8,128)(2,1)S(1)}, u32[]{:S(2)}, u32[]{:S(2)}) %collective-permute-start.37) | collective-permute-done | bytes 153632 | tf_op jit(solution)/shard_map/ppermute | solution.py:592
  166.4 0.9 copy.58
  (228 shorter events, 21.2 us)
Async XLA Ops:
  0.6 63.3 %copy-start = (bf16[960,640]{1,0:T(8,128)(2,1)S(1)}, bf16[960,640]{1,0:T(8,128)(2,1)}, u32[]{:S(2)}) copy-start(bf16[960,640]{1,0:T(8,128)(2,1)} %param.18) | copy-start | bytes 3686404
  0.7 9.0 %copy-start.20 = (bf16[1,128,960]{1,2,0:T(8,128)(2,1)S(1)}, bf16[1,128,960]{1,2,0:T(8,128)(2,1)}, u32[]{:S(2)}) copy-start(bf16[1,128,960]{1,2,0:T(8,128)(2,1)} %param.11) | copy-start | bytes 737284
  0.7 9.0 %collective-permute-start = (bf16[128,960]{0,1:T(8,128)(2,1)}, bf16[128,960]{0,1:T(8,128)(2,1)S(1)}, u32[]{:S(2)}, u32[]{:S(2)}) collective-permute-start(bf16[128,960]{0,1:T(8,128)(2,1)} %bitcast.128), channel_id=1, source_target_pairs={{0,24},{24,0},{8,16},{16,8},{1,25},{25,1},{9,17},{17,9},{2,26},{26... | collective-permute-start | bytes 737288 | tf_op jit(solution)/shard_map/ppermute | solution.py:345
  4.8 7.4 %copy-start.2 = (bf16[408,960]{1,0:T(8,128)(2,1)}, bf16[408,960]{1,0:T(8,128)(2,1)S(1)}, u32[]{:S(2)}) copy-start(bf16[408,960]{1,0:T(8,128)(2,1)S(1)} %fusion.11.own_ref) | copy-start | bytes 2350084
  4.9 22.6 %collective-permute-start.3 = (bf16[408,960]{1,0:T(8,128)(2,1)S(1)}, bf16[408,960]{1,0:T(8,128)(2,1)}, u32[]{:S(2)}, u32[]{:S(2)}) collective-permute-start(bf16[408,960]{1,0:T(8,128)(2,1)S(1)} %fusion.11.own_ref), channel_id=1, source_target_pairs={{0,24},{24,0},{8,16},{16,8},{1,25},{25,1},{9,17},{17,9},{2,26},{26... | collective-permute-start | bytes 2350088 | tf_op jit(solution)/shard_map/ppermute | solution.py:345
  5.1 25.9 %collective-permute-start.2 = (bf16[408,960]{1,0:T(8,128)(2,1)S(1)}, bf16[408,960]{1,0:T(8,128)(2,1)}, u32[]{:S(2)}, u32[]{:S(2)}) collective-permute-start(bf16[408,960]{1,0:T(8,128)(2,1)S(1)} %fusion.11.own_ref), channel_id=1, source_target_pairs={{0,8},{8,0},{16,24},{24,16},{1,9},{9,1},{17,25},{25,17},{2,10},{10... | collective-permute-start | bytes 2350088 | tf_op jit(solution)/shard_map/ppermute | solution.py:342
  9.8 3.7 %collective-permute-start.1 = (bf16[256,960]{0,1:T(8,128)(2,1)S(1)}, bf16[256,960]{0,1:T(8,128)(2,1)S(1)}, u32[]{:S(2)}, u32[]{:S(2)}) collective-permute-start(bf16[256,960]{0,1:T(8,128)(2,1)S(1)} %pad_maximum_fusion.7), channel_id=1, source_target_pairs={{0,8},{8,0},{16,24},{24,16},{1,9},{9,1},{17,25},{25,17},{2,10},{10... | collective-permute-start | bytes 1474568 | tf_op jit(solution)/shard_map/ppermute | solution.py:342
  27.4 3.5 %collective-permute-start.4 = (bf16[408,960]{1,0:T(8,128)(2,1)}, bf16[408,960]{1,0:T(8,128)(2,1)}, u32[]{:S(2)}, u32[]{:S(2)}) collective-permute-start(bf16[408,960]{1,0:T(8,128)(2,1)} %collective-permute-done.3.cross_ref), channel_id=1, source_target_pairs={{0,8},{8,0},{16,24},{24,16},{1,9},{9,1},{17,25},{25,17},{2,10},{10... | collective-permute-start | bytes 2350088 | tf_op jit(solution)/shard_map/ppermute | solution.py:342
  27.8 18.6 %collective-permute-start.6 = (bf16[240,960]{0,1:T(8,128)(2,1)}, bf16[240,960]{0,1:T(8,128)(2,1)}, u32[]{:S(2)}, u32[]{:S(2)}) collective-permute-start(bf16[240,960]{0,1:T(8,128)(2,1)} %bitcast.6), channel_id=1, source_target_pairs={{0,24},{24,0},{8,16},{16,8},{1,25},{25,1},{9,17},{17,9},{2,26},{26... | collective-permute-start | bytes 1382408 | tf_op jit(solution)/shard_map/ppermute | solution.py:345
  29.1 17.3 %collective-permute-start.7 = (bf16[128,960]{0,1:T(8,128)(2,1)}, bf16[128,960]{0,1:T(8,128)(2,1)}, u32[]{:S(2)}, u32[]{:S(2)}) collective-permute-start(bf16[128,960]{0,1:T(8,128)(2,1)} %bitcast.11), channel_id=1, source_target_pairs={{0,24},{24,0},{8,16},{16,8},{1,25},{25,1},{9,17},{17,9},{2,26},{26... | collective-permute-start | bytes 737288 | tf_op jit(solution)/shard_map/ppermute | solution.py:345
  30.7 18.1 %collective-permute-start.5 = (bf16[240,960]{0,1:T(8,128)(2,1)}, bf16[240,960]{0,1:T(8,128)(2,1)S(1)}, u32[]{:S(2)}, u32[]{:S(2)}) collective-permute-start(bf16[240,960]{0,1:T(8,128)(2,1)} %bitcast.6), channel_id=1, source_target_pairs={{0,8},{8,0},{16,24},{24,16},{1,9},{9,1},{17,25},{25,17},{2,10},{10... | collective-permute-start | bytes 1382408 | tf_op jit(solution)/shard_map/ppermute | solution.py:342
  32.1 14.8 %copy-start.23 = (bf16[128,960]{0,1:T(8,128)(2,1)S(1)}, bf16[128,960]{0,1:T(8,128)(2,1)}, u32[]{:S(2)}) copy-start(bf16[128,960]{0,1:T(8,128)(2,1)} %copy-done.22) | copy-start | bytes 737284
  32.1 14.8 %copy-start.26 = (bf16[128,960]{0,1:T(8,128)(2,1)S(1)}, bf16[128,960]{0,1:T(8,128)(2,1)}, u32[]{:S(2)}) copy-start(bf16[128,960]{0,1:T(8,128)(2,1)} %copy-done.25) | copy-start | bytes 737284
  32.1 15.3 %copy-start.41 = (bf16[480,640]{1,0:T(8,128)(2,1)S(1)}, bf16[480,640]{1,0:T(8,128)(2,1)}, u32[]{:S(2)}) copy-start(bf16[480,640]{1,0:T(8,128)(2,1)} %pad_maximum_fusion.5) | copy-start | bytes 1843204
  43.3 7.0 %copy-start.4 = (bf16[960,256]{1,0:T(8,128)(2,1)}, bf16[960,256]{1,0:T(8,128)(2,1)S(1)}, u32[]{:S(2)}) copy-start(bf16[960,256]{1,0:T(8,128)(2,1)S(1)} %get-tuple-element.131.q_ref) | copy-start | bytes 1474564
  43.3 7.0 %copy-start.6 = (bf16[320,512]{1,0:T(8,128)(2,1)}, bf16[320,512]{1,0:T(8,128)(2,1)S(1)}, u32[]{:S(2)}) copy-start(bf16[320,512]{1,0:T(8,128)(2,1)S(1)} %get-tuple-element.132.k_ref) | copy-start | bytes 983044
  43.3 7.0 %copy-start.8 = (bf16[320,512]{1,0:T(8,128)(2,1)}, bf16[320,512]{1,0:T(8,128)(2,1)S(1)}, u32[]{:S(2)}) copy-start(bf16[320,512]{1,0:T(8,128)(2,1)S(1)} %get-tuple-element.133.v_ref) | copy-start | bytes 983044
  46.4 2.4 %collective-permute-start.8 = (bf16[240,960]{0,1:T(8,128)(2,1)}, bf16[240,960]{0,1:T(8,128)(2,1)S(1)}, u32[]{:S(2)}, u32[]{:S(2)}) collective-permute-start(bf16[240,960]{0,1:T(8,128)(2,1)} %collective-permute-done.6), channel_id=1, source_target_pairs={{0,8},{8,0},{16,24},{24,16},{1,9},{9,1},{17,25},{25,17},{2,10},{10... | collective-permute-start | bytes 1382408 | tf_op jit(solution)/shard_map/ppermute | solution.py:342
  46.6 7.1 %collective-permute-start.10 = (bf16[128,960]{0,1:T(8,128)(2,1)}, bf16[128,960]{0,1:T(8,128)(2,1)S(1)}, u32[]{:S(2)}, u32[]{:S(2)}) collective-permute-start(bf16[128,960]{0,1:T(8,128)(2,1)} %bitcast.11), channel_id=1, source_target_pairs={{0,8},{8,0},{16,24},{24,16},{1,9},{9,1},{17,25},{25,17},{2,10},{10... | collective-permute-start | bytes 737288 | tf_op jit(solution)/shard_map/ppermute | solution.py:342
  47.1 6.6 %collective-permute-start.11 = (bf16[128,960]{0,1:T(8,128)(2,1)}, bf16[128,960]{0,1:T(8,128)(2,1)S(1)}, u32[]{:S(2)}, u32[]{:S(2)}) collective-permute-start(bf16[128,960]{0,1:T(8,128)(2,1)} %collective-permute-done.7), channel_id=1, source_target_pairs={{0,8},{8,0},{16,24},{24,16},{1,9},{9,1},{17,25},{25,17},{2,10},{10... | collective-permute-start | bytes 737288 | tf_op jit(solution)/shard_map/ppermute | solution.py:342
  47.4 15.8 %collective-permute-start.12 = (bf16[480,640]{1,0:T(8,128)(2,1)S(1)}, bf16[480,640]{1,0:T(8,128)(2,1)S(1)}, u32[]{:S(2)}, u32[]{:S(2)}) collective-permute-start(bf16[480,640]{1,0:T(8,128)(2,1)S(1)} %copy-done.41), channel_id=1, source_target_pairs={{0,24},{24,0},{8,16},{16,8},{1,25},{25,1},{9,17},{17,9},{2,26},{26... | collective-permute-start | bytes 1843208 | tf_op jit(solution)/shard_map/ppermute | solution.py:345
  53.2 35.2 %copy-start.12 = (f32[256,960]{0,1:T(8,128)}, f32[256,960]{0,1:T(8,128)S(1)}, u32[]{:S(2)}) copy-start(f32[256,960]{0,1:T(8,128)S(1)} %get-tuple-element.248) | copy-start | bytes 2949124
  53.4 9.7 %copy-start.35 = (bf16[240,640]{1,0:T(8,128)(2,1)S(1)}, bf16[240,640]{1,0:T(8,128)(2,1)}, u32[]{:S(2)}) copy-start(bf16[240,640]{1,0:T(8,128)(2,1)} %get-tuple-element.113) | copy-start | bytes 921604
  53.5 10.3 %collective-permute-start.9 = (bf16[256,960]{0,1:T(8,128)(2,1)S(1)}, bf16[256,960]{0,1:T(8,128)(2,1)S(1)}, u32[]{:S(2)}, u32[]{:S(2)}) collective-permute-start(bf16[256,960]{0,1:T(8,128)(2,1)S(1)} %multiply_convert_fusion.3), channel_id=1, source_target_pairs={{0,8},{8,0},{16,24},{24,16},{1,9},{9,1},{17,25},{25,17},{2,10},{10... | collective-permute-start | bytes 1474568 | tf_op jit(solution)/shard_map/ppermute | solution.py:342
  63.3 3.2 %collective-permute-start.13 = (bf16[480,640]{1,0:T(8,128)(2,1)S(1)}, bf16[480,640]{1,0:T(8,128)(2,1)S(1)}, u32[]{:S(2)}, u32[]{:S(2)}) collective-permute-start(bf16[480,640]{1,0:T(8,128)(2,1)S(1)} %pad_maximum_fusion.6), channel_id=1, source_target_pairs={{0,8},{8,0},{16,24},{24,16},{1,9},{9,1},{17,25},{25,17},{2,10},{10... | collective-permute-start | bytes 1843208 | tf_op jit(solution)/shard_map/ppermute | solution.py:342
  69.1 4.1 %copy-start.39 = (bf16[512,640]{1,0:T(8,128)(2,1)}, bf16[512,640]{1,0:T(8,128)(2,1)S(1)}, u32[]{:S(2)}) copy-start(bf16[512,640]{1,0:T(8,128)(2,1)S(1)} %get-tuple-element.151) | copy-start | bytes 1966084
  71.1 3.0 %collective-permute-start.14 = (bf16[256,960]{0,1:T(8,128)(2,1)S(1)}, bf16[256,960]{0,1:T(8,128)(2,1)S(1)}, u32[]{:S(2)}, u32[]{:S(2)}) collective-permute-start(bf16[256,960]{0,1:T(8,128)(2,1)S(1)} %constant_dynamic-slice_fusion.16), channel_id=1, source_target_pairs={{0,8},{8,0},{16,24},{24,16},{1,9},{9,1},{17,25},{25,17},{2,10},{10... | collective-permute-start | bytes 1474568 | tf_op jit(solution)/shard_map/ppermute | solution.py:342
  72.2 3.8 %copy-start.16 = (f32[960,640]{1,0:T(8,128)}, f32[960,640]{1,0:T(8,128)S(1)}, u32[]{:S(2)}) copy-start(f32[960,640]{1,0:T(8,128)S(1)} %fusion.66) | copy-start | bytes 7372804
  73.1 3.9 %copy-start.18 = (f32[960,640]{1,0:T(8,128)}, f32[960,640]{1,0:T(8,128)S(1)}, u32[]{:S(2)}) copy-start(f32[960,640]{1,0:T(8,128)S(1)} %fusion.67) | copy-start | bytes 7372804
  74.1 5.2 %copy-start.14 = (f32[960,640]{1,0:T(8,128)}, f32[960,640]{1,0:T(8,128)S(1)}, u32[]{:S(2)}) copy-start(f32[960,640]{1,0:T(8,128)S(1)} %fusion.68) | copy-start | bytes 7372804
  74.2 13.7 %collective-permute-start.15 = (bf16[256,960]{0,1:T(8,128)(2,1)S(1)}, bf16[256,960]{0,1:T(8,128)(2,1)S(1)}, u32[]{:S(2)}, u32[]{:S(2)}) collective-permute-start(bf16[256,960]{0,1:T(8,128)(2,1)S(1)} %fusion.10), channel_id=1, source_target_pairs={{0,24},{24,0},{8,16},{16,8},{1,25},{25,1},{9,17},{17,9},{2,26},{26... | collective-permute-start | bytes 1474568 | tf_op jit(solution)/shard_map/ppermute | solution.py:345
  75.8 27.2 %collective-permute-start.18 = (bf16[960,256]{1,0:T(8,128)(2,1)}, bf16[960,256]{1,0:T(8,128)(2,1)}, u32[]{:S(2)}, u32[]{:S(2)}) collective-permute-start(bf16[960,256]{1,0:T(8,128)(2,1)} %get-tuple-element.146.o_ref), channel_id=1, source_target_pairs={{0,8},{8,0},{16,24},{24,16},{1,9},{9,1},{17,25},{25,17},{2,10},{10... | collective-permute-start | bytes 1474568 | tf_op jit(solution)/shard_map/ppermute | solution.py:342
  76.8 21.4 %collective-permute-start.19 = (bf16[2,2,120,640]{3,2,0,1:T(8,128)(2,1)}, bf16[2,2,120,640]{3,2,0,1:T(8,128)(2,1)}, u32[]{:S(2)}, u32[]{:S(2)}) collective-permute-start(bf16[2,2,120,640]{3,2,0,1:T(8,128)(2,1)} %fusion.16), channel_id=1, source_target_pairs={{0,1},{1,0},{2,3},{3,2},{4,5},{5,4},{6,7},{7,6},{8,9},{9,8},{10,11... | collective-permute-start | bytes 1843208 | tf_op jit(solution)/shard_map/ppermute | solution.py:252
  78.0 20.5 %collective-permute-start.20 = (bf16[2,2,120,640]{3,2,0,1:T(8,128)(2,1)}, bf16[2,2,120,640]{3,2,0,1:T(8,128)(2,1)}, u32[]{:S(2)}, u32[]{:S(2)}) collective-permute-start(bf16[2,2,120,640]{3,2,0,1:T(8,128)(2,1)} %fusion.17), channel_id=1, source_target_pairs={{0,2},{1,3},{2,0},{3,1},{4,6},{5,7},{6,4},{7,5},{8,10},{9,11},{10,... | collective-permute-start | bytes 1843208 | tf_op jit(solution)/shard_map/ppermute | solution.py:252
  80.2 36.8 %collective-permute-start.27 = (bf16[2,240,640]{2,1,0:T(8,128)(2,1)}, bf16[2,240,640]{2,1,0:T(8,128)(2,1)}, u32[]{:S(2)}, u32[]{:S(2)}) collective-permute-start(bf16[2,240,640]{2,1,0:T(8,128)(2,1)} %fusion.18), channel_id=1, source_target_pairs={{0,1},{1,0},{2,3},{3,2},{4,5},{5,4},{6,7},{7,6},{8,9},{9,8},{10,11... | collective-permute-start | bytes 1843208 | tf_op jit(solution)/shard_map/ppermute | solution.py:252
  90.9 7.8 %copy-start.17 = (f32[960,640]{1,0:T(8,128)S(1)}, f32[960,640]{1,0:T(8,128)}, u32[]{:S(2)}) copy-start(f32[960,640]{1,0:T(8,128)} %copy-done.16) | copy-start | bytes 7372804
  91.0 13.3 %collective-permute-start.21 = (bf16[256,240]{0,1:T(8,128)(2,1)S(1)}, bf16[256,240]{0,1:T(8,128)(2,1)S(1)}, u32[]{:S(2)}, u32[]{:S(2)}) collective-permute-start(bf16[256,240]{0,1:T(8,128)(2,1)S(1)} %constant_dynamic-slice_fusion.10), channel_id=1, source_target_pairs={{0,8},{8,0},{16,24},{24,16},{1,9},{9,1},{17,25},{25,17},{2,10},{10... | collective-permute-start | bytes 368648 | tf_op jit(solution)/shard_map/ppermute | solution.py:342
  98.2 10.0 %collective-permute-start.16 = (bf16[240,256]{1,0:T(8,128)(2,1)S(1)}, bf16[240,256]{1,0:T(8,128)(2,1)S(1)}, u32[]{:S(2)}, u32[]{:S(2)}) collective-permute-start(bf16[240,256]{1,0:T(8,128)(2,1)S(1)} %constant_dynamic-slice_fusion.15), channel_id=1, source_target_pairs={{0,8},{8,0},{16,24},{24,16},{1,9},{9,1},{17,25},{25,17},{2,10},{10... | collective-permute-start | bytes 368648 | tf_op jit(solution)/shard_map/ppermute | solution.py:342
  98.5 11.5 %collective-permute-start.17 = (bf16[640,512]{1,0:T(8,128)(2,1)S(1)}, bf16[640,512]{1,0:T(8,128)(2,1)S(1)}, u32[]{:S(2)}, u32[]{:S(2)}) collective-permute-start(bf16[640,512]{1,0:T(8,128)(2,1)S(1)} %get-tuple-element.137), channel_id=1, source_target_pairs={{0,8},{8,0},{16,24},{24,16},{1,9},{9,1},{17,25},{25,17},{2,10},{10... | collective-permute-start | bytes 1966088 | tf_op jit(solution)/shard_map/ppermute | solution.py:342
  102.2 5.1 %copy-start.28 = (f32[2,2,120,640]{3,2,0,1:T(8,128)}, f32[2,2,120,640]{3,2,0,1:T(8,128)S(1)}, u32[]{:S(2)}) copy-start(f32[2,2,120,640]{3,2,0,1:T(8,128)S(1)} %bitcast_add_fusion.2) | copy-start | bytes 3686404
  103.0 21.3 %collective-permute-start.26 = (bf16[2,120,640]{2,1,0:T(8,128)(2,1)}, bf16[2,120,640]{2,1,0:T(8,128)(2,1)S(1)}, u32[]{:S(2)}, u32[]{:S(2)}) collective-permute-start(bf16[2,120,640]{2,1,0:T(8,128)(2,1)} %fusion.28), channel_id=1, source_target_pairs={{0,1},{1,0},{2,3},{3,2},{4,5},{5,4},{6,7},{7,6},{8,9},{9,8},{10,11... | collective-permute-start | bytes 921608 | tf_op jit(solution)/shard_map/ppermute | solution.py:252
  104.3 11.8 %collective-permute-start.23 = (bf16[2,120,640]{2,1,0:T(8,128)(2,1)}, bf16[2,120,640]{2,1,0:T(8,128)(2,1)}, u32[]{:S(2)}, u32[]{:S(2)}) collective-permute-start(bf16[2,120,640]{2,1,0:T(8,128)(2,1)} %fusion.27), channel_id=1, source_target_pairs={{0,2},{1,3},{2,0},{3,1},{4,6},{5,7},{6,4},{7,5},{8,10},{9,11},{10,... | collective-permute-start | bytes 921608 | tf_op jit(solution)/shard_map/ppermute | solution.py:252
  108.2 17.1 %collective-permute-start.25 = (bf16[2,2,120,256]{3,2,0,1:T(8,128)(2,1)}, bf16[2,2,120,256]{3,2,0,1:T(8,128)(2,1)}, u32[]{:S(2)}, u32[]{:S(2)}) collective-permute-start(bf16[2,2,120,256]{3,2,0,1:T(8,128)(2,1)} %fusion.31), channel_id=1, source_target_pairs={{0,1},{1,0},{2,3},{3,2},{4,5},{5,4},{6,7},{7,6},{8,9},{9,8},{10,11... | collective-permute-start | bytes 737288 | tf_op jit(solution)/shard_map/ppermute | solution.py:252
  114.5 1.9 %collective-permute-start.22 = (f32[2,240]{1,0:T(2,128)S(1)}, f32[2,240]{1,0:T(2,128)S(1)}, u32[]{:S(2)}, u32[]{:S(2)}) collective-permute-start(f32[2,240]{1,0:T(2,128)S(1)} %fusion.51), channel_id=1, source_target_pairs={{0,8},{8,0},{16,24},{24,16},{1,9},{9,1},{17,25},{25,17},{2,10},{10... | collective-permute-start | bytes 5768 | tf_op jit(solution)/shard_map/ppermute | solution.py:342
  116.7 12.9 %collective-permute-start.31 = (bf16[2,2,248,256]{3,2,0,1:T(8,128)(2,1)S(1)}, bf16[2,2,248,256]{3,2,0,1:T(8,128)(2,1)S(1)}, u32[]{:S(2)}, u32[]{:S(2)}) collective-permute-start(bf16[2,2,248,256]{3,2,0,1:T(8,128)(2,1)S(1)} %fusion.21), channel_id=1, source_target_pairs={{0,1},{1,0},{2,3},{3,2},{4,5},{5,4},{6,7},{7,6},{8,9},{9,8},{10,11... | collective-permute-start | bytes 1523720 | tf_op jit(solution)/shard_map/ppermute | solution.py:252
  119.4 4.0 %copy-start.40 = (bf16[512,640]{1,0:T(8,128)(2,1)S(1)}, bf16[512,640]{1,0:T(8,128)(2,1)}, u32[]{:S(2)}) copy-start(bf16[512,640]{1,0:T(8,128)(2,1)} %copy-done.39) | copy-start | bytes 1966084
  119.4 4.0 %copy-start.43 = (bf16[240,640]{1,0:T(8,128)(2,1)S(1)}, bf16[240,640]{1,0:T(8,128)(2,1)}, u32[]{:S(2)}) copy-start(bf16[240,640]{1,0:T(8,128)(2,1)} %copy-done.42) | copy-start | bytes 921604
  119.4 4.0 %copy-start.45 = (bf16[240,640]{1,0:T(8,128)(2,1)S(1)}, bf16[240,640]{1,0:T(8,128)(2,1)}, u32[]{:S(2)}) copy-start(bf16[240,640]{1,0:T(8,128)(2,1)} %copy-done.44) | copy-start | bytes 921604
  119.4 3.9 %copy-start.47 = (bf16[240,640]{1,0:T(8,128)(2,1)S(1)}, bf16[240,640]{1,0:T(8,128)(2,1)}, u32[]{:S(2)}) copy-start(bf16[240,640]{1,0:T(8,128)(2,1)} %copy-done.46) | copy-start | bytes 921604
  119.4 3.9 %copy-start.49 = (bf16[240,640]{1,0:T(8,128)(2,1)S(1)}, bf16[240,640]{1,0:T(8,128)(2,1)}, u32[]{:S(2)}) copy-start(bf16[240,640]{1,0:T(8,128)(2,1)} %copy-done.48) | copy-start | bytes 921604
  119.5 13.8 %collective-permute-start.30 = (bf16[240,640]{1,0:T(8,128)(2,1)S(1)}, bf16[240,640]{1,0:T(8,128)(2,1)S(1)}, u32[]{:S(2)}, u32[]{:S(2)}) collective-permute-start(bf16[240,640]{1,0:T(8,128)(2,1)S(1)} %fusion.29), channel_id=1, source_target_pairs={{0,2},{1,3},{2,0},{3,1},{4,6},{5,7},{6,4},{7,5},{8,10},{9,11},{10,... | collective-permute-start | bytes 921608 | tf_op jit(solution)/shard_map/ppermute | solution.py:252
  121.0 4.2 %copy-start.29 = (f32[2,2,120,640]{3,2,0,1:T(8,128)S(1)}, f32[2,2,120,640]{3,2,0,1:T(8,128)}, u32[]{:S(2)}) copy-start(f32[2,2,120,640]{3,2,0,1:T(8,128)} %copy-done.28) | copy-start | bytes 3686404
  121.0 30.7 %collective-permute-start.34 = (bf16[120,640]{1,0:T(8,128)(2,1)S(1)}, bf16[120,640]{1,0:T(8,128)(2,1)S(1)}, u32[]{:S(2)}, u32[]{:S(2)}) collective-permute-start(bf16[120,640]{1,0:T(8,128)(2,1)S(1)} %fusion.44), channel_id=1, source_target_pairs={{0,4},{1,5},{2,6},{3,7},{4,0},{5,1},{6,2},{7,3},{8,12},{9,13},{10,... | collective-permute-start | bytes 460808 | tf_op jit(solution)/shard_map/ppermute | solution.py:252
  124.4 2.3 %collective-permute-start.24 = (bf16[256,960]{0,1:T(8,128)(2,1)S(1)}, bf16[256,960]{0,1:T(8,128)(2,1)S(1)}, u32[]{:S(2)}, u32[]{:S(2)}) collective-permute-start(bf16[256,960]{0,1:T(8,128)(2,1)S(1)} %constant_dynamic-slice_fusion.3), channel_id=1, source_target_pairs={{0,8},{8,0},{16,24},{24,16},{1,9},{9,1},{17,25},{25,17},{2,10},{10... | collective-permute-start | bytes 1474568 | tf_op jit(solution)/shard_map/ppermute | solution.py:342
  125.3 25.6 %collective-permute-start.36 = (bf16[120,640]{1,0:T(8,128)(2,1)S(1)}, bf16[120,640]{1,0:T(8,128)(2,1)S(1)}, u32[]{:S(2)}, u32[]{:S(2)}) collective-permute-start(bf16[120,640]{1,0:T(8,128)(2,1)S(1)} %fusion.45), channel_id=1, source_target_pairs={{0,4},{1,5},{2,6},{3,7},{4,0},{5,1},{6,2},{7,3},{8,12},{9,13},{10,... | collective-permute-start | bytes 460808 | tf_op jit(solution)/shard_map/ppermute | solution.py:252
  126.7 9.2 %collective-permute-start.29 = (bf16[2,120,256]{2,1,0:T(8,128)(2,1)S(1)}, bf16[2,120,256]{2,1,0:T(8,128)(2,1)S(1)}, u32[]{:S(2)}, u32[]{:S(2)}) collective-permute-start(bf16[2,120,256]{2,1,0:T(8,128)(2,1)S(1)} %fusion.47), channel_id=1, source_target_pairs={{0,2},{1,3},{2,0},{3,1},{4,6},{5,7},{6,4},{7,5},{8,10},{9,11},{10,... | collective-permute-start | bytes 368648 | tf_op jit(solution)/shard_map/ppermute | solution.py:252
  129.6 10.1 %collective-permute-start.28 = (bf16[128,960]{0,1:T(8,128)(2,1)S(1)}, bf16[128,960]{0,1:T(8,128)(2,1)S(1)}, u32[]{:S(2)}, u32[]{:S(2)}) collective-permute-start(bf16[128,960]{0,1:T(8,128)(2,1)S(1)} %dynamic-slice_convert_fusion.4), channel_id=1, source_target_pairs={{0,24},{24,0},{8,16},{16,8},{1,25},{25,1},{9,17},{17,9},{2,26},{26... | collective-permute-start | bytes 737288 | tf_op jit(solution)/shard_map/ppermute | solution.py:345
  132.1 8.9 %copy-start.13 = (f32[256,960]{0,1:T(8,128)S(1)}, f32[256,960]{0,1:T(8,128)}, u32[]{:S(2)}) copy-start(f32[256,960]{0,1:T(8,128)} %copy-done.12) | copy-start | bytes 2949124
  133.2 13.7 %collective-permute-start.32 = (bf16[2,248,256]{2,1,0:T(8,128)(2,1)S(1)}, bf16[2,248,256]{2,1,0:T(8,128)(2,1)S(1)}, u32[]{:S(2)}, u32[]{:S(2)}) collective-permute-start(bf16[2,248,256]{2,1,0:T(8,128)(2,1)S(1)} %fusion.30), channel_id=1, source_target_pairs={{0,2},{1,3},{2,0},{3,1},{4,6},{5,7},{6,4},{7,5},{8,10},{9,11},{10,... | collective-permute-start | bytes 761864 | tf_op jit(solution)/shard_map/ppermute | solution.py:252
  136.0 11.2 %collective-permute-start.35 = (bf16[240,320]{1,0:T(8,128)(2,1)S(1)}, bf16[240,320]{1,0:T(8,128)(2,1)S(1)}, u32[]{:S(2)}, u32[]{:S(2)}) collective-permute-start(bf16[240,320]{1,0:T(8,128)(2,1)S(1)} %select_convert_fusion), channel_id=1, source_target_pairs={{0,4},{1,5},{2,6},{3,7},{4,0},{5,1},{6,2},{7,3},{8,12},{9,13},{10,... | collective-permute-start | bytes 460808 | tf_op jit(solution)/shard_map/ppermute | solution.py:265
  139.8 27.5 %collective-permute-start.38 = (bf16[120,256]{1,0:T(8,128)(2,1)S(1)}, bf16[120,256]{1,0:T(8,128)(2,1)S(1)}, u32[]{:S(2)}, u32[]{:S(2)}) collective-permute-start(bf16[120,256]{1,0:T(8,128)(2,1)S(1)} %fusion.48), channel_id=1, source_target_pairs={{0,4},{1,5},{2,6},{3,7},{4,0},{5,1},{6,2},{7,3},{8,12},{9,13},{10,... | collective-permute-start | bytes 184328 | tf_op jit(solution)/shard_map/ppermute | solution.py:252
  147.0 18.0 %collective-permute-start.33 = (bf16[248,256]{1,0:T(8,128)(2,1)S(1)}, bf16[248,256]{1,0:T(8,128)(2,1)S(1)}, u32[]{:S(2)}, u32[]{:S(2)}) collective-permute-start(bf16[248,256]{1,0:T(8,128)(2,1)S(1)} %fusion.46), channel_id=1, source_target_pairs={{0,4},{1,5},{2,6},{3,7},{4,0},{5,1},{6,2},{7,3},{8,12},{9,13},{10,... | collective-permute-start | bytes 380936 | tf_op jit(solution)/shard_map/ppermute | solution.py:252
  147.3 17.7 %collective-permute-start.37 = (bf16[240,320]{1,0:T(8,128)(2,1)S(1)}, bf16[240,320]{1,0:T(8,128)(2,1)S(1)}, u32[]{:S(2)}, u32[]{:S(2)}) collective-permute-start(bf16[240,320]{1,0:T(8,128)(2,1)S(1)} %add_convert_fusion.2), channel_id=1, source_target_pairs={{0,0},{8,2},{16,4},{24,6},{1,8},{9,10},{17,12},{25,14},{2,16},{10,... | collective-permute-start | bytes 460808 | tf_op jit(solution)/shard_map/ppermute | solution.py:592
  150.9 18.4 %copy-start.1 = (bf16[960,640]{1,0:T(8,128)(2,1)S(1)}, bf16[960,640]{1,0:T(8,128)(2,1)}, u32[]{:S(2)}) copy-start(bf16[960,640]{1,0:T(8,128)(2,1)} %param.18) | copy-start | bytes 3686404
  (27 other events, 52.6 us)

commit v3 on v2

--- a/solution.py
+++ b/solution.py
@@ -514,9 +514,6 @@
     def full_lanes(values):
         return jnp.pad(values, ((0, 0), (0, 0), (0, -values.shape[2] % 128)))
 
-    o_all = jnp.concatenate(sets(*turn.hold(o_t, o_beside)), axis=1)
-    out_sum = RepSum(row_major(full_lanes(by_rep(dot_nn(o_all, columns_of(d_x2_low))))), (0, 1))
-    turn.mark(out_sum.sent)
     d_kv, d_kv_beside = turn.hold(d_kv, d_kv_beside)
     d_kv = (d_kv + d_kv_beside.astype(jnp.float32)).astype(bf16)
 
@@ -551,6 +548,9 @@
     attn_sum = RepSum(row_major(bundle), (0, 1))
     turn.mark(attn_sum.sent)
 
+    o_all = jnp.concatenate(sets(*turn.hold(o_t, o_beside)), axis=1)
+    out_sum = RepSum(row_major(full_lanes(by_rep(dot_nn(o_all, columns_of(d_x2_low))))), (0, 1))
+    turn.mark(out_sum.sent)
     out_part = dot_nt(turn.hold(hidden), down_rows_t).astype(bf16)
     out_beside = core_swap(lax.dynamic_slice_in_dim(out_part, beside_start, half_rows, 0))
     down_held = joined((down_pair[0], turn.hold(down_pair[1])))

time: 172 us -> 172 us (level)
  starting transfers between devices: 33.3 us -> 36.2 us
  other arithmetic: 23.4 us -> 21.1 us
  matrix products: 17.1 us -> 19 us
    ppermute x1, waiting for transfers between devices: 12.6 us -> 10.5 us  [per_device(): g_down = lax.ppermute(down_sent, ('grp', 'rep'), homes)]
    ppermute x14, starting transfers between devices: 11.1 us -> 13.2 us  [swap_over_rep(): came = lax.ppermute(away, 'rep', [(i, i ^ 1 << bit) for i in range(count)])]
    dot_general x5, matrix products: 7.22 us -> 9.15 us  [dot_any(): lax.dot_general(left, right, (((left_dim,), (right_dim,)), ((), ())), pre...]
    unnamed x108 -> x110, local copies, waits for them, and re-layouts: 10.6 us -> 11 us
where the time goes in v3:
time: 172 us; the launch traced here: 170 us
  waiting for transfers between devices  56 us (33%)
  starting transfers between devices  36.2 us (21%)
  other arithmetic  21.1 us (12%)
  local copies, waits for them, and re-layouts  19.4 us (11%)
  matrix products  19 us (11%)
  Pallas kernels  16.4 us (10%)
  between operations  1.82 us (1%)
    ppermute x7, waiting for transfers between devices, chip_cross(): return lax.ppermute(values, 'grp', CROSS_SWAP)  36.5 us
    pallas_call x2, Pallas kernels, whole(): pl.pallas_call(kernel, out_shape=outs, in_specs=[pl.BlockSpec(memory_spac...  16.4 us
    ppermute x14, starting transfers between devices, swap_over_rep(): came = lax.ppermute(away, 'rep', [(i, i ^ 1 << bit) for i in range(count)])  13.2 us
    unnamed x110, local copies, waits for them, and re-layouts  11 us
    ppermute x1, waiting for transfers between devices, per_device(): g_down = lax.ppermute(down_sent, ('grp', 'rep'), homes)  10.5 us
    ppermute x7, starting transfers between devices, chip_cross(): return lax.ppermute(values, 'grp', CROSS_SWAP)  9.4 us
    dot_general x5, matrix products, dot_any(): lax.dot_general(left, right, (((left_dim,), (right_dim,)), ((), ())), pre...  9.15 us
    ppermute x14, waiting for transfers between devices, swap_over_rep(): came = lax.ppermute(away, 'rep', [(i, i ^ 1 << bit) for i in range(count)])  8.66 us
  transfers between devices with their start and end apart: 39, of which 11 were waited for; matrix products, arithmetic and copies ran while one was open for 28% of the time, Pallas kernels for 10%

profile of v3, /device:TPU:5, one launch (start us, length us, event | category | flops | bytes accessed | tf_op | source)
XLA Modules:
  0.0 169.9 jit_solution(13076559237829058222)
XLA Ops:
  0.7 1.8 %collective-permute-start = (bf16[128,960]{0,1:T(8,128)(2,1)}, bf16[128,960]{0,1:T(8,128)(2,1)S(1)}, u32[]{:S(2)}, u32[]{:S(2)}) collective-permute-start(bf16[128,960]{0,1:T(8,128)(2,1)} %bitcast.128), channel_id=1, source_target_pairs={{0,24},{24,0},{8,16},{16,8},{1,25},{25,1},{9,17},{17,9},{2,26},{26... | collective-permute-start | bytes 737288 | tf_op jit(solution)/shard_map/ppermute | solution.py:345
  2.5 1.2 copy.45
  3.7 1.1 fusion.11.own_ref
  5.6 4.1 %collective-permute-done = bf16[128,960]{0,1:T(8,128)(2,1)S(1)} collective-permute-done((bf16[128,960]{0,1:T(8,128)(2,1)}, bf16[128,960]{0,1:T(8,128)(2,1)S(1)}, u32[]{:S(2)}, u32[]{:S(2)}) %collective-permute-start) | collective-permute-done | bytes 245792 | tf_op jit(solution)/shard_map/ppermute | solution.py:345
  10.0 2.2 %dynamic-slice_bitcast_fusion.1 = (bf16[240,640]{1,0:T(8,128)(2,1)S(1)}, bf16[240,640]{1,0:T(8,128)(2,1)S(1)}, bf16[240,640]{1,0:T(8,128)(2,1)}, bf16[240,640]{1,0:T(8,128)(2,1)}) fusion(bf16[2560,240]{0,1:T(8,128)(2,1)} %param.20, s32[]{:T(128)S(6)} %select_n.368, s32[]{:T(128)S(6)} %select_n.369, s32[]{:T(128)S(6)} %select_n.367, s32[]{:T(128)S(6)} %select_n.366), kind=kLoop, calls=%fused_computation.110 | loop fusion | bytes 2457616 | tf_op jit(solution)/shard_map/dynamic_slice | solution.py:393
  12.2 0.9 pad_maximum_fusion.5
  13.8 13.7 %collective-permute-done.3.cross_ref = bf16[408,960]{1,0:T(8,128)(2,1)} collective-permute-done((bf16[408,960]{1,0:T(8,128)(2,1)S(1)}, bf16[408,960]{1,0:T(8,128)(2,1)}, u32[]{:S(2)}, u32[]{:S(2)}) %collective-permute-start.3) | collective-permute-done | bytes 783392 | tf_op jit(solution)/shard_map/ppermute | solution.py:345
  27.8 1.3 collective-permute-start.6
  29.7 1.1 fusion.26
  31.0 1.1 copy-done.3
  32.1 9.5 %shard_map.186 = (bf16[960,512]{1,0:T(8,128)(2,1)S(1)}, bf16[1600,960]{1,0:T(8,128)(2,1)S(1)}, f32[8,960]{1,0:T(8,128)S(1)}, bf16[960,256]{1,0:T(8,128)(2,1)S(1)...) custom-call(s32[2]{0:T(128)S(1)} %pad_add_fusion.me_ref, ...), custom_call_target="tpu_custom_call" | custom-call | flops 1000000 | bytes 1000000 | tf_op jit(solution)/shard_map/pallas_call | solution.py:212
  41.6 1.7 %copy-done.10 = bf16[1600,960]{1,0:T(8,128)(2,1)} copy-done((bf16[1600,960]{1,0:T(8,128)(2,1)}, bf16[1600,960]{1,0:T(8,128)(2,1)S(1)}, u32[]{:S(2)}) %copy-start.10) | copy-done | bytes 3072024
  43.3 3.1 %collective-permute-done.7 = bf16[128,960]{0,1:T(8,128)(2,1)} collective-permute-done((bf16[128,960]{0,1:T(8,128)(2,1)}, bf16[128,960]{0,1:T(8,128)(2,1)}, u32[]{:S(2)}, u32[]{:S(2)}) %collective-permute-start.7) | collective-permute-done | bytes 245792 | tf_op jit(solution)/shard_map/ppermute | solution.py:345
  47.4 1.4 collective-permute-start.12
  48.8 1.4 select_select_fusion.3
  50.3 3.3 %multiply_reduce_fusion.2 = (f32[256]{0:T(256)S(1)}, f32[256,960]{0,1:T(8,128)S(1)}) fusion(bf16[960,256]{1,0:T(8,128)(2,1)} %get-tuple-element.150.o_ref, bf16[240,960]{0,1:T(8,128)(2,1)S(1)} %get-tuple-element.212, bf16[240,960]{0,1:T(8,128)(2,1)S(1)} %get-tuple-element.213, bf16[240,960]{0,1:T(8,128)(2,1)S(1)} %get-tuple-element.214, ...), kind=kOutput, calls=%fused_computation.48 | convolution fusion | flops 480952064 | bytes 3810304 | tf_op jit(solution)/shard_map/dot_general | solution.py:56
  54.2 1.2 select_select_fusion.11
  55.5 7.7 %collective-permute-done.12 = bf16[480,640]{1,0:T(8,128)(2,1)S(1)} collective-permute-done((bf16[480,640]{1,0:T(8,128)(2,1)S(1)}, bf16[480,640]{1,0:T(8,128)(2,1)S(1)}, u32[]{:S(2)}, u32[]{:S(2)}) %collective-permute-start.12) | collective-permute-done | bytes 614432 | tf_op jit(solution)/shard_map/ppermute | solution.py:345
  64.0 1.2 fusion.61
  65.3 1.0 fusion.60
  66.4 0.9 copy-done.34
  67.5 1.5 multiply_convert_fusion
  69.0 1.0 fusion.65
  70.0 1.0 add_convert_fusion
  71.2 0.9 fusion.66
  72.2 0.9 fusion.67
  73.1 0.9 fusion.68
  74.2 1.6 collective-permute-start.16
  75.9 0.9 fusion.16
  77.1 0.9 fusion.17
  77.9 1.3 collective-permute-start.20
  79.2 0.9 fusion.18
  80.1 1.2 collective-permute-start.27
  81.4 6.5 %collective-permute-done.16 = bf16[256,960]{0,1:T(8,128)(2,1)S(1)} collective-permute-done((bf16[256,960]{0,1:T(8,128)(2,1)S(1)}, bf16[256,960]{0,1:T(8,128)(2,1)S(1)}, u32[]{:S(2)}, u32[]{:S(2)}) %collective-permute-start.16) | collective-permute-done | bytes 491552 | tf_op jit(solution)/shard_map/ppermute | solution.py:345
  88.4 1.4 fusion.62
  90.0 2.5 %convolution_convert_fusion.1.do_ref = bf16[960,256]{1,0:T(8,128)(2,1)S(1)} fusion(bf16[256,960]{0,1:T(8,128)(2,1)S(1)} %get-tuple-element.206, bf16[240,960]{0,1:T(8,128)(2,1)} %copy-done.40, bf16[240,960]{0,1:T(8,128)(2,1)} %copy-done.41, bf16[240,960]{0,1:T(8,128)(2,1)} %copy-done.42, bf16[240,960]{0,1:T(8,128)(2,1)} %copy-done.39), kind=kOutput, calls=%fused_computation.21 | convolution fusion | flops 479477760 | bytes 2826240 | tf_op jit(solution)/shard_map/dot_general | solution.py:56
  92.5 6.9 %shard_map.187 = (bf16[960,256]{1,0:T(8,128)(2,1)S(1)}, f32[640,512]{1,0:T(8,128)S(1)}, bf16[640,512]{1,0:T(8,128)(2,1)S(1)}) custom-call(s32[2]{0:T(128)S(1)} %pad_add_fusion.me_ref, bf16[960,256]{1,0:T(8,128)(2,1)S(1)} %convolution_convert_fusion.1.do_ref, bf16[960,256]{1,0:T(8,128)(2,1)} %get-tuple-element.150.o_ref, bf16[960,256]{1,0:T(8,128)(2,1)S(1)} %copy-done.5, ...), custom_call_target="tpu_custom_call" | custom-call | flops 1000000 | bytes 1000000 | tf_op jit(solution)/shard_map/pallas_call | solution.py:212
  100.3 1.0 copy-done.30
  102.1 1.2 bitcast_add_fusion.2
  103.3 1.4 collective-permute-start.22
  106.8 1.5 copy-done.11
  108.3 2.5 %fusion.5 = (f32[960]{0:T(1024)S(1)}, f32[256,960]{0,1:T(8,128)}) fusion(f32[256]{0:T(256)S(1)} %add_rsqrt_fusion, bf16[128,960]{0,1:T(8,128)(2,1)S(1)} %copy-done.27, bf16[128,960]{0,1:T(8,128)(2,1)S(1)} %copy-done.24, bf16[1600,960]{1,0:T(8,128)(2,1)S(1)} %copy-done.11, bf16[640,256]{1,0:T(8,128)(2,1)S(1)} %slice_select_fusion, ...), kind=kOutput, calls=%fused_computation.33 | convolution fusion | flops 789789760 | bytes 5370624 | tf_op jit(solution)/shard_map/dot_general | solution.py:56
  110.9 1.1 collective-permute-start.21
  113.1 1.2 broadcast_select_fusion.1
  114.9 1.3 collective-permute-start.25
  116.5 1.0 convolution_convert_fusion
  117.5 1.2 collective-permute-start.24
  118.8 1.2 bitcast_add_fusion
  120.0 1.4 collective-permute-start.30
  121.4 1.0 bitcast_add_fusion.5
  122.5 2.4 %collective-permute-start.34 = (bf16[120,640]{1,0:T(8,128)(2,1)S(1)}, bf16[120,640]{1,0:T(8,128)(2,1)S(1)}, u32[]{:S(2)}, u32[]{:S(2)}) collective-permute-start(bf16[120,640]{1,0:T(8,128)(2,1)S(1)} %fusion.44), channel_id=1, source_target_pairs={{0,4},{1,5},{2,6},{3,7},{4,0},{5,1},{6,2},{7,3},{8,12},{9,13},{10,... | collective-permute-start | bytes 460808 | tf_op jit(solution)/shard_map/ppermute | solution.py:252
  124.9 1.0 bitcast_add_fusion.6
  127.6 1.0 fusion.25
  128.6 4.2 %collective-permute-done.31 = bf16[2,2,248,256]{3,2,0,1:T(8,128)(2,1)S(1)} collective-permute-done((bf16[2,2,248,256]{3,2,0,1:T(8,128)(2,1)S(1)}, bf16[2,2,248,256]{3,2,0,1:T(8,128)(2,1)S(1)}, u32[]{:S(2)}, u32[]{:S(2)}) %collective-permute-start.31) | collective-permute-done | bytes 507936 | tf_op jit(solution)/shard_map/ppermute | solution.py:252
  132.8 2.6 %collective-permute-start.28 = (bf16[128,960]{0,1:T(8,128)(2,1)S(1)}, bf16[128,960]{0,1:T(8,128)(2,1)S(1)}, u32[]{:S(2)}, u32[]{:S(2)}) collective-permute-start(bf16[128,960]{0,1:T(8,128)(2,1)S(1)} %dynamic-slice_convert_fusion.4), channel_id=1, source_target_pairs={{0,24},{24,0},{8,16},{16,8},{1,25},{25,1},{9,17},{17,9},{2,26},{26... | collective-permute-start | bytes 737288 | tf_op jit(solution)/shard_map/ppermute | solution.py:345
  136.5 0.8 collective-permute-done.29
  137.4 3.3 %collective-permute-start.35 = (bf16[240,320]{1,0:T(8,128)(2,1)S(1)}, bf16[240,320]{1,0:T(8,128)(2,1)S(1)}, u32[]{:S(2)}, u32[]{:S(2)}) collective-permute-start(bf16[240,320]{1,0:T(8,128)(2,1)S(1)} %select_convert_fusion), channel_id=1, source_target_pairs={{0,4},{1,5},{2,6},{3,7},{4,0},{5,1},{6,2},{7,3},{8,12},{9,13},{10,... | collective-permute-start | bytes 460808 | tf_op jit(solution)/shard_map/ppermute | solution.py:265
  140.7 1.5 collective-permute-done.28
  142.1 2.3 %collective-permute-start.38 = (bf16[120,256]{1,0:T(8,128)(2,1)S(1)}, bf16[120,256]{1,0:T(8,128)(2,1)S(1)}, u32[]{:S(2)}, u32[]{:S(2)}) collective-permute-start(bf16[120,256]{1,0:T(8,128)(2,1)S(1)} %fusion.48), channel_id=1, source_target_pairs={{0,4},{1,5},{2,6},{3,7},{4,0},{5,1},{6,2},{7,3},{8,12},{9,13},{10,... | collective-permute-start | bytes 184328 | tf_op jit(solution)/shard_map/ppermute | solution.py:252
  144.4 0.9 convert_add_fusion.4
  145.3 3.6 %collective-permute-done.32 = bf16[2,248,256]{2,1,0:T(8,128)(2,1)S(1)} collective-permute-done((bf16[2,248,256]{2,1,0:T(8,128)(2,1)S(1)}, bf16[2,248,256]{2,1,0:T(8,128)(2,1)S(1)}, u32[]{:S(2)}, u32[]{:S(2)}) %collective-permute-start.32) | collective-permute-done | bytes 253984 | tf_op jit(solution)/shard_map/ppermute | solution.py:252
  149.3 4.2 %collective-permute-start.37 = (bf16[240,320]{1,0:T(8,128)(2,1)S(1)}, bf16[240,320]{1,0:T(8,128)(2,1)S(1)}, u32[]{:S(2)}, u32[]{:S(2)}) collective-permute-start(bf16[240,320]{1,0:T(8,128)(2,1)S(1)} %add_convert_fusion.2), channel_id=1, source_target_pairs={{0,0},{8,2},{16,4},{24,6},{1,8},{9,10},{17,12},{25,14},{2,16},{10,... | collective-permute-start | bytes 460808 | tf_op jit(solution)/shard_map/ppermute | solution.py:592
  155.0 10.5 %collective-permute-done.37 = bf16[240,320]{1,0:T(8,128)(2,1)S(1)} collective-permute-done((bf16[240,320]{1,0:T(8,128)(2,1)S(1)}, bf16[240,320]{1,0:T(8,128)(2,1)S(1)}, u32[]{:S(2)}, u32[]{:S(2)}) %collective-permute-start.37) | collective-permute-done | bytes 153632 | tf_op jit(solution)/shard_map/ppermute | solution.py:592
  166.9 0.9 copy.58
  (230 shorter events, 20.9 us)
Async XLA Ops:
  0.6 63.3 %copy-start = (bf16[960,640]{1,0:T(8,128)(2,1)S(1)}, bf16[960,640]{1,0:T(8,128)(2,1)}, u32[]{:S(2)}) copy-start(bf16[960,640]{1,0:T(8,128)(2,1)} %param.18) | copy-start | bytes 3686404
  0.7 9.0 %copy-start.20 = (bf16[1,128,960]{1,2,0:T(8,128)(2,1)S(1)}, bf16[1,128,960]{1,2,0:T(8,128)(2,1)}, u32[]{:S(2)}) copy-start(bf16[1,128,960]{1,2,0:T(8,128)(2,1)} %param.11) | copy-start | bytes 737284
  0.7 9.0 %collective-permute-start = (bf16[128,960]{0,1:T(8,128)(2,1)}, bf16[128,960]{0,1:T(8,128)(2,1)S(1)}, u32[]{:S(2)}, u32[]{:S(2)}) collective-permute-start(bf16[128,960]{0,1:T(8,128)(2,1)} %bitcast.128), channel_id=1, source_target_pairs={{0,24},{24,0},{8,16},{16,8},{1,25},{25,1},{9,17},{17,9},{2,26},{26... | collective-permute-start | bytes 737288 | tf_op jit(solution)/shard_map/ppermute | solution.py:345
  4.8 7.4 %copy-start.2 = (bf16[408,960]{1,0:T(8,128)(2,1)}, bf16[408,960]{1,0:T(8,128)(2,1)S(1)}, u32[]{:S(2)}) copy-start(bf16[408,960]{1,0:T(8,128)(2,1)S(1)} %fusion.11.own_ref) | copy-start | bytes 2350084
  4.9 22.6 %collective-permute-start.3 = (bf16[408,960]{1,0:T(8,128)(2,1)S(1)}, bf16[408,960]{1,0:T(8,128)(2,1)}, u32[]{:S(2)}, u32[]{:S(2)}) collective-permute-start(bf16[408,960]{1,0:T(8,128)(2,1)S(1)} %fusion.11.own_ref), channel_id=1, source_target_pairs={{0,24},{24,0},{8,16},{16,8},{1,25},{25,1},{9,17},{17,9},{2,26},{26... | collective-permute-start | bytes 2350088 | tf_op jit(solution)/shard_map/ppermute | solution.py:345
  5.1 25.9 %collective-permute-start.2 = (bf16[408,960]{1,0:T(8,128)(2,1)S(1)}, bf16[408,960]{1,0:T(8,128)(2,1)}, u32[]{:S(2)}, u32[]{:S(2)}) collective-permute-start(bf16[408,960]{1,0:T(8,128)(2,1)S(1)} %fusion.11.own_ref), channel_id=1, source_target_pairs={{0,8},{8,0},{16,24},{24,16},{1,9},{9,1},{17,25},{25,17},{2,10},{10... | collective-permute-start | bytes 2350088 | tf_op jit(solution)/shard_map/ppermute | solution.py:342
  9.7 3.8 %copy-start.22 = (bf16[128,960]{0,1:T(8,128)(2,1)}, bf16[128,960]{0,1:T(8,128)(2,1)S(1)}, u32[]{:S(2)}) copy-start(bf16[128,960]{0,1:T(8,128)(2,1)S(1)} %get-tuple-element.239) | copy-start | bytes 737284
  9.7 3.8 %copy-start.25 = (bf16[128,960]{0,1:T(8,128)(2,1)}, bf16[128,960]{0,1:T(8,128)(2,1)S(1)}, u32[]{:S(2)}) copy-start(bf16[128,960]{0,1:T(8,128)(2,1)S(1)} %get-tuple-element.240) | copy-start | bytes 737284
  9.8 3.7 %collective-permute-start.1 = (bf16[256,960]{0,1:T(8,128)(2,1)S(1)}, bf16[256,960]{0,1:T(8,128)(2,1)S(1)}, u32[]{:S(2)}, u32[]{:S(2)}) collective-permute-start(bf16[256,960]{0,1:T(8,128)(2,1)S(1)} %pad_maximum_fusion.7), channel_id=1, source_target_pairs={{0,8},{8,0},{16,24},{24,16},{1,9},{9,1},{17,25},{25,17},{2,10},{10... | collective-permute-start | bytes 1474568 | tf_op jit(solution)/shard_map/ppermute | solution.py:342
  27.4 3.5 %collective-permute-start.4 = (bf16[408,960]{1,0:T(8,128)(2,1)}, bf16[408,960]{1,0:T(8,128)(2,1)}, u32[]{:S(2)}, u32[]{:S(2)}) collective-permute-start(bf16[408,960]{1,0:T(8,128)(2,1)} %collective-permute-done.3.cross_ref), channel_id=1, source_target_pairs={{0,8},{8,0},{16,24},{24,16},{1,9},{9,1},{17,25},{25,17},{2,10},{10... | collective-permute-start | bytes 2350088 | tf_op jit(solution)/shard_map/ppermute | solution.py:342
  27.8 18.6 %collective-permute-start.6 = (bf16[240,960]{0,1:T(8,128)(2,1)}, bf16[240,960]{0,1:T(8,128)(2,1)}, u32[]{:S(2)}, u32[]{:S(2)}) collective-permute-start(bf16[240,960]{0,1:T(8,128)(2,1)} %bitcast.6), channel_id=1, source_target_pairs={{0,24},{24,0},{8,16},{16,8},{1,25},{25,1},{9,17},{17,9},{2,26},{26... | collective-permute-start | bytes 1382408 | tf_op jit(solution)/shard_map/ppermute | solution.py:345
  29.1 17.3 %collective-permute-start.7 = (bf16[128,960]{0,1:T(8,128)(2,1)}, bf16[128,960]{0,1:T(8,128)(2,1)}, u32[]{:S(2)}, u32[]{:S(2)}) collective-permute-start(bf16[128,960]{0,1:T(8,128)(2,1)} %bitcast.11), channel_id=1, source_target_pairs={{0,24},{24,0},{8,16},{16,8},{1,25},{25,1},{9,17},{17,9},{2,26},{26... | collective-permute-start | bytes 737288 | tf_op jit(solution)/shard_map/ppermute | solution.py:345
  30.7 18.1 %collective-permute-start.5 = (bf16[240,960]{0,1:T(8,128)(2,1)}, bf16[240,960]{0,1:T(8,128)(2,1)S(1)}, u32[]{:S(2)}, u32[]{:S(2)}) collective-permute-start(bf16[240,960]{0,1:T(8,128)(2,1)} %bitcast.6), channel_id=1, source_target_pairs={{0,8},{8,0},{16,24},{24,16},{1,9},{9,1},{17,25},{25,17},{2,10},{10... | collective-permute-start | bytes 1382408 | tf_op jit(solution)/shard_map/ppermute | solution.py:342
  32.1 14.8 %copy-start.23 = (bf16[128,960]{0,1:T(8,128)(2,1)S(1)}, bf16[128,960]{0,1:T(8,128)(2,1)}, u32[]{:S(2)}) copy-start(bf16[128,960]{0,1:T(8,128)(2,1)} %copy-done.22) | copy-start | bytes 737284
  32.1 14.8 %copy-start.26 = (bf16[128,960]{0,1:T(8,128)(2,1)S(1)}, bf16[128,960]{0,1:T(8,128)(2,1)}, u32[]{:S(2)}) copy-start(bf16[128,960]{0,1:T(8,128)(2,1)} %copy-done.25) | copy-start | bytes 737284
  32.1 15.3 %copy-start.38 = (bf16[480,640]{1,0:T(8,128)(2,1)S(1)}, bf16[480,640]{1,0:T(8,128)(2,1)}, u32[]{:S(2)}) copy-start(bf16[480,640]{1,0:T(8,128)(2,1)} %pad_maximum_fusion.5) | copy-start | bytes 1843204
  43.3 6.9 %copy-start.4 = (bf16[960,256]{1,0:T(8,128)(2,1)}, bf16[960,256]{1,0:T(8,128)(2,1)S(1)}, u32[]{:S(2)}) copy-start(bf16[960,256]{1,0:T(8,128)(2,1)S(1)} %get-tuple-element.132.q_ref) | copy-start | bytes 1474564
  43.3 6.9 %copy-start.6 = (bf16[320,512]{1,0:T(8,128)(2,1)}, bf16[320,512]{1,0:T(8,128)(2,1)S(1)}, u32[]{:S(2)}) copy-start(bf16[320,512]{1,0:T(8,128)(2,1)S(1)} %get-tuple-element.133.k_ref) | copy-start | bytes 983044
  43.3 6.9 %copy-start.8 = (bf16[320,512]{1,0:T(8,128)(2,1)}, bf16[320,512]{1,0:T(8,128)(2,1)S(1)}, u32[]{:S(2)}) copy-start(bf16[320,512]{1,0:T(8,128)(2,1)S(1)} %get-tuple-element.134.v_ref) | copy-start | bytes 983044
  46.4 2.4 %collective-permute-start.8 = (bf16[240,960]{0,1:T(8,128)(2,1)}, bf16[240,960]{0,1:T(8,128)(2,1)S(1)}, u32[]{:S(2)}, u32[]{:S(2)}) collective-permute-start(bf16[240,960]{0,1:T(8,128)(2,1)} %collective-permute-done.6), channel_id=1, source_target_pairs={{0,8},{8,0},{16,24},{24,16},{1,9},{9,1},{17,25},{25,17},{2,10},{10... | collective-permute-start | bytes 1382408 | tf_op jit(solution)/shard_map/ppermute | solution.py:342
  46.6 7.5 %collective-permute-start.10 = (bf16[128,960]{0,1:T(8,128)(2,1)}, bf16[128,960]{0,1:T(8,128)(2,1)S(1)}, u32[]{:S(2)}, u32[]{:S(2)}) collective-permute-start(bf16[128,960]{0,1:T(8,128)(2,1)} %bitcast.11), channel_id=1, source_target_pairs={{0,8},{8,0},{16,24},{24,16},{1,9},{9,1},{17,25},{25,17},{2,10},{10... | collective-permute-start | bytes 737288 | tf_op jit(solution)/shard_map/ppermute | solution.py:342
  47.1 7.0 %collective-permute-start.11 = (bf16[128,960]{0,1:T(8,128)(2,1)}, bf16[128,960]{0,1:T(8,128)(2,1)S(1)}, u32[]{:S(2)}, u32[]{:S(2)}) collective-permute-start(bf16[128,960]{0,1:T(8,128)(2,1)} %collective-permute-done.7), channel_id=1, source_target_pairs={{0,8},{8,0},{16,24},{24,16},{1,9},{9,1},{17,25},{25,17},{2,10},{10... | collective-permute-start | bytes 737288 | tf_op jit(solution)/shard_map/ppermute | solution.py:342
  47.4 15.8 %collective-permute-start.12 = (bf16[480,640]{1,0:T(8,128)(2,1)S(1)}, bf16[480,640]{1,0:T(8,128)(2,1)S(1)}, u32[]{:S(2)}, u32[]{:S(2)}) collective-permute-start(bf16[480,640]{1,0:T(8,128)(2,1)S(1)} %copy-done.38), channel_id=1, source_target_pairs={{0,24},{24,0},{8,16},{16,8},{1,25},{25,1},{9,17},{17,9},{2,26},{26... | collective-permute-start | bytes 1843208 | tf_op jit(solution)/shard_map/ppermute | solution.py:345
  50.3 5.0 %copy-start.39 = (bf16[240,960]{0,1:T(8,128)(2,1)}, bf16[240,960]{0,1:T(8,128)(2,1)S(1)}, u32[]{:S(2)}) copy-start(bf16[240,960]{0,1:T(8,128)(2,1)S(1)} %get-tuple-element.211) | copy-start | bytes 1382404
  50.3 5.0 %copy-start.40 = (bf16[240,960]{0,1:T(8,128)(2,1)}, bf16[240,960]{0,1:T(8,128)(2,1)S(1)}, u32[]{:S(2)}) copy-start(bf16[240,960]{0,1:T(8,128)(2,1)S(1)} %get-tuple-element.212) | copy-start | bytes 1382404
  53.6 34.8 %copy-start.12 = (f32[256,960]{0,1:T(8,128)}, f32[256,960]{0,1:T(8,128)S(1)}, u32[]{:S(2)}) copy-start(f32[256,960]{0,1:T(8,128)S(1)} %get-tuple-element.248) | copy-start | bytes 2949124
  53.9 9.3 %copy-start.33 = (bf16[240,640]{1,0:T(8,128)(2,1)S(1)}, bf16[240,640]{1,0:T(8,128)(2,1)}, u32[]{:S(2)}) copy-start(bf16[240,640]{1,0:T(8,128)(2,1)} %get-tuple-element.113) | copy-start | bytes 921604
  53.9 9.8 %collective-permute-start.9 = (bf16[256,960]{0,1:T(8,128)(2,1)S(1)}, bf16[256,960]{0,1:T(8,128)(2,1)S(1)}, u32[]{:S(2)}, u32[]{:S(2)}) collective-permute-start(bf16[256,960]{0,1:T(8,128)(2,1)S(1)} %multiply_convert_fusion.3), channel_id=1, source_target_pairs={{0,8},{8,0},{16,24},{24,16},{1,9},{9,1},{17,25},{25,17},{2,10},{10... | collective-permute-start | bytes 1474568 | tf_op jit(solution)/shard_map/ppermute | solution.py:342
  63.3 3.1 %collective-permute-start.13 = (bf16[480,640]{1,0:T(8,128)(2,1)S(1)}, bf16[480,640]{1,0:T(8,128)(2,1)S(1)}, u32[]{:S(2)}, u32[]{:S(2)}) collective-permute-start(bf16[480,640]{1,0:T(8,128)(2,1)S(1)} %pad_maximum_fusion.6), channel_id=1, source_target_pairs={{0,8},{8,0},{16,24},{24,16},{1,9},{9,1},{17,25},{25,17},{2,10},{10... | collective-permute-start | bytes 1843208 | tf_op jit(solution)/shard_map/ppermute | solution.py:342
  69.0 4.1 %copy-start.36 = (bf16[512,640]{1,0:T(8,128)(2,1)}, bf16[512,640]{1,0:T(8,128)(2,1)S(1)}, u32[]{:S(2)}) copy-start(bf16[512,640]{1,0:T(8,128)(2,1)S(1)} %get-tuple-element.151) | copy-start | bytes 1966084
  71.0 3.0 %collective-permute-start.15 = (bf16[256,960]{0,1:T(8,128)(2,1)S(1)}, bf16[256,960]{0,1:T(8,128)(2,1)S(1)}, u32[]{:S(2)}, u32[]{:S(2)}) collective-permute-start(bf16[256,960]{0,1:T(8,128)(2,1)S(1)} %constant_dynamic-slice_fusion.16), channel_id=1, source_target_pairs={{0,8},{8,0},{16,24},{24,16},{1,9},{9,1},{17,25},{25,17},{2,10},{10... | collective-permute-start | bytes 1474568 | tf_op jit(solution)/shard_map/ppermute | solution.py:342
  72.2 3.8 %copy-start.16 = (f32[960,640]{1,0:T(8,128)}, f32[960,640]{1,0:T(8,128)S(1)}, u32[]{:S(2)}) copy-start(f32[960,640]{1,0:T(8,128)S(1)} %fusion.66) | copy-start | bytes 7372804
  73.1 3.9 %copy-start.18 = (f32[960,640]{1,0:T(8,128)}, f32[960,640]{1,0:T(8,128)S(1)}, u32[]{:S(2)}) copy-start(f32[960,640]{1,0:T(8,128)S(1)} %fusion.67) | copy-start | bytes 7372804
  74.0 5.2 %copy-start.14 = (f32[960,640]{1,0:T(8,128)}, f32[960,640]{1,0:T(8,128)S(1)}, u32[]{:S(2)}) copy-start(f32[960,640]{1,0:T(8,128)S(1)} %fusion.68) | copy-start | bytes 7372804
  74.2 13.7 %collective-permute-start.16 = (bf16[256,960]{0,1:T(8,128)(2,1)S(1)}, bf16[256,960]{0,1:T(8,128)(2,1)S(1)}, u32[]{:S(2)}, u32[]{:S(2)}) collective-permute-start(bf16[256,960]{0,1:T(8,128)(2,1)S(1)} %fusion.10), channel_id=1, source_target_pairs={{0,24},{24,0},{8,16},{16,8},{1,25},{25,1},{9,17},{17,9},{2,26},{26... | collective-permute-start | bytes 1474568 | tf_op jit(solution)/shard_map/ppermute | solution.py:345
  75.8 37.3 %collective-permute-start.14 = (bf16[960,256]{1,0:T(8,128)(2,1)}, bf16[960,256]{1,0:T(8,128)(2,1)}, u32[]{:S(2)}, u32[]{:S(2)}) collective-permute-start(bf16[960,256]{1,0:T(8,128)(2,1)} %get-tuple-element.150.o_ref), channel_id=1, source_target_pairs={{0,8},{8,0},{16,24},{24,16},{1,9},{9,1},{17,25},{25,17},{2,10},{10... | collective-permute-start | bytes 1474568 | tf_op jit(solution)/shard_map/ppermute | solution.py:342
  76.8 22.7 %collective-permute-start.19 = (bf16[2,2,120,640]{3,2,0,1:T(8,128)(2,1)}, bf16[2,2,120,640]{3,2,0,1:T(8,128)(2,1)S(1)}, u32[]{:S(2)}, u32[]{:S(2)}) collective-permute-start(bf16[2,2,120,640]{3,2,0,1:T(8,128)(2,1)} %fusion.16), channel_id=1, source_target_pairs={{0,1},{1,0},{2,3},{3,2},{4,5},{5,4},{6,7},{7,6},{8,9},{9,8},{10,11... | collective-permute-start | bytes 1843208 | tf_op jit(solution)/shard_map/ppermute | solution.py:252
  77.9 22.1 %collective-permute-start.20 = (bf16[2,2,120,640]{3,2,0,1:T(8,128)(2,1)}, bf16[2,2,120,640]{3,2,0,1:T(8,128)(2,1)}, u32[]{:S(2)}, u32[]{:S(2)}) collective-permute-start(bf16[2,2,120,640]{3,2,0,1:T(8,128)(2,1)} %fusion.17), channel_id=1, source_target_pairs={{0,2},{1,3},{2,0},{3,1},{4,6},{5,7},{6,4},{7,5},{8,10},{9,11},{10,... | collective-permute-start | bytes 1843208 | tf_op jit(solution)/shard_map/ppermute | solution.py:252
  80.1 38.7 %collective-permute-start.27 = (bf16[2,240,640]{2,1,0:T(8,128)(2,1)}, bf16[2,240,640]{2,1,0:T(8,128)(2,1)}, u32[]{:S(2)}, u32[]{:S(2)}) collective-permute-start(bf16[2,240,640]{2,1,0:T(8,128)(2,1)} %fusion.18), channel_id=1, source_target_pairs={{0,1},{1,0},{2,3},{3,2},{4,5},{5,4},{6,7},{7,6},{8,9},{9,8},{10,11... | collective-permute-start | bytes 1843208 | tf_op jit(solution)/shard_map/ppermute | solution.py:252
  92.4 7.7 %copy-start.17 = (f32[960,640]{1,0:T(8,128)S(1)}, f32[960,640]{1,0:T(8,128)}, u32[]{:S(2)}) copy-start(f32[960,640]{1,0:T(8,128)} %copy-done.16) | copy-start | bytes 7372804
  99.4 7.0 %collective-permute-start.18 = (bf16[640,512]{1,0:T(8,128)(2,1)S(1)}, bf16[640,512]{1,0:T(8,128)(2,1)S(1)}, u32[]{:S(2)}, u32[]{:S(2)}) collective-permute-start(bf16[640,512]{1,0:T(8,128)(2,1)S(1)} %get-tuple-element.138), channel_id=1, source_target_pairs={{0,8},{8,0},{16,24},{24,16},{1,9},{9,1},{17,25},{25,17},{2,10},{10... | collective-permute-start | bytes 1966088 | tf_op jit(solution)/shard_map/ppermute | solution.py:342
  99.5 3.8 %collective-permute-start.17 = (bf16[240,256]{1,0:T(8,128)(2,1)S(1)}, bf16[240,256]{1,0:T(8,128)(2,1)S(1)}, u32[]{:S(2)}, u32[]{:S(2)}) collective-permute-start(bf16[240,256]{1,0:T(8,128)(2,1)S(1)} %constant_dynamic-slice_fusion.15), channel_id=1, source_target_pairs={{0,8},{8,0},{16,24},{24,16},{1,9},{9,1},{17,25},{25,17},{2,10},{10... | collective-permute-start | bytes 368648 | tf_op jit(solution)/shard_map/ppermute | solution.py:342
  100.1 5.5 %collective-permute-start.23 = (bf16[256,240]{0,1:T(8,128)(2,1)S(1)}, bf16[256,240]{0,1:T(8,128)(2,1)S(1)}, u32[]{:S(2)}, u32[]{:S(2)}) collective-permute-start(bf16[256,240]{0,1:T(8,128)(2,1)S(1)} %constant_dynamic-slice_fusion.5), channel_id=1, source_target_pairs={{0,8},{8,0},{16,24},{24,16},{1,9},{9,1},{17,25},{25,17},{2,10},{10... | collective-permute-start | bytes 368648 | tf_op jit(solution)/shard_map/ppermute | solution.py:342
  103.3 9.1 %collective-permute-start.22 = (bf16[2,120,640]{2,1,0:T(8,128)(2,1)}, bf16[2,120,640]{2,1,0:T(8,128)(2,1)}, u32[]{:S(2)}, u32[]{:S(2)}) collective-permute-start(bf16[2,120,640]{2,1,0:T(8,128)(2,1)} %fusion.27), channel_id=1, source_target_pairs={{0,2},{1,3},{2,0},{3,1},{4,6},{5,7},{6,4},{7,5},{8,10},{9,11},{10,... | collective-permute-start | bytes 921608 | tf_op jit(solution)/shard_map/ppermute | solution.py:252
  105.6 16.9 %collective-permute-start.26 = (bf16[2,120,640]{2,1,0:T(8,128)(2,1)}, bf16[2,120,640]{2,1,0:T(8,128)(2,1)}, u32[]{:S(2)}, u32[]{:S(2)}) collective-permute-start(bf16[2,120,640]{2,1,0:T(8,128)(2,1)} %fusion.28), channel_id=1, source_target_pairs={{0,1},{1,0},{2,3},{3,2},{4,5},{5,4},{6,7},{7,6},{8,9},{9,8},{10,11... | collective-permute-start | bytes 921608 | tf_op jit(solution)/shard_map/ppermute | solution.py:252
  110.9 1.9 %collective-permute-start.21 = (f32[2,240]{1,0:T(2,128)S(1)}, f32[2,240]{1,0:T(2,128)S(1)}, u32[]{:S(2)}, u32[]{:S(2)}) collective-permute-start(f32[2,240]{1,0:T(2,128)S(1)} %fusion.51), channel_id=1, source_target_pairs={{0,8},{8,0},{16,24},{24,16},{1,9},{9,1},{17,25},{25,17},{2,10},{10... | collective-permute-start | bytes 5768 | tf_op jit(solution)/shard_map/ppermute | solution.py:342
  114.9 3.9 %copy-start.15 = (f32[960,640]{1,0:T(8,128)S(1)}, f32[960,640]{1,0:T(8,128)}, u32[]{:S(2)}) copy-start(f32[960,640]{1,0:T(8,128)} %copy-done.14) | copy-start | bytes 7372804
  114.9 11.0 %collective-permute-start.25 = (bf16[2,2,120,256]{3,2,0,1:T(8,128)(2,1)S(1)}, bf16[2,2,120,256]{3,2,0,1:T(8,128)(2,1)S(1)}, u32[]{:S(2)}, u32[]{:S(2)}) collective-permute-start(bf16[2,2,120,256]{3,2,0,1:T(8,128)(2,1)S(1)} %fusion.31), channel_id=1, source_target_pairs={{0,1},{1,0},{2,3},{3,2},{4,5},{5,4},{6,7},{7,6},{8,9},{9,8},{10,11... | collective-permute-start | bytes 737288 | tf_op jit(solution)/shard_map/ppermute | solution.py:252
  116.2 16.5 %collective-permute-start.31 = (bf16[2,2,248,256]{3,2,0,1:T(8,128)(2,1)S(1)}, bf16[2,2,248,256]{3,2,0,1:T(8,128)(2,1)S(1)}, u32[]{:S(2)}, u32[]{:S(2)}) collective-permute-start(bf16[2,2,248,256]{3,2,0,1:T(8,128)(2,1)S(1)} %fusion.21), channel_id=1, source_target_pairs={{0,1},{1,0},{2,3},{3,2},{4,5},{5,4},{6,7},{7,6},{8,9},{9,8},{10,11... | collective-permute-start | bytes 1523720 | tf_op jit(solution)/shard_map/ppermute | solution.py:252
  117.5 3.9 %copy-start.31 = (f32[2,2,120,640]{3,2,0,1:T(8,128)S(1)}, f32[2,2,120,640]{3,2,0,1:T(8,128)}, u32[]{:S(2)}) copy-start(f32[2,2,120,640]{3,2,0,1:T(8,128)} %copy-done.30) | copy-start | bytes 3686404
  117.5 8.7 %collective-permute-start.24 = (bf16[256,960]{0,1:T(8,128)(2,1)S(1)}, bf16[256,960]{0,1:T(8,128)(2,1)S(1)}, u32[]{:S(2)}, u32[]{:S(2)}) collective-permute-start(bf16[256,960]{0,1:T(8,128)(2,1)S(1)} %constant_dynamic-slice_fusion.3), channel_id=1, source_target_pairs={{0,8},{8,0},{16,24},{24,16},{1,9},{9,1},{17,25},{25,17},{2,10},{10... | collective-permute-start | bytes 1474568 | tf_op jit(solution)/shard_map/ppermute | solution.py:342
  120.0 4.9 %copy-start.29 = (f32[2,2,120,640]{3,2,0,1:T(8,128)S(1)}, f32[2,2,120,640]{3,2,0,1:T(8,128)}, u32[]{:S(2)}) copy-start(f32[2,2,120,640]{3,2,0,1:T(8,128)} %copy-done.28) | copy-start | bytes 3686404
  120.0 15.5 %collective-permute-start.30 = (bf16[240,640]{1,0:T(8,128)(2,1)S(1)}, bf16[240,640]{1,0:T(8,128)(2,1)S(1)}, u32[]{:S(2)}, u32[]{:S(2)}) collective-permute-start(bf16[240,640]{1,0:T(8,128)(2,1)S(1)} %fusion.29), channel_id=1, source_target_pairs={{0,2},{1,3},{2,0},{3,1},{4,6},{5,7},{6,4},{7,5},{8,10},{9,11},{10,... | collective-permute-start | bytes 921608 | tf_op jit(solution)/shard_map/ppermute | solution.py:252
  122.5 31.0 %collective-permute-start.34 = (bf16[120,640]{1,0:T(8,128)(2,1)S(1)}, bf16[120,640]{1,0:T(8,128)(2,1)S(1)}, u32[]{:S(2)}, u32[]{:S(2)}) collective-permute-start(bf16[120,640]{1,0:T(8,128)(2,1)S(1)} %fusion.44), channel_id=1, source_target_pairs={{0,4},{1,5},{2,6},{3,7},{4,0},{5,1},{6,2},{7,3},{8,12},{9,13},{10,... | collective-permute-start | bytes 460808 | tf_op jit(solution)/shard_map/ppermute | solution.py:252
  126.0 28.3 %collective-permute-start.36 = (bf16[120,640]{1,0:T(8,128)(2,1)S(1)}, bf16[120,640]{1,0:T(8,128)(2,1)S(1)}, u32[]{:S(2)}, u32[]{:S(2)}) collective-permute-start(bf16[120,640]{1,0:T(8,128)(2,1)S(1)} %fusion.45), channel_id=1, source_target_pairs={{0,4},{1,5},{2,6},{3,7},{4,0},{5,1},{6,2},{7,3},{8,12},{9,13},{10,... | collective-permute-start | bytes 460808 | tf_op jit(solution)/shard_map/ppermute | solution.py:252
  126.2 11.1 %collective-permute-start.29 = (bf16[2,120,256]{2,1,0:T(8,128)(2,1)S(1)}, bf16[2,120,256]{2,1,0:T(8,128)(2,1)S(1)}, u32[]{:S(2)}, u32[]{:S(2)}) collective-permute-start(bf16[2,120,256]{2,1,0:T(8,128)(2,1)S(1)} %fusion.47), channel_id=1, source_target_pairs={{0,2},{1,3},{2,0},{3,1},{4,6},{5,7},{6,4},{7,5},{8,10},{9,11},{10,... | collective-permute-start | bytes 368648 | tf_op jit(solution)/shard_map/ppermute | solution.py:252
  132.8 9.4 %collective-permute-start.28 = (bf16[128,960]{0,1:T(8,128)(2,1)S(1)}, bf16[128,960]{0,1:T(8,128)(2,1)S(1)}, u32[]{:S(2)}, u32[]{:S(2)}) collective-permute-start(bf16[128,960]{0,1:T(8,128)(2,1)S(1)} %dynamic-slice_convert_fusion.4), channel_id=1, source_target_pairs={{0,24},{24,0},{8,16},{16,8},{1,25},{25,1},{9,17},{17,9},{2,26},{26... | collective-permute-start | bytes 737288 | tf_op jit(solution)/shard_map/ppermute | solution.py:345
  135.5 9.0 %copy-start.13 = (f32[256,960]{0,1:T(8,128)S(1)}, f32[256,960]{0,1:T(8,128)}, u32[]{:S(2)}) copy-start(f32[256,960]{0,1:T(8,128)} %copy-done.12) | copy-start | bytes 2949124
  135.6 13.4 %collective-permute-start.32 = (bf16[2,248,256]{2,1,0:T(8,128)(2,1)S(1)}, bf16[2,248,256]{2,1,0:T(8,128)(2,1)S(1)}, u32[]{:S(2)}, u32[]{:S(2)}) collective-permute-start(bf16[2,248,256]{2,1,0:T(8,128)(2,1)S(1)} %fusion.30), channel_id=1, source_target_pairs={{0,2},{1,3},{2,0},{3,1},{4,6},{5,7},{6,4},{7,5},{8,10},{9,11},{10,... | collective-permute-start | bytes 761864 | tf_op jit(solution)/shard_map/ppermute | solution.py:252
  137.4 11.8 %collective-permute-start.35 = (bf16[240,320]{1,0:T(8,128)(2,1)S(1)}, bf16[240,320]{1,0:T(8,128)(2,1)S(1)}, u32[]{:S(2)}, u32[]{:S(2)}) collective-permute-start(bf16[240,320]{1,0:T(8,128)(2,1)S(1)} %select_convert_fusion), channel_id=1, source_target_pairs={{0,4},{1,5},{2,6},{3,7},{4,0},{5,1},{6,2},{7,3},{8,12},{9,13},{10,... | collective-permute-start | bytes 460808 | tf_op jit(solution)/shard_map/ppermute | solution.py:265
  142.1 27.1 %collective-permute-start.38 = (bf16[120,256]{1,0:T(8,128)(2,1)S(1)}, bf16[120,256]{1,0:T(8,128)(2,1)S(1)}, u32[]{:S(2)}, u32[]{:S(2)}) collective-permute-start(bf16[120,256]{1,0:T(8,128)(2,1)S(1)} %fusion.48), channel_id=1, source_target_pairs={{0,4},{1,5},{2,6},{3,7},{4,0},{5,1},{6,2},{7,3},{8,12},{9,13},{10,... | collective-permute-start | bytes 184328 | tf_op jit(solution)/shard_map/ppermute | solution.py:252
  149.1 16.5 %collective-permute-start.33 = (bf16[248,256]{1,0:T(8,128)(2,1)S(1)}, bf16[248,256]{1,0:T(8,128)(2,1)S(1)}, u32[]{:S(2)}, u32[]{:S(2)}) collective-permute-start(bf16[248,256]{1,0:T(8,128)(2,1)S(1)} %fusion.46), channel_id=1, source_target_pairs={{0,4},{1,5},{2,6},{3,7},{4,0},{5,1},{6,2},{7,3},{8,12},{9,13},{10,... | collective-permute-start | bytes 380936 | tf_op jit(solution)/shard_map/ppermute | solution.py:252
  149.3 16.2 %collective-permute-start.37 = (bf16[240,320]{1,0:T(8,128)(2,1)S(1)}, bf16[240,320]{1,0:T(8,128)(2,1)S(1)}, u32[]{:S(2)}, u32[]{:S(2)}) collective-permute-start(bf16[240,320]{1,0:T(8,128)(2,1)S(1)} %add_convert_fusion.2), channel_id=1, source_target_pairs={{0,0},{8,2},{16,4},{24,6},{1,8},{9,10},{17,12},{25,14},{2,16},{10,... | collective-permute-start | bytes 460808 | tf_op jit(solution)/shard_map/ppermute | solution.py:592
  153.5 16.4 %copy-start.1 = (bf16[960,640]{1,0:T(8,128)(2,1)S(1)}, bf16[960,640]{1,0:T(8,128)(2,1)}, u32[]{:S(2)}) copy-start(bf16[960,640]{1,0:T(8,128)(2,1)} %param.18) | copy-start | bytes 3686404
  (28 other events, 54.1 us)
